TPU v7x, 32 devices: a whole 2x2x4 slice. The times are simulated.
32 devices in a mesh: seq: 4 (over x, core), fsdp: 8 (over z, y).
Axes of the slice: x: 2, y: 2, z: 4, core: 2. Of those that a mesh axis runs over, the one named last changes fastest.
Arguments:
- tokens: bfloat16 [3, 8, 1024, 1024], P(None, None, ('seq', 'fsdp')), may hold values from -6 to 6
- cotangent: bfloat16 [3, 8, 1024, 1024], P(None, 'fsdp', 'seq'), may hold values from -6 to 6
- seq_lengths: int32 [3, 8], replicated, may hold values from 256 to 1024, as said below
- seq_slots: int32 [3, 8], replicated, may hold values from 0 to 7, each once within a row
- norm_gain: bfloat16 [1024], P(('seq', 'fsdp')), may hold values from 0.5 to 1.5
- w_query: bfloat16 [1024, 1024], P(('seq', 'fsdp')), may hold values from -0.1875 to 0.1875
- w_key: bfloat16 [1024, 1024], P(('seq', 'fsdp')), may hold values from -0.1875 to 0.1875
- w_value: bfloat16 [1024, 2048], P(('seq', 'fsdp')), may hold values from -0.1875 to 0.1875
- w_decay: bfloat16 [1024, 8], P(('seq', 'fsdp')), may hold values from -0.1875 to 0.1875
- w_beta: bfloat16 [1024, 8], P(('seq', 'fsdp')), may hold values from -0.1875 to 0.1875
- w_outgate: bfloat16 [1024, 2048], P(('seq', 'fsdp')), may hold values from -0.1875 to 0.1875
- query_filter: bfloat16 [4, 1024], P(None, ('seq', 'fsdp')), may hold values from -2.5 to 2.5
- key_filter: bfloat16 [4, 1024], P(None, ('seq', 'fsdp')), may hold values from -2.5 to 2.5
- value_filter: bfloat16 [4, 2048], P(None, ('seq', 'fsdp')), may hold values from -2.5 to 2.5
- decay_log: float32 [8], replicated, may hold values from -5 to 0
- decay_bias: float32 [8], replicated, may hold values from -6 to 0
- head_gain: bfloat16 [256], replicated, may hold values from 0.5 to 1.5
- w_output: bfloat16 [2048, 1024], P(None, ('seq', 'fsdp')), may hold values from -0.1875 to 0.1875
- ffn_gain: bfloat16 [1024], P(('seq', 'fsdp')), may hold values from 0.5 to 1.5
- w_gate: bfloat16 [1024, 2816], P(('seq', 'fsdp')), may hold values from -0.1875 to 0.1875
- w_up: bfloat16 [1024, 2816], P(('seq', 'fsdp')), may hold values from -0.1875 to 0.1875
- w_down: bfloat16 [2816, 1024], P(None, ('seq', 'fsdp')), may hold values from -0.15625 to 0.15625
Outputs:
- mixed: float32 [3, 8, 1024, 1024], P(None, 'fsdp', 'seq')
- tokens_grad: float32 [3, 8, 1024, 1024], P(None, None, ('seq', 'fsdp'))
- norm_gain_grad: float32 [1024], P(('seq', 'fsdp'))
- query_grad: float32 [1024, 1024], P(('seq', 'fsdp'))
- key_grad: float32 [1024, 1024], P(('seq', 'fsdp'))
- value_grad: float32 [1024, 2048], P(('seq', 'fsdp'))
- decay_grad: float32 [1024, 8], P(('seq', 'fsdp'))
- beta_grad: float32 [1024, 8], P(('seq', 'fsdp'))
- outgate_grad: float32 [1024, 2048], P(('seq', 'fsdp'))
- query_filter_grad: float32 [4, 1024], P(None, ('seq', 'fsdp'))
- key_filter_grad: float32 [4, 1024], P(None, ('seq', 'fsdp'))
- value_filter_grad: float32 [4, 2048], P(None, ('seq', 'fsdp'))
- decay_log_grad: float32 [8], replicated
- decay_bias_grad: float32 [8], replicated
- head_gain_grad: float32 [256], replicated
- output_grad: float32 [2048, 1024], P(None, ('seq', 'fsdp'))
- ffn_gain_grad: float32 [1024], P(('seq', 'fsdp'))
- gate_grad: float32 [1024, 2816], P(('seq', 'fsdp'))
- up_grad: float32 [1024, 2816], P(('seq', 'fsdp'))
- down_grad: float32 [2816, 1024], P(None, ('seq', 'fsdp'))
Inputs may be any that keep to these rules, and one draw needn't show every extreme that they name: `seq_lengths`: every length is at least 256; in each micro-batch some sequence has exactly 1024. `seq_slots`: each micro-batch's row is a permutation of the slots; slots j * 1 to (j + 1) - 1 form sequence group j.
All inputs are finite; a program needn't handle non-finite values.
Results may differ from a plain program's by a relative error of at most 0.02.
Values may be sent and summed in bfloat16 or wider, within the bound.
A program may use at most 256 MiB of HBM per device.

v0:
```python
import jax
import jax.numpy as jnp
from jax import lax
from jax.sharding import PartitionSpec as P

SPAN = 64


EPS = 1e-06
HIGH = lax.Precision.HIGHEST


def rms_scale(values, gain):
    return values * lax.rsqrt(jnp.mean(values * values, -1, keepdims=True) + EPS) * gain


def gated_norm(values, gate_pre, gain):
    head_size = gain.shape[0]
    split_vals = values.reshape(values.shape[:-1] + (values.shape[-1] // head_size, head_size))
    scaled = (
        split_vals * lax.rsqrt(jnp.mean(split_vals * split_vals, -1, keepdims=True) + EPS) * gain
    )
    return scaled.reshape(values.shape) * jax.nn.silu(gate_pre)


def swish_gate(gate_val, upper_val):
    return jax.nn.silu(gate_val) * upper_val


def causal_filter(series, taps_weight):
    tap_count = taps_weight.shape[0]
    seq_len = series.shape[1]
    padded = jnp.pad(series, ((0, 0), (tap_count - 1, 0), (0, 0)))
    running = padded[:, 0:seq_len, :] * taps_weight[0]
    for offset in range(1, tap_count):
        running = running + padded[:, offset : offset + seq_len, :] * taps_weight[offset]
    return jax.nn.silu(running)


def span_step(memory, pieces):
    query_in, keys_in, values_in, log_decay, beta_rate = pieces
    span_len = log_decay.shape[-1]
    log_cumul = jnp.cumsum(log_decay, -1)
    row_ids = jnp.arange(span_len)[:, None]
    col_ids = jnp.arange(span_len)[None, :]
    lower_mask = row_ids >= col_ids
    strict_mask = row_ids > col_ids
    log_gap = log_cumul[..., :, None] - log_cumul[..., None, :]
    decay = jnp.where(lower_mask, jnp.exp(jnp.where(lower_mask, log_gap, 0.0)), 0.0)
    keys_dot = jnp.einsum("bhid,bhjd->bhij", keys_in, keys_in, precision=HIGH)
    mixing = jnp.eye(span_len, dtype=jnp.float32) + beta_rate[..., :, None] * jnp.where(
        strict_mask, decay * keys_dot, 0.0
    )
    growth = jnp.exp(log_cumul)
    target = beta_rate[..., None] * (
        values_in
        - growth[..., None] * jnp.einsum("bhid,bhde->bhie", keys_in, memory, precision=HIGH)
    )
    update = lax.linalg.triangular_solve(
        mixing, target, left_side=True, lower=True, unit_diagonal=True
    )
    scores = jnp.where(
        lower_mask, decay * jnp.einsum("bhid,bhjd->bhij", query_in, keys_in, precision=HIGH), 0.0
    )
    output = growth[..., None] * jnp.einsum("bhid,bhde->bhie", query_in, memory, precision=HIGH)
    output = output + jnp.einsum("bhij,bhje->bhie", scores, update, precision=HIGH)
    last_log = log_cumul[..., -1:]
    carried = keys_in * jnp.exp(last_log - log_cumul)[..., None]
    memory = jnp.exp(last_log)[..., None] * memory + jnp.einsum(
        "bhid,bhie->bhde", carried, update, precision=HIGH
    )
    return (memory, output)


def delta_rule(query_in, keys_in, values_in, log_decay, beta_rate):
    batch, seq_len, heads, key_dim = query_in.shape
    value_dim = values_in.shape[-1]
    count = seq_len // SPAN

    def blocks_four(array):
        return array.reshape((batch, count, SPAN, heads, array.shape[-1])).transpose(1, 0, 3, 2, 4)

    def blocks_three(array):
        return array.reshape((batch, count, SPAN, heads)).transpose(1, 0, 3, 2)

    start = jnp.zeros((batch, heads, key_dim, value_dim), jnp.float32)
    _, outputs = lax.scan(
        jax.checkpoint(span_step),
        start,
        (
            blocks_four(query_in),
            blocks_four(keys_in),
            blocks_four(values_in),
            blocks_three(log_decay),
            blocks_three(beta_rate),
        ),
    )
    return outputs.transpose(1, 0, 3, 2, 4).reshape(batch, seq_len, heads * value_dim)


def mixer(
    query_pre,
    key_pre,
    value_pre,
    decay_pre,
    beta_pre,
    filter_query,
    filter_key,
    filter_value,
    decay_log,
    decay_bias,
):
    batch, seq_len, _ = query_pre.shape
    heads = decay_pre.shape[-1]
    query_conv = causal_filter(query_pre, filter_query).reshape(batch, seq_len, heads, -1)
    key_conv = causal_filter(key_pre, filter_key).reshape(batch, seq_len, heads, -1)
    value_conv = causal_filter(value_pre, filter_value).reshape(batch, seq_len, heads, -1)
    query_hat = (
        query_conv
        * lax.rsqrt(jnp.sum(query_conv * query_conv, -1, keepdims=True) + EPS)
        * query_conv.shape[-1] ** (-0.5)
    )
    key_hat = key_conv * lax.rsqrt(jnp.sum(key_conv * key_conv, -1, keepdims=True) + EPS)
    beta_rate = jax.nn.sigmoid(beta_pre)
    log_decay = -jnp.exp(decay_log) * jax.nn.softplus(decay_pre + decay_bias)
    return delta_rule(query_hat, key_hat, value_conv, log_decay, beta_rate)


def product(left, right):
    return jnp.dot(left, right, preferred_element_type=jnp.float32)


def outer_sum(left, right):
    return lax.dot_general(
        left, right, (((0,), (0,)), ((), ())), preferred_element_type=jnp.float32
    )


def back_through(left, right):
    return lax.dot_general(
        left, right, (((1,), (1,)), ((), ())), preferred_element_type=jnp.float32
    )


def place_slice(local, full_shape, start, along):
    return lax.dynamic_update_slice_in_dim(jnp.zeros(full_shape, jnp.float32), local, start, along)


def take_rows(source, order):
    return jnp.take(source, order, axis=0)


def run_block(inputs, cot_rows, weights, decay_log, decay_bias, head_gain, blocks, shard_pos):
    (
        norm_in,
        w_query,
        w_key,
        w_value,
        w_decay,
        w_beta,
        w_outgate,
        query_filter,
        key_filter,
        value_filter,
        w_output,
        ffn_gain,
        w_gate,
        w_up,
        w_down,
    ) = weights
    row_count = inputs.shape[0]
    piece_rows = row_count // blocks

    def to_blocks(values):
        return values.reshape(blocks, piece_rows, values.shape[-1])

    residual = inputs.astype(jnp.float32)
    normed, norm_back = jax.vjp(rms_scale, residual, norm_in.astype(jnp.float32))
    normed = normed.astype(jnp.bfloat16)
    query_pre = to_blocks(product(normed, w_query).astype(jnp.bfloat16))
    key_pre = to_blocks(product(normed, w_key).astype(jnp.bfloat16))
    value_pre = to_blocks(product(normed, w_value).astype(jnp.bfloat16))
    decay_pre = to_blocks(product(normed, w_decay).astype(jnp.bfloat16))
    beta_pre = to_blocks(product(normed, w_beta).astype(jnp.bfloat16))
    outgate_pre = product(normed, w_outgate)
    heads_in = (
        lax.all_to_all(query_pre, "seq", split_axis=2, concat_axis=1, tiled=True),
        lax.all_to_all(key_pre, "seq", split_axis=2, concat_axis=1, tiled=True),
        lax.all_to_all(value_pre, "seq", split_axis=2, concat_axis=1, tiled=True),
        lax.all_to_all(decay_pre, "seq", split_axis=2, concat_axis=1, tiled=True),
        lax.all_to_all(beta_pre, "seq", split_axis=2, concat_axis=1, tiled=True),
    )
    qk_cols = heads_in[0].shape[2]
    value_cols = heads_in[2].shape[2]
    local_heads = heads_in[3].shape[2]
    filter_query = lax.dynamic_slice_in_dim(query_filter, shard_pos * qk_cols, qk_cols, 1).astype(
        jnp.float32
    )
    filter_key = lax.dynamic_slice_in_dim(key_filter, shard_pos * qk_cols, qk_cols, 1).astype(
        jnp.float32
    )
    filter_value = lax.dynamic_slice_in_dim(
        value_filter, shard_pos * value_cols, value_cols, 1
    ).astype(jnp.float32)
    decay_here = lax.dynamic_slice_in_dim(decay_log, shard_pos * local_heads, local_heads, 0)
    bias_here = lax.dynamic_slice_in_dim(decay_bias, shard_pos * local_heads, local_heads, 0)
    mixed_heads, mixer_back = jax.vjp(
        mixer,
        heads_in[0].astype(jnp.float32),
        heads_in[1].astype(jnp.float32),
        heads_in[2].astype(jnp.float32),
        heads_in[3].astype(jnp.float32),
        heads_in[4].astype(jnp.float32),
        filter_query,
        filter_key,
        filter_value,
        decay_here,
        bias_here,
    )
    mixed_tok = lax.all_to_all(
        mixed_heads.astype(jnp.bfloat16), "seq", split_axis=1, concat_axis=2, tiled=True
    )
    mixed_rows = mixed_tok.reshape(row_count, mixed_tok.shape[2]).astype(jnp.float32)
    gated_rows, gated_back = jax.vjp(
        gated_norm, mixed_rows, outgate_pre, head_gain.astype(jnp.float32)
    )
    gated_rows = gated_rows.astype(jnp.bfloat16)
    attended = residual + product(gated_rows, w_output)
    ffn_in, ffn_back = jax.vjp(rms_scale, attended, ffn_gain.astype(jnp.float32))
    ffn_in = ffn_in.astype(jnp.bfloat16)
    hidden, hidden_back = jax.vjp(swish_gate, product(ffn_in, w_gate), product(ffn_in, w_up))
    hidden = hidden.astype(jnp.bfloat16)
    output = attended + product(hidden, w_down)
    down_in = cot_rows.astype(jnp.bfloat16)
    down_grad = outer_sum(hidden, down_in)
    gate_back, upper_back = hidden_back(back_through(down_in, w_down))
    gate_back = gate_back.astype(jnp.bfloat16)
    upper_back = upper_back.astype(jnp.bfloat16)
    gate_grad = outer_sum(ffn_in, gate_back)
    up_grad = outer_sum(ffn_in, upper_back)
    attended_back, ffn_gain_grad = ffn_back(
        back_through(gate_back, w_gate) + back_through(upper_back, w_up)
    )
    attended_back = cot_rows + attended_back
    branch_in = attended_back.astype(jnp.bfloat16)
    output_grad = outer_sum(gated_rows, branch_in)
    mixed_back, outgate_back, head_gain_grad = gated_back(back_through(branch_in, w_output))
    heads_back = lax.all_to_all(
        to_blocks(mixed_back.astype(jnp.bfloat16)), "seq", split_axis=2, concat_axis=1, tiled=True
    )
    (
        query_back,
        key_back,
        value_back,
        decay_back,
        beta_back,
        filter_query_grad,
        filter_key_grad,
        filter_value_grad,
        decay_log_local,
        decay_bias_local,
    ) = mixer_back(heads_back.astype(jnp.float32))
    returned = (
        lax.all_to_all(
            query_back.astype(jnp.bfloat16), "seq", split_axis=1, concat_axis=2, tiled=True
        ),
        lax.all_to_all(
            key_back.astype(jnp.bfloat16), "seq", split_axis=1, concat_axis=2, tiled=True
        ),
        lax.all_to_all(
            value_back.astype(jnp.bfloat16), "seq", split_axis=1, concat_axis=2, tiled=True
        ),
        lax.all_to_all(
            decay_back.astype(jnp.bfloat16), "seq", split_axis=1, concat_axis=2, tiled=True
        ),
        lax.all_to_all(
            beta_back.astype(jnp.bfloat16), "seq", split_axis=1, concat_axis=2, tiled=True
        ),
    )
    rows_back = tuple((item.reshape(row_count, item.shape[2]) for item in returned))
    outgate_low = outgate_back.astype(jnp.bfloat16)
    normed_back = back_through(outgate_low, w_outgate)
    for grad_rows, weight in zip(rows_back, (w_query, w_key, w_value, w_decay, w_beta)):
        normed_back = normed_back + back_through(grad_rows, weight)
    input_back, norm_gain_grad = norm_back(normed_back)
    input_grad = attended_back + input_back
    large_grads = (
        norm_gain_grad,
        outer_sum(normed, rows_back[0]),
        outer_sum(normed, rows_back[1]),
        outer_sum(normed, rows_back[2]),
        outer_sum(normed, rows_back[3]),
        outer_sum(normed, rows_back[4]),
        outer_sum(normed, outgate_low),
        place_slice(filter_query_grad, query_filter.shape, shard_pos * qk_cols, 1),
        place_slice(filter_key_grad, key_filter.shape, shard_pos * qk_cols, 1),
        place_slice(filter_value_grad, value_filter.shape, shard_pos * value_cols, 1),
        output_grad,
        ffn_gain_grad,
        gate_grad,
        up_grad,
        down_grad,
    )
    small_grads = (
        head_gain_grad,
        place_slice(decay_log_local, decay_log.shape, shard_pos * local_heads, 0),
        place_slice(decay_bias_local, decay_bias.shape, shard_pos * local_heads, 0),
    )
    return (output, input_grad, large_grads, small_grads)


def body(
    tokens,
    cotangent,
    seq_lengths,
    seq_slots,
    norm_gain,
    w_query,
    w_key,
    w_value,
    w_decay,
    w_beta,
    w_outgate,
    query_filter,
    key_filter,
    value_filter,
    decay_log,
    decay_bias,
    head_gain,
    w_output,
    ffn_gain,
    w_gate,
    w_up,
    w_down,
):
    micro_count = tokens.shape[0]
    slot_count = seq_slots.shape[1]
    group_count = lax.axis_size("fsdp")
    per_group = slot_count // group_count
    group_pos = lax.axis_index("fsdp")
    shard_pos = lax.axis_index("seq")
    piece_rows = cotangent.shape[2]
    width = tokens.shape[3]
    slot_ids = jnp.arange(slot_count, dtype=jnp.int32)
    matches = seq_slots[:, :, None] == slot_ids[None, None, :]
    source_of = jnp.sum(jnp.where(matches, slot_ids[None, :, None], 0), axis=1)
    slot_length = jnp.sum(jnp.where(matches, seq_lengths[:, :, None], 0), axis=1)
    local_length = lax.dynamic_slice_in_dim(slot_length, group_pos * per_group, per_group, 1)
    row_ids = shard_pos * piece_rows + jnp.arange(piece_rows, dtype=jnp.int32)
    valid_rows = (row_ids[None, None, :] < local_length[:, :, None]).astype(jnp.float32)[..., None]
    ordered = jax.vmap(take_rows)(tokens, source_of)
    dealt_rows = lax.all_to_all(ordered, "fsdp", split_axis=1, concat_axis=2, tiled=True)
    outputs = []
    input_grads = []
    large_total = None
    small_total = None
    shard_total = None
    for batch_pos in range(micro_count):
        weights = (
            lax.all_gather(norm_gain, ("seq", "fsdp"), axis=0, tiled=True),
            lax.all_gather(w_query, ("seq", "fsdp"), axis=0, tiled=True),
            lax.all_gather(w_key, ("seq", "fsdp"), axis=0, tiled=True),
            lax.all_gather(w_value, ("seq", "fsdp"), axis=0, tiled=True),
            lax.all_gather(w_decay, ("seq", "fsdp"), axis=0, tiled=True),
            lax.all_gather(w_beta, ("seq", "fsdp"), axis=0, tiled=True),
            lax.all_gather(w_outgate, ("seq", "fsdp"), axis=0, tiled=True),
            lax.all_gather(query_filter, ("seq", "fsdp"), axis=1, tiled=True),
            lax.all_gather(key_filter, ("seq", "fsdp"), axis=1, tiled=True),
            lax.all_gather(value_filter, ("seq", "fsdp"), axis=1, tiled=True),
            lax.all_gather(w_output, ("seq", "fsdp"), axis=1, tiled=True),
            lax.all_gather(ffn_gain, ("seq", "fsdp"), axis=0, tiled=True),
            lax.all_gather(w_gate, ("seq", "fsdp"), axis=0, tiled=True),
            lax.all_gather(w_up, ("seq", "fsdp"), axis=0, tiled=True),
            lax.all_gather(w_down, ("seq", "fsdp"), axis=1, tiled=True),
        )
        rows_in = dealt_rows[batch_pos].reshape(per_group * piece_rows, width)
        cot_rows = (cotangent[batch_pos].astype(jnp.float32) * valid_rows[batch_pos]).reshape(
            per_group * piece_rows, width
        )
        output, input_grad, large_grads, small_grads = run_block(
            rows_in, cot_rows, weights, decay_log, decay_bias, head_gain, per_group, shard_pos
        )
        outputs.append(output.reshape(per_group, piece_rows, width) * valid_rows[batch_pos])
        input_grads.append(input_grad.reshape(per_group, piece_rows, width))
        small_total = (
            small_grads if small_total is None else jax.tree.map(jnp.add, small_total, small_grads)
        )
        large_total = (
            large_grads if large_total is None else jax.tree.map(jnp.add, large_total, large_grads)
        )
    partial_end = (
        lax.psum_scatter(
            large_total[0].astype(jnp.bfloat16), "seq", scatter_dimension=0, tiled=True
        ).astype(jnp.float32),
        lax.psum_scatter(
            large_total[1].astype(jnp.bfloat16), "seq", scatter_dimension=0, tiled=True
        ).astype(jnp.float32),
        lax.psum_scatter(
            large_total[2].astype(jnp.bfloat16), "seq", scatter_dimension=0, tiled=True
        ).astype(jnp.float32),
        lax.psum_scatter(
            large_total[3].astype(jnp.bfloat16), "seq", scatter_dimension=0, tiled=True
        ).astype(jnp.float32),
        lax.psum_scatter(
            large_total[4].astype(jnp.bfloat16), "seq", scatter_dimension=0, tiled=True
        ).astype(jnp.float32),
        lax.psum_scatter(
            large_total[5].astype(jnp.bfloat16), "seq", scatter_dimension=0, tiled=True
        ).astype(jnp.float32),
        lax.psum_scatter(
            large_total[6].astype(jnp.bfloat16), "seq", scatter_dimension=0, tiled=True
        ).astype(jnp.float32),
        lax.psum_scatter(
            large_total[7].astype(jnp.bfloat16), "seq", scatter_dimension=1, tiled=True
        ).astype(jnp.float32),
        lax.psum_scatter(
            large_total[8].astype(jnp.bfloat16), "seq", scatter_dimension=1, tiled=True
        ).astype(jnp.float32),
        lax.psum_scatter(
            large_total[9].astype(jnp.bfloat16), "seq", scatter_dimension=1, tiled=True
        ).astype(jnp.float32),
        lax.psum_scatter(
            large_total[10].astype(jnp.bfloat16), "seq", scatter_dimension=1, tiled=True
        ).astype(jnp.float32),
        lax.psum_scatter(
            large_total[11].astype(jnp.bfloat16), "seq", scatter_dimension=0, tiled=True
        ).astype(jnp.float32),
        lax.psum_scatter(
            large_total[12].astype(jnp.bfloat16), "seq", scatter_dimension=0, tiled=True
        ).astype(jnp.float32),
        lax.psum_scatter(
            large_total[13].astype(jnp.bfloat16), "seq", scatter_dimension=0, tiled=True
        ).astype(jnp.float32),
        lax.psum_scatter(
            large_total[14].astype(jnp.bfloat16), "seq", scatter_dimension=1, tiled=True
        ).astype(jnp.float32),
    )
    shard_total = (
        lax.psum_scatter(
            partial_end[0].astype(jnp.bfloat16), "fsdp", scatter_dimension=0, tiled=True
        ).astype(jnp.float32),
        lax.psum_scatter(
            partial_end[1].astype(jnp.bfloat16), "fsdp", scatter_dimension=0, tiled=True
        ).astype(jnp.float32),
        lax.psum_scatter(
            partial_end[2].astype(jnp.bfloat16), "fsdp", scatter_dimension=0, tiled=True
        ).astype(jnp.float32),
        lax.psum_scatter(
            partial_end[3].astype(jnp.bfloat16), "fsdp", scatter_dimension=0, tiled=True
        ).astype(jnp.float32),
        lax.psum_scatter(
            partial_end[4].astype(jnp.bfloat16), "fsdp", scatter_dimension=0, tiled=True
        ).astype(jnp.float32),
        lax.psum_scatter(
            partial_end[5].astype(jnp.bfloat16), "fsdp", scatter_dimension=0, tiled=True
        ).astype(jnp.float32),
        lax.psum_scatter(
            partial_end[6].astype(jnp.bfloat16), "fsdp", scatter_dimension=0, tiled=True
        ).astype(jnp.float32),
        lax.psum_scatter(
            partial_end[7].astype(jnp.bfloat16), "fsdp", scatter_dimension=1, tiled=True
        ).astype(jnp.float32),
        lax.psum_scatter(
            partial_end[8].astype(jnp.bfloat16), "fsdp", scatter_dimension=1, tiled=True
        ).astype(jnp.float32),
        lax.psum_scatter(
            partial_end[9].astype(jnp.bfloat16), "fsdp", scatter_dimension=1, tiled=True
        ).astype(jnp.float32),
        lax.psum_scatter(
            partial_end[10].astype(jnp.bfloat16), "fsdp", scatter_dimension=1, tiled=True
        ).astype(jnp.float32),
        lax.psum_scatter(
            partial_end[11].astype(jnp.bfloat16), "fsdp", scatter_dimension=0, tiled=True
        ).astype(jnp.float32),
        lax.psum_scatter(
            partial_end[12].astype(jnp.bfloat16), "fsdp", scatter_dimension=0, tiled=True
        ).astype(jnp.float32),
        lax.psum_scatter(
            partial_end[13].astype(jnp.bfloat16), "fsdp", scatter_dimension=0, tiled=True
        ).astype(jnp.float32),
        lax.psum_scatter(
            partial_end[14].astype(jnp.bfloat16), "fsdp", scatter_dimension=1, tiled=True
        ).astype(jnp.float32),
    )
    summed_small = lax.psum((small_total[0], small_total[1], small_total[2]), ("seq", "fsdp"))
    mixed = jnp.stack(outputs)
    slot_grad = jnp.stack(input_grads)
    back_home = lax.all_to_all(
        slot_grad.astype(jnp.bfloat16), "fsdp", split_axis=2, concat_axis=1, tiled=True
    ).astype(slot_grad.dtype)
    tokens_grad = jax.vmap(take_rows)(back_home, seq_slots)
    return (
        mixed,
        tokens_grad,
        shard_total[0],
        shard_total[1],
        shard_total[2],
        shard_total[3],
        shard_total[4],
        shard_total[5],
        shard_total[6],
        shard_total[7],
        shard_total[8],
        shard_total[9],
        summed_small[1],
        summed_small[2],
        summed_small[0],
        shard_total[10],
        shard_total[11],
        shard_total[12],
        shard_total[13],
        shard_total[14],
    )


def solution(mesh):
    placed = (
        P(None, None, ("seq", "fsdp"), None),
        P(None, "fsdp", "seq", None),
        P(),
        P(),
        P(("seq", "fsdp")),
        P(("seq", "fsdp"), None),
        P(("seq", "fsdp"), None),
        P(("seq", "fsdp"), None),
        P(("seq", "fsdp"), None),
        P(("seq", "fsdp"), None),
        P(("seq", "fsdp"), None),
        P(None, ("seq", "fsdp")),
        P(None, ("seq", "fsdp")),
        P(None, ("seq", "fsdp")),
        P(),
        P(),
        P(),
        P(None, ("seq", "fsdp")),
        P(("seq", "fsdp")),
        P(("seq", "fsdp"), None),
        P(("seq", "fsdp"), None),
        P(None, ("seq", "fsdp")),
    )
    return jax.shard_map(
        body,
        mesh=mesh,
        in_specs=placed,
        out_specs=(
            P(None, "fsdp", "seq", None),
            P(None, None, ("seq", "fsdp"), None),
            P(("seq", "fsdp")),
            P(("seq", "fsdp"), None),
            P(("seq", "fsdp"), None),
            P(("seq", "fsdp"), None),
            P(("seq", "fsdp"), None),
            P(("seq", "fsdp"), None),
            P(("seq", "fsdp"), None),
            P(None, ("seq", "fsdp")),
            P(None, ("seq", "fsdp")),
            P(None, ("seq", "fsdp")),
            P(),
            P(),
            P(),
            P(None, ("seq", "fsdp")),
            P(("seq", "fsdp")),
            P(("seq", "fsdp"), None),
            P(("seq", "fsdp"), None),
            P(None, ("seq", "fsdp")),
        ),
        check_vma=False,
    )
```

profile of v0, /device:TPU:0, one launch (start us, length us, event | category | flops | bytes accessed | tf_op | source)
XLA Modules:
  0.0 5004.6 jit_solution(13646425674406399393)
XLA Ops:
  26.3 57.3 %all-reduce.91 = (bf16[1024]{0:T(1024)(128)(2,1)S(1)}, bf16[1024]{0:T(1024)(128)(2,1)S(1)}) all-reduce(bf16[1024]{0:T(1024)(128)(2,1)S(1)} %dynamic-update-slice.10, bf16[1024]{0:T(1024)(128)(2,1)S(1)} %dynamic-update-slice.11), channel_id=1, replica_groups=mesh['seq'=4,'fsdp'=8] {'seq','fsdp'}, use_global_device_ids=true, to_apply=%add.84 | all-reduce | flops 2048 | bytes 8192
  83.7 66.6 %all-gather = bf16[32,32,8]{1,2,0:T(8,128)(2,1)S(1)} all-gather(bf16[1,32,8]{1,2,0:T(8,128)(2,1)S(1)} %bitcast.2748), channel_id=1, replica_groups=mesh['seq'=4,'fsdp'=8] {'seq','fsdp'}, dimensions={0}, use_global_device_ids=true | all-gather | bytes 16896 | tf_op jit(solution)/shard_map/all_gather | solution.py:364
  150.4 63.6 %all-gather.1 = bf16[32,32,4]{1,2,0:T(4,128)(2,1)S(1)} all-gather(bf16[1,32,4]{1,2,0:T(4,128)(2,1)S(1)} %bitcast.2750), channel_id=1, replica_groups=mesh['seq'=4,'fsdp'=8] {'seq','fsdp'}, dimensions={0}, use_global_device_ids=true | all-gather | bytes 8448 | tf_op jit(solution)/shard_map/all_gather | solution.py:368
  214.1 66.4 %all-gather.2 = bf16[32,32,8]{1,2,0:T(8,128)(2,1)S(1)} all-gather(bf16[1,32,8]{1,2,0:T(8,128)(2,1)S(1)} %bitcast.2749), channel_id=1, replica_groups=mesh['seq'=4,'fsdp'=8] {'seq','fsdp'}, dimensions={0}, use_global_device_ids=true | all-gather | bytes 16896 | tf_op jit(solution)/shard_map/all_gather | solution.py:365
  280.7 63.6 %all-gather.3 = bf16[32,64,4]{1,2,0:T(4,128)(2,1)S(1)} all-gather(bf16[1,64,4]{1,2,0:T(4,128)(2,1)S(1)} %bitcast.2751), channel_id=1, replica_groups=mesh['seq'=4,'fsdp'=8] {'seq','fsdp'}, dimensions={0}, use_global_device_ids=true | all-gather | bytes 16896 | tf_op jit(solution)/shard_map/all_gather | solution.py:369
  344.4 65.8 %all-gather.4 = bf16[32,32,4]{1,2,0:T(4,128)(2,1)S(1)} all-gather(bf16[1,32,4]{1,2,0:T(4,128)(2,1)S(1)} %bitcast.2752), channel_id=1, replica_groups=mesh['seq'=4,'fsdp'=8] {'seq','fsdp'}, dimensions={0}, use_global_device_ids=true | all-gather | bytes 8448 | tf_op jit(solution)/shard_map/all_gather | solution.py:367
  639.7 12.7 reduce.290
  768.7 307.1 %while.132 = (s32[]{:T(128)}, f32[1,2,128,256]{3,2,1,0:T(8,128)S(1)}, bf16[16,1,2,64,256]{4,3,2,1,0:T(8,128)(2,1)S(1)}, f32[16,1,2,128,256]{4,3,2,1,0:T(8,128)},...) while((s32[]{:T(128)}, ...), condition=%wide.region_6.9_spmd.clone.clone, body=%wide.region_4.8_spmd.clone.clone.sunk | while | flops 227209280 | bytes 3984097 | solution.py:87
  1109.0 307.0 %while.133 = (s32[]{:T(128)}, f32[1,2,128,256]{3,2,1,0:T(8,128)S(1)}, bf16[16,1,2,64,256]{4,3,2,1,0:T(8,128)(2,1)S(1)}, f32[16,1,2,128,256]{4,3,2,1,0:T(8,128)},...) while((s32[]{:T(128)}, ...), condition=%wide.region_15.18_spmd.clone.clone, body=%wide.region_13.17_spmd.clone.clone.sunk | while | flops 227209280 | bytes 3984097 | solution.py:87
  1445.7 306.4 %while.134 = (s32[]{:T(128)}, f32[1,2,128,256]{3,2,1,0:T(8,128)S(1)}, bf16[16,1,2,64,256]{4,3,2,1,0:T(8,128)(2,1)S(1)}, f32[16,1,2,128,256]{4,3,2,1,0:T(8,128)},...) while((s32[]{:T(128)}, ...), condition=%wide.region_23.26_spmd.clone.clone, body=%wide.region_21.25_spmd.clone.clone.sunk | while | flops 227209280 | bytes 3984097 | solution.py:87
  1948.7 12.2 fusion.586
  2049.6 468.1 %while.131 = (s32[]{:T(128)}, f32[1,2,128,256]{2,3,1,0:T(8,128)}, f32[16,1,2,64,128]{4,3,2,1,0:T(8,128)S(1)}, f32[16,1,2,64,128]{4,3,0,2,1:T(8,128)}, f32[16,1,2...) while((s32[]{:T(128)}, f32[1,2,128,256]{2,3,1,0:T(8,128)}, ...), condition=%wide.region_76.81_spmd.clone, body=%wide.region_64.80_spmd.clone.sunk | while | flops 612070080 | bytes 11443579 | solution.py:87
  2540.9 477.9 %while.130 = (s32[]{:T(128)}, f32[1,2,128,256]{2,3,1,0:T(8,128)}, f32[16,1,2,64,128]{4,3,2,1,0:T(8,128)}, f32[16,1,2,64,128]{4,3,0,2,1:T(8,128)}, f32[16,1,2,64,...) while((s32[]{:T(128)}, f32[1,2,128,256]{2,3,1,0:T(8,128)}, ...), condition=%wide.region_58.63_spmd.clone, body=%wide.region_46.62_spmd.clone.sunk | while | flops 612070080 | bytes 11443579 | solution.py:87
  3054.6 431.6 %while.129 = (s32[]{:T(128)}, f32[1,2,128,256]{2,3,1,0:T(8,128)S(1)}, f32[16,1,2,64,128]{4,3,2,1,0:T(8,128)}, f32[16,1,2,64,128]{4,3,0,2,1:T(8,128)}, f32[16,1,2...) while((s32[]{:T(128)}, ...), condition=%wide.region_40.45_spmd.clone, body=%wide.region_28.44_spmd.clone.sunk | while | flops 612070080 | bytes 11443579 | solution.py:87
  4011.1 19.2 reduce-scatter.77.cloned.1.call-done
  4050.9 37.0 reduce-scatter.69.cloned.1.call-done
  4113.3 31.9 reduce-scatter.73.cloned.1.call-done
  4153.0 39.5 all-reduce.90
  4192.5 17.8 reduce-scatter.85.cloned.1.call-done
  4211.7 62.7 %reduce-scatter.89.cloned.1.call-done = bf16[32,4]{1,0:T(8,128)(2,1)} async-done(((bf16[256,4]{1,0:T(8,128)(2,1)}), bf16[32,4]{1,0:T(8,128)(2,1)}) %reduce-scatter.89.cloned.1.call-update) | async-done | bytes 272
  4275.8 62.1 %reduce-scatter.93.cloned.1.call-done = bf16[64,4]{1,0:T(8,128)(2,1)} async-done(((bf16[512,4]{1,0:T(8,128)(2,1)}), bf16[64,4]{1,0:T(8,128)(2,1)}) %reduce-scatter.93.cloned.1.call-update) | async-done | bytes 528
  4339.3 63.2 %reduce-scatter.79.cloned.1.call-done = bf16[32,8]{1,0:T(8,128)(2,1)} async-done(((bf16[256,8]{1,0:T(8,128)(2,1)}), bf16[32,8]{1,0:T(8,128)(2,1)}) %reduce-scatter.79.cloned.1.call-update) | async-done | bytes 528
  4404.0 63.1 %reduce-scatter.81.cloned.1.call-done = bf16[32,8]{1,0:T(8,128)(2,1)} async-done(((bf16[256,8]{1,0:T(8,128)(2,1)}), bf16[32,8]{1,0:T(8,128)(2,1)}) %reduce-scatter.81.cloned.1.call-update) | async-done | bytes 528
  4474.3 19.5 all-reduce.92
  4504.0 27.7 reduce-scatter.49.cloned.1.call-done
  4533.2 62.8 %reduce-scatter.53.cloned.1.call-done = bf16[32,1024]{1,0:T(8,128)(2,1)} async-done(((bf16[256,1024]{1,0:T(8,128)(2,1)}), bf16[32,1024]{1,0:T(8,128)(2,1)}) %reduce-scatter.53.cloned.1.call-update) | async-done | bytes 65552 | tf_op jit(solution)/shard_map/reduce_scatter | solution.py:445
  4597.5 64.8 %reduce-scatter.95.cloned.1.call-done = bf16[32,2048]{1,0:T(8,128)(2,1)} async-done(((bf16[256,2048]{1,0:T(8,128)(2,1)}), bf16[32,2048]{1,0:T(8,128)(2,1)}) %reduce-scatter.95.cloned.1.call-update) | async-done | bytes 131088
  4664.3 63.6 %reduce-scatter.65.cloned.1.call-done = bf16[32,2048]{1,0:T(8,128)(2,1)} async-done(((bf16[256,2048]{1,0:T(8,128)(2,1)}), bf16[32,2048]{1,0:T(8,128)(2,1)}) %reduce-scatter.65.cloned.1.call-update) | async-done | bytes 131088 | tf_op jit(solution)/shard_map/reduce_scatter | solution.py:457
  4729.5 64.7 %reduce-scatter.57.cloned.1.call-done = bf16[32,2048]{1,0:T(8,128)(2,1)} async-done(((bf16[256,2048]{1,0:T(8,128)(2,1)}), bf16[32,2048]{1,0:T(8,128)(2,1)}) %reduce-scatter.57.cloned.1.call-update) | async-done | bytes 131088 | tf_op jit(solution)/shard_map/reduce_scatter | solution.py:448
  4795.8 65.8 %reduce-scatter.97.cloned.1.call-done = bf16[32,2816]{1,0:T(8,128)(2,1)} async-done(((bf16[256,2816]{1,0:T(8,128)(2,1)}), bf16[32,2816]{1,0:T(8,128)(2,1)}) %reduce-scatter.97.cloned.1.call-update) | async-done | bytes 180240
  4863.9 64.8 %reduce-scatter.71.cloned.1.call-done = bf16[32,2816]{1,0:T(8,128)(2,1)} async-done(((bf16[256,2816]{1,0:T(8,128)(2,1)}), bf16[32,2816]{1,0:T(8,128)(2,1)}) %reduce-scatter.71.cloned.1.call-update) | async-done | bytes 180240 | tf_op jit(solution)/shard_map/reduce_scatter | solution.py:475
  4930.4 65.4 %reduce-scatter.75.cloned.1.call-done = bf16[32,2816]{1,0:T(8,128)(2,1)} async-done(((bf16[256,2816]{1,0:T(8,128)(2,1)}), bf16[32,2816]{1,0:T(8,128)(2,1)}) %reduce-scatter.75.cloned.1.call-update) | async-done | bytes 180240 | tf_op jit(solution)/shard_map/reduce_scatter | solution.py:478
  (4704 shorter events, 3666.5 us)
Async XLA Ops:
  7.2 455.4 %all-gather.14.cloned.1.call-start = ((), (), s32[]{:S(2)}) async-start(), calls=%async_computation.64 | async-start | bytes 2162688 | tf_op jit(solution)/shard_map/all_gather | solution.py:362
  7.9 489.3 %all-gather.18.cloned.1.call-start = ((), (), s32[]{:S(2)}) async-start(), calls=%async_computation.66 | async-start | bytes 2162688 | tf_op jit(solution)/shard_map/all_gather | solution.py:361
  8.7 620.6 %all-gather.16.cloned.1.call-start = ((), (), s32[]{:S(2)}) async-start(), calls=%async_computation.65 | async-start | bytes 4325376 | tf_op jit(solution)/shard_map/all_gather | solution.py:363
  9.4 715.9 %all-gather.20.cloned.1.call-start = ((), (), s32[]{:S(2)}) async-start(), calls=%async_computation.67 | async-start | bytes 4325376 | tf_op jit(solution)/shard_map/all_gather | solution.py:366
  10.0 1822.6 %all-gather.22.cloned.1.call-start = ((), (), s32[]{:S(2)}) async-start(), calls=%async_computation.68 | async-start | bytes 4325376 | tf_op jit(solution)/shard_map/all_gather | solution.py:370
  10.6 1831.7 %all-gather.24.cloned.1.call-start = ((), (), s32[]{:S(2)}) async-start(), calls=%async_computation.69 | async-start | bytes 5947392 | tf_op jit(solution)/shard_map/all_gather | solution.py:372
  11.2 1837.2 %all-gather.26.cloned.1.call-start = ((), (), s32[]{:S(2)}) async-start(), calls=%async_computation.70 | async-start | bytes 5947392 | tf_op jit(solution)/shard_map/all_gather | solution.py:373
  15.0 397.2 %all-to-all-start = ((bf16[3,8,32,1024]{3,2,0,1:T(8,128)(2,1)}), bf16[3,8,32,1024]{3,2,0,1:T(8,128)(2,1)S(1)}, u32[]{:S(2)}, u32[]{:S(2)}) async-start(bf16[3,8,32,1024]{3,2,0,1:T(8,128)(2,1)} %copy.1842), calls=%async_computation | async-start | bytes 3145728 | tf_op jit(solution)/shard_map/all_to_all | solution.py:352
  22.3 1838.8 %all-gather.28.cloned.1.call-start = ((), (), s32[]{:S(2)}) async-start(), calls=%async_computation.71 | async-start | bytes 5947392 | tf_op jit(solution)/shard_map/all_gather | solution.py:374
  1096.3 342.7 %all-to-all-start.6 = ((bf16[4,2,65536]{2,1,0:T(2,128)(2,1)}), bf16[4,2,65536]{2,1,0:T(2,128)(2,1)}, u32[]{:S(2)}, u32[]{:S(2)}) async-start(bf16[4,2,65536]{2,1,0:T(2,128)(2,1)} %reshape.5939), calls=%async_computation.6 | async-start | bytes 2097152 | tf_op jit(solution)/shard_map/all_to_all | solution.py:220
  1439.0 333.4 %all-to-all-start.12 = ((bf16[4,2,65536]{2,1,0:T(2,128)(2,1)}), bf16[4,2,65536]{2,1,0:T(2,128)(2,1)}, u32[]{:S(2)}, u32[]{:S(2)}) async-start(bf16[4,2,65536]{2,1,0:T(2,128)(2,1)} %reshape.5951), calls=%async_computation.12 | async-start | bytes 2097152 | tf_op jit(solution)/shard_map/all_to_all | solution.py:220
  2030.4 487.4 %all-to-all-start.25 = ((bf16[4,2,65536]{2,1,0:T(2,128)(2,1)}), bf16[4,2,65536]{2,1,0:T(2,128)(2,1)}, u32[]{:S(2)}, u32[]{:S(2)}) async-start(bf16[4,2,65536]{2,1,0:T(2,128)(2,1)} %reshape.5977), calls=%async_computation.25 | async-start | bytes 2097152 | tf_op jit(solution)/shard_map/all_to_all | solution.py:248
  2517.7 518.3 %all-to-all-start.19 = ((bf16[4,2,65536]{2,1,0:T(2,128)(2,1)}), bf16[4,2,65536]{2,1,0:T(2,128)(2,1)}, u32[]{:S(2)}, u32[]{:S(2)}) async-start(bf16[4,2,65536]{2,1,0:T(2,128)(2,1)} %reshape.5989), calls=%async_computation.19 | async-start | bytes 2097152 | tf_op jit(solution)/shard_map/all_to_all | solution.py:248
  3567.3 411.8 %reduce-scatter.83.cloned.1.call-start = ((), (), s32[]{:S(2)}) async-start(), calls=%async_computation.90 | async-start | bytes 327680
  3586.1 393.7 %reduce-scatter.87.cloned.1.call-start = ((), (), s32[]{:S(2)}) async-start(), calls=%async_computation.92 | async-start | bytes 327680
  3648.8 331.8 %reduce-scatter.91.cloned.1.call-start = ((), (), s32[]{:S(2)}) async-start(), calls=%async_computation.94 | async-start | bytes 655360
  3686.2 295.0 %reduce-scatter.59.cloned.1.call-start = ((), (), s32[]{:S(2)}) async-start(), calls=%async_computation.78 | async-start | bytes 20480 | tf_op jit(solution)/shard_map/reduce_scatter | solution.py:404
  3699.1 283.6 %reduce-scatter.61.cloned.1.call-start = ((), (), s32[]{:S(2)}) async-start(), calls=%async_computation.79 | async-start | bytes 20480 | tf_op jit(solution)/shard_map/reduce_scatter | solution.py:407
  3700.2 284.0 %reduce-scatter.47.cloned.1.call-start = ((), (), s32[]{:S(2)}) async-start(), calls=%async_computation.72 | async-start | bytes 2621440 | tf_op jit(solution)/shard_map/reduce_scatter | solution.py:395
  3979.8 294.6 %reduce-scatter.89.cloned.1.call-start = ((), (), s32[]{:S(2)}) async-start(), calls=%async_computation.93 | async-start | bytes 73728
  3980.5 357.4 %reduce-scatter.93.cloned.1.call-start = ((), (), s32[]{:S(2)}) async-start(), calls=%async_computation.95 | async-start | bytes 147456
  3981.1 421.5 %reduce-scatter.79.cloned.1.call-start = ((), (), s32[]{:S(2)}) async-start(), calls=%async_computation.88 | async-start | bytes 73728
  3982.6 484.5 %reduce-scatter.81.cloned.1.call-start = ((), (), s32[]{:S(2)}) async-start(), calls=%async_computation.89 | async-start | bytes 73728
  3984.1 547.5 %reduce-scatter.49.cloned.1.call-start = ((), (), s32[]{:S(2)}) async-start(), calls=%async_computation.73 | async-start | bytes 589824 | tf_op jit(solution)/shard_map/reduce_scatter | solution.py:442
  3984.7 611.2 %reduce-scatter.53.cloned.1.call-start = ((), (), s32[]{:S(2)}) async-start(), calls=%async_computation.75 | async-start | bytes 589824 | tf_op jit(solution)/shard_map/reduce_scatter | solution.py:445
  3985.5 676.7 %reduce-scatter.95.cloned.1.call-start = ((), (), s32[]{:S(2)}) async-start(), calls=%async_computation.96 | async-start | bytes 1179648
  3988.1 739.8 %reduce-scatter.65.cloned.1.call-start = ((), (), s32[]{:S(2)}) async-start(), calls=%async_computation.81 | async-start | bytes 1179648 | tf_op jit(solution)/shard_map/reduce_scatter | solution.py:457
  3988.6 805.6 %reduce-scatter.57.cloned.1.call-start = ((), (), s32[]{:S(2)}) async-start(), calls=%async_computation.77 | async-start | bytes 1179648 | tf_op jit(solution)/shard_map/reduce_scatter | solution.py:448
  3995.5 866.1 %reduce-scatter.97.cloned.1.call-start = ((), (), s32[]{:S(2)}) async-start(), calls=%async_computation.97 | async-start | bytes 1622016
  4033.0 895.8 %reduce-scatter.71.cloned.1.call-start = ((), (), s32[]{:S(2)}) async-start(), calls=%async_computation.84 | async-start | bytes 1622016 | tf_op jit(solution)/shard_map/reduce_scatter | solution.py:475
  4097.7 397.3 %all-to-all-start.37 = ((bf16[3,1,256,1024]{3,0,1,2:T(4,128)(2,1)}), bf16[3,1,256,1024]{3,0,1,2:T(4,128)(2,1)}, u32[]{:S(2)}, u32[]{:S(2)}) async-start(bf16[3,1,256,1024]{3,0,1,2:T(4,128)(2,1)} %copy.2055), calls=%async_computation.37 | async-start | bytes 4194304 | tf_op jit(solution)/shard_map/all_to_all | solution.py:488
  4103.3 892.5 %reduce-scatter.75.cloned.1.call-start = ((), (), s32[]{:S(2)}) async-start(), calls=%async_computation.86 | async-start | bytes 1622016 | tf_op jit(solution)/shard_map/reduce_scatter | solution.py:478
  (392 other events, 10141.8 us)
Sparse Core Ops, SparseCore 0:
  11.0 72.4 all-gather.13
  86.5 55.4 all-gather.17
  145.1 60.9 all-gather.15
  209.0 60.6 all-gather.19
  272.5 60.6 all-gather.21
  336.0 65.9 all-gather.23
  404.9 66.3 all-gather.25
  474.2 68.9 all-gather.27
  3607.1 19.9 reduce-scatter.86
  3667.5 19.3 reduce-scatter.90
  3690.2 21.8 reduce-scatter.58
  3736.9 36.6 reduce-scatter.46
  3791.2 29.1 reduce-scatter.50
  3822.9 58.7 reduce-scatter.66
  3884.0 42.6 reduce-scatter.62
  3929.2 43.6 reduce-scatter.54
  3975.5 54.8 reduce-scatter.76
  4032.9 54.8 reduce-scatter.68
  4090.4 54.8 reduce-scatter.72
  4149.0 61.2 reduce-scatter.84
  4214.1 60.2 reduce-scatter.88
  4278.0 59.9 reduce-scatter.92
  4342.3 60.2 reduce-scatter.78
  4406.8 60.2 reduce-scatter.80
  4470.6 60.9 reduce-scatter.48
  4535.0 60.9 reduce-scatter.52
  4599.7 62.4 reduce-scatter.94
  4665.5 62.3 reduce-scatter.64
  4731.7 62.4 reduce-scatter.56
  4797.6 63.9 reduce-scatter.96
  4864.9 63.8 reduce-scatter.70
  4932.2 63.6 reduce-scatter.74
  (2 shorter events, 36.9 us)
where the time goes:
time: 5040 us; the launch traced here: 5000 us
  other arithmetic  1540 us (31%)
  matrix products  1030 us (20%)
  waiting for transfers between devices  896 us (18%)
  local copies, waits for them, and re-layouts  894 us (18%)
  blocking collectives  448 us (9%)
  starting transfers between devices  157 us (3%)
    another operation x384, other arithmetic, span_step(): lax.linalg.triangular_solve(mixing, target, left_side=True, lower=True, u...  1000 us
    unnamed x44, waiting for transfers between devices  409 us
    unnamed x840, local copies, waits for them, and re-layouts  236 us
    unnamed x51, other arithmetic  202 us
    dot_general x192, matrix products, span_step(): jnp.einsum('bhid,bhde->bhie', keys_in, memory, precision=HIGH)  155 us
    squeeze x192, local copies, waits for them, and re-layouts, delta_rule(): lax.scan(jax.checkpoint(span_step), start, (blocks_four(query_in), blocks...  154 us
    dot_general x192, matrix products, span_step(): jnp.einsum('bhid,bhde->bhie', query_in, memory, precision=HIGH)  146 us
    dot_general x192, matrix products, span_step(): jnp.einsum('bhid,bhjd->bhij', query_in, keys_in, precision=HIGH)  115 us

commit v1 on v0

v1 whole, which is shorter than its diff:
```python
import functools
import jax
import jax.numpy as jnp
from jax import lax
from jax.experimental import pallas as pl
from jax.experimental.pallas import tpu as pltpu
from jax.sharding import PartitionSpec as P

EPS = 1e-6
C = 128
KD = 128
VD = 256
F32 = jnp.float32
BF = jnp.bfloat16
HIGHEST = lax.Precision.HIGHEST

def iota(shape, dim):
    return lax.broadcasted_iota(jnp.int32, shape, dim)

def mm(a, b, ca=1, cb=0):
    return lax.dot_general(a.astype(BF), b.astype(BF), (((ca,), (cb,)), ((), ())), preferred_element_type=F32)

def exact(a, b):
    return lax.dot_general(a, b, (((1,), (0,)), ((), ())), precision=HIGHEST, preferred_element_type=F32)

def unit_inverse(low):
    rows, cols = iota((C, C), 0), iota((C, C), 1)
    diag = jnp.where(rows // 16 == cols // 16, low, 0.0)
    packed = jnp.sum(diag.reshape(C // 16, 16, C), axis=0)
    prow, pcol = iota((16, C), 0), iota((16, C), 1)
    inv = jnp.where(prow == pcol % 16, 1.0, 0.0).astype(F32)
    base = (pcol // 16) * 16
    for j in range(15):
        col = jnp.take_along_axis(packed, base + j, axis=1)
        inv = inv - col * inv[j:j + 1, :]
    full = jnp.broadcast_to(inv[None], (C // 16, 16, C)).reshape(C, C)
    full = jnp.where(rows // 16 == cols // 16, full, 0.0)
    size = 16
    while size < C:
        off = jnp.where((rows // (2 * size) == cols // (2 * size)) & (rows // size == cols // size + 1), low, 0.0)
        full = full - mm(mm(full, off), full)
        size *= 2
    return full

def gates(pre, dlog, dbias):
    arg = pre + dbias
    soft = jnp.maximum(arg, 0.0) + jnp.log1p(jnp.exp(-jnp.abs(arg)))
    log_decay = -jnp.exp(dlog) * soft
    rows, cols = iota((C, C), 0), iota((C, C), 1)
    tri = jnp.where(rows >= cols, 1.0, 0.0).astype(F32)
    cum = exact(tri, log_decay)
    return log_decay, cum

def sig(x):
    return 1.0 / (1.0 + jnp.exp(-x))

def conv_taps(ext_ref, taps, width):
    acc = ext_ref[pl.ds(5, C), :] * taps[0:1, :]
    for i in range(1, 4):
        acc = acc + ext_ref[pl.ds(5 + i, C), :] * taps[i:i + 1, :]
    return acc

def load_ext(qkv, halo, ext_ref, first):
    ahead = halo[8:16, :].astype(F32)
    ext_ref[pl.ds(0, 8), :] = jnp.where(first, 0.0, ahead)
    ext_ref[pl.ds(8, C), :] = qkv.astype(F32)

def forward_kernel(heads, micro, qkv_ref, halo_ref, og_ref, db_ref, taps_ref, small_ref, gain_ref,
                   gated_ref, mix_ref, inv_ref, upd_ref, state_ref, mem_ref, ext_ref):
    step = pl.program_id(0)
    first = step == 0

    @pl.when(first)
    def _():
        mem_ref[...] = jnp.zeros_like(mem_ref)

    taps = taps_ref[...]
    rows, cols = iota((C, C), 0), iota((C, C), 1)
    lower = rows >= cols
    gain = gain_ref[0:1, :]
    for m in range(micro):
        ext = ext_ref.at[m]
        load_ext(qkv_ref[m], halo_ref[m], ext, first)
        act = conv_taps(ext, taps, None)
        act = act * sig(act)
        pre = db_ref[m].astype(F32)
        _, cum = gates(pre, small_ref[0:1, :], small_ref[1:2, :])
        rate = sig(pre)
        cum_t = jnp.transpose(cum)
        for h in range(heads):
            u = m * heads + h
            q = act[:, h * KD:(h + 1) * KD]
            k = act[:, (heads + h) * KD:(heads + h + 1) * KD]
            v = act[:, 2 * heads * KD + h * VD:2 * heads * KD + (h + 1) * VD]
            q = q * (lax.rsqrt(jnp.sum(q * q, -1, keepdims=True) + EPS) * KD ** -0.5)
            k = k * lax.rsqrt(jnp.sum(k * k, -1, keepdims=True) + EPS)
            beta = rate[:, heads + h:heads + h + 1]
            gcol = cum[:, h:h + 1]
            grow = cum_t[h:h + 1, :]
            decay = jnp.where(lower, jnp.exp(jnp.where(lower, gcol - grow, 0.0)), 0.0)
            grow_col = jnp.exp(gcol)
            glast = cum[C - 1:C, h:h + 1]
            dots = mm(jnp.concatenate([k, q], 0), k, 1, 1)
            low = jnp.where(rows > cols, beta * decay * dots[:C], 0.0)
            scores = decay * dots[C:]
            inv = unit_inverse(low)
            mem = mem_ref[u]
            state_ref[0, u] = mem.astype(state_ref.dtype)
            from_mem = mm(jnp.concatenate([grow_col * k, grow_col * q], 0), mem)
            upd = mm(inv, beta * (v - from_mem[:C]))
            out = from_mem[C:] + mm(scores, upd)
            mem_ref[u] = jnp.exp(glast) * mem + mm(k * jnp.exp(glast - gcol), upd, 0, 0)
            inv_ref[0, u] = inv.astype(inv_ref.dtype)
            upd_ref[0, u] = upd.astype(upd_ref.dtype)
            mix = out.astype(BF)
            mix_ref[0, u] = mix
            mix = mix.astype(F32)
            og = og_ref[m, :, h * VD:(h + 1) * VD].astype(F32)
            scale = lax.rsqrt(jnp.mean(mix * mix, -1, keepdims=True) + EPS)
            gated = mix * scale * gain * (og * sig(og))
            gated_ref[0, m, :, h * VD:(h + 1) * VD] = gated.astype(BF)


def mixer_forward(pre, taps, small, gain, heads, shards):
    micro, length, _ = pre.shape
    count = length // C
    units = micro * heads
    qkv_cols, v_cols = heads * (2 * KD + VD), heads * VD
    per = count // shards
    lead = (2 * heads * KD + 2 * v_cols) // 128
    return pl.pallas_call(
        functools.partial(forward_kernel, heads, micro),
        grid=(count,),
        in_specs=[
            pl.BlockSpec((micro, C, qkv_cols), lambda c: (0, c, 0)),
            pl.BlockSpec((micro, 16, qkv_cols), lambda c: (0, jnp.maximum(c * (C // 16) - 1, 0), 0)),
            pl.BlockSpec((micro, C, v_cols), lambda c: (0, c, 2)),
            pl.BlockSpec((micro, C, 128), lambda c: (0, c, lead + 0)),
            pl.BlockSpec((8, qkv_cols), lambda c: (0, 0)),
            pl.BlockSpec((8, 128), lambda c: (0, 0)),
            pl.BlockSpec((8, VD), lambda c: (0, 0)),
        ],
        out_specs=[
            pl.BlockSpec((1, micro, C, v_cols), lambda c: (c // per, 0, c % per, 0)),
            pl.BlockSpec((1, units, C, VD), lambda c: (c, 0, 0, 0)),
            pl.BlockSpec((1, units, C, C), lambda c: (c, 0, 0, 0)),
            pl.BlockSpec((1, units, C, VD), lambda c: (c, 0, 0, 0)),
            pl.BlockSpec((1, units, KD, VD), lambda c: (c, 0, 0, 0)),
        ],
        out_shape=[
            jax.ShapeDtypeStruct((shards, micro, length // shards, v_cols), BF),
            jax.ShapeDtypeStruct((count, units, C, VD), BF),
            jax.ShapeDtypeStruct((count, units, C, C), BF),
            jax.ShapeDtypeStruct((count, units, C, VD), BF),
            jax.ShapeDtypeStruct((count, units, KD, VD), BF),
        ],
        scratch_shapes=[
            pltpu.VMEM((units, KD, VD), F32),
            pltpu.VMEM((micro, C + 8, qkv_cols), F32),
        ],
        compiler_params=pltpu.CompilerParams(
            dimension_semantics=("arbitrary",), vmem_limit_bytes=50 * 1024 * 1024
        ),
    )(pre, pre, pre, pre, taps, small, gain)


def backward_kernel(heads, micro, qkv_ref, halo_ref, og_ref, db_ref, dgated_ref, mix_ref, inv_ref, upd_ref, state_ref,
                    taps_ref, small_ref, gain_ref,
                    dpre_ref, dtaps_ref, dsmall_ref, dgain_ref, dmem_ref, ext_ref, dy_ref):
    step = pl.program_id(0)
    count = pl.num_programs(0)

    @pl.when(step == 0)
    def _():
        dmem_ref[...] = jnp.zeros_like(dmem_ref)
        dtaps_ref[...] = jnp.zeros_like(dtaps_ref)
        dsmall_ref[...] = jnp.zeros_like(dsmall_ref)
        dgain_ref[...] = jnp.zeros_like(dgain_ref)

    taps = taps_ref[...]
    rows, cols = iota((C, C), 0), iota((C, C), 1)
    lower = rows >= cols
    upper = jnp.where(rows <= cols, 1.0, 0.0).astype(F32)
    gain = gain_ref[0:1, :]
    qk_cols = heads * KD
    for m in range(micro):
        ext, dy = ext_ref.at[m], dy_ref.at[m]
        load_ext(qkv_ref[m], halo_ref[m], ext, step == count - 1)
        dy[pl.ds(C, 8), :] = jnp.where(step == 0, 0.0, dy[pl.ds(0, 8), :])
        conv = conv_taps(ext, taps, None)
        gate = sig(conv)
        act = conv * gate
        dgate = gate * (1.0 + conv * (1.0 - gate))
        pre = db_ref[m].astype(F32)
        log_decay, cum = gates(pre, small_ref[0:1, :], small_ref[1:2, :])
        rate = sig(pre)
        cum_t = jnp.transpose(cum)
        dcum = jnp.zeros((C, 128), F32)
        drate = jnp.zeros((C, 128), F32)
        for h in range(heads):
            u = m * heads + h
            q0 = act[:, h * KD:(h + 1) * KD]
            k0 = act[:, qk_cols + h * KD:qk_cols + (h + 1) * KD]
            v = act[:, 2 * qk_cols + h * VD:2 * qk_cols + (h + 1) * VD]
            qr = lax.rsqrt(jnp.sum(q0 * q0, -1, keepdims=True) + EPS)
            kr = lax.rsqrt(jnp.sum(k0 * k0, -1, keepdims=True) + EPS)
            qn, k = q0 * qr, k0 * kr
            q = qn * KD ** -0.5
            beta = rate[:, heads + h:heads + h + 1]
            gcol = cum[:, h:h + 1]
            grow = cum_t[h:h + 1, :]
            decay = jnp.where(lower, jnp.exp(jnp.where(lower, gcol - grow, 0.0)), 0.0)
            growth = jnp.exp(gcol)
            glast = cum[C - 1:C, h:h + 1]
            tail = jnp.exp(glast - gcol)
            dots = mm(jnp.concatenate([k, q], 0), k, 1, 1)
            near = jnp.where(rows > cols, decay * dots[:C], 0.0)
            scores = decay * dots[C:]
            mix = mix_ref[0, u].astype(F32)
            og = og_ref[m, :, h * VD:(h + 1) * VD].astype(F32)
            dgated = dgated_ref[0, m, :, h * VD:(h + 1) * VD].astype(F32)
            scale = lax.rsqrt(jnp.mean(mix * mix, -1, keepdims=True) + EPS)
            mixn = mix * scale
            osig = sig(og)
            dog = dgated * mixn * gain * (osig * (1.0 + og * (1.0 - osig)))
            dn = dgated * (og * osig)
            dgain_ref[0:1, :] += jnp.sum(dn * mixn, 0, keepdims=True)
            dn = dn * gain
            dout = scale * (dn - mixn * jnp.mean(dn * mixn, -1, keepdims=True))
            dout = dout.astype(BF)
            upd, mem, inv, dmem = upd_ref[0, u], state_ref[0, u], inv_ref[0, u], dmem_ref[u]
            dmem_low = dmem.astype(BF)
            both = jnp.concatenate([upd, mem], 0)
            one = mm(dout, both, 1, 1)
            dscores = jnp.where(lower, one[:, :C], 0.0)
            dq_in = one[:, C:]
            ktail = k * tail
            dupd = mm(scores, dout, 0, 0) + mm(ktail, dmem_low)
            dres = mm(inv, dupd, 0, 0)
            two = mm(dres, both, 1, 1)
            dlow = jnp.where(rows > cols, -two[:, :C], 0.0)
            dk_in = two[:, C:]
            kin, qin = growth * k, growth * q
            dk_scaled = -beta * dk_in
            dmem_new = jnp.exp(glast) * dmem + mm(qin, dout, 0, 0) - mm(beta * kin, dres, 0, 0)
            dk_tail = mm(upd, dmem_low, 1, 1)
            pull = dscores * scores
            pull_low = dlow * near
            pulls = pull + beta * pull_low
            in_parts = jnp.sum(dq_in * qin + dk_scaled * kin - dk_tail * ktail + pulls, -1, keepdims=True)
            tail_sum = jnp.sum(jnp.sum(dk_tail * ktail, -1, keepdims=True), 0, keepdims=True)
            mem_sum = jnp.sum(jnp.sum(dmem * mem.astype(F32), -1, keepdims=True), 0, keepdims=True)
            dcum_col = in_parts - jnp.transpose(jnp.broadcast_to(jnp.sum(pulls, 0, keepdims=True), (C, C)))[:, 0:1]
            last = iota((C, 1), 0) == C - 1
            dcum_col = dcum_col + jnp.where(last, tail_sum + jnp.exp(glast) * mem_sum, 0.0)
            dbeta = jnp.sum(dres * v, -1, keepdims=True) + jnp.sum(pull_low - dk_in * kin, -1, keepdims=True)
            lane = iota((C, 128), 1)
            dcum = jnp.where(lane == h, dcum_col, dcum)
            drate = jnp.where(lane == heads + h, dbeta, drate)
            dqk = dscores * decay
            dkk = dlow * decay * beta
            left = mm(jnp.concatenate([dqk, dkk], 0), k)
            dq = left[:C] + growth * dq_in
            dk = left[C:] + mm(dqk, q, 0, 0) + mm(dkk, k, 0, 0) + growth * dk_scaled + tail * dk_tail
            dv = beta * dres
            dmem_ref[u] = dmem_new
            dq = dq * KD ** -0.5
            dq = qr * (dq - qn * jnp.sum(dq * qn, -1, keepdims=True))
            dk = kr * (dk - k * jnp.sum(dk * k, -1, keepdims=True))
            for part, at, wide in ((dq, h * KD, KD), (dk, qk_cols + h * KD, KD), (dv, 2 * qk_cols + h * VD, VD)):
                dy[pl.ds(0, C), at:at + wide] = part * dgate[:, at:at + wide]
            at = 2 * qk_cols + heads * VD + h * VD
            dpre_ref[m, :, at:at + VD] = dog.astype(BF)
        grad = dy[pl.ds(0, C), :]
        dx = dy[pl.ds(3, C), :] * taps[0:1, :]
        for i in range(1, 4):
            dx = dx + dy[pl.ds(3 - i, C), :] * taps[i:i + 1, :]
        dpre_ref[m, :, 0:2 * qk_cols + heads * VD] = dx.astype(BF)
        for i in range(4):
            dtaps_ref[i:i + 1, :] += jnp.sum(grad * ext[pl.ds(5 + i, C), :], 0, keepdims=True)
        dlog = exact(upper, dcum)
        speed = -jnp.exp(small_ref[0:1, :])
        ddecay = dlog * speed * sig(pre + small_ref[1:2, :])
        dsmall_ref[0:1, :] += jnp.sum(dlog * log_decay, 0, keepdims=True)
        dsmall_ref[1:2, :] += jnp.sum(ddecay, 0, keepdims=True)
        ddb = ddecay + drate * rate * (1.0 - rate)
        at = 2 * qk_cols + 2 * heads * VD
        dpre_ref[m, :, at:at + 128] = ddb.astype(BF)


def mixer_backward(pre, dgated, saved, taps, small, gain, heads):
    mix, inv, upd, state = saved
    shards, micro, part, v_cols = dgated.shape
    length, width = pre.shape[1:]
    count = length // C
    units = micro * heads
    qkv_cols = heads * (2 * KD + VD)
    per = count // shards
    lead = (2 * heads * KD + 2 * v_cols) // 128
    end = count - 1
    keep = lambda *s: pl.BlockSpec((1, units) + s, lambda c: (end - c, 0, 0, 0))
    return pl.pallas_call(
        functools.partial(backward_kernel, heads, micro),
        grid=(count,),
        in_specs=[
            pl.BlockSpec((micro, C, qkv_cols), lambda c: (0, end - c, 0)),
            pl.BlockSpec((micro, 16, qkv_cols), lambda c: (0, jnp.maximum((end - c) * (C // 16) - 1, 0), 0)),
            pl.BlockSpec((micro, C, v_cols), lambda c: (0, end - c, 2)),
            pl.BlockSpec((micro, C, 128), lambda c: (0, end - c, lead)),
            pl.BlockSpec((1, micro, C, v_cols), lambda c: ((end - c) // per, 0, (end - c) % per, 0)),
            keep(C, VD), keep(C, C), keep(C, VD), keep(KD, VD),
            pl.BlockSpec((8, qkv_cols), lambda c: (0, 0)),
            pl.BlockSpec((8, 128), lambda c: (0, 0)),
            pl.BlockSpec((8, VD), lambda c: (0, 0)),
        ],
        out_specs=[
            pl.BlockSpec((micro, C, width), lambda c: (0, end - c, 0)),
            pl.BlockSpec((8, qkv_cols), lambda c: (0, 0)),
            pl.BlockSpec((8, 128), lambda c: (0, 0)),
            pl.BlockSpec((8, VD), lambda c: (0, 0)),
        ],
        out_shape=[
            jax.ShapeDtypeStruct((micro, length, width), BF),
            jax.ShapeDtypeStruct((8, qkv_cols), F32),
            jax.ShapeDtypeStruct((8, 128), F32),
            jax.ShapeDtypeStruct((8, VD), F32),
        ],
        scratch_shapes=[
            pltpu.VMEM((units, KD, VD), F32),
            pltpu.VMEM((micro, C + 8, qkv_cols), F32),
            pltpu.VMEM((micro, C + 8, qkv_cols), F32),
        ],
        compiler_params=pltpu.CompilerParams(
            dimension_semantics=("arbitrary",), vmem_limit_bytes=50 * 1024 * 1024
        ),
    )(pre, pre, pre, pre, dgated, mix, inv, upd, state, taps, small, gain)


def rms_scale(values, gain):
    return values * lax.rsqrt(jnp.mean(values * values, -1, keepdims=True) + EPS) * gain


def swish_gate(gate_val, upper_val):
    return jax.nn.silu(gate_val) * upper_val


def product(left, right):
    return jnp.dot(left, right, preferred_element_type=F32)


def outer_sum(left, right):
    return lax.dot_general(left, right, (((0,), (0,)), ((), ())), preferred_element_type=F32)


def back_through(left, right):
    return lax.dot_general(left, right, (((1,), (1,)), ((), ())), preferred_element_type=F32)


def take_rows(source, order):
    return jnp.take(source, order, axis=0)


BOTH = ("seq", "fsdp")


def body(tokens, cotangent, seq_lengths, seq_slots, norm_gain, w_query, w_key, w_value, w_decay, w_beta, w_outgate,
         query_filter, key_filter, value_filter, decay_log, decay_bias, head_gain, w_output, ffn_gain, w_gate, w_up, w_down):
    shards, groups = lax.axis_size("seq"), lax.axis_size("fsdp")
    group_pos, shard_pos = lax.axis_index("fsdp"), lax.axis_index("seq")
    micro, slots = seq_slots.shape
    width = tokens.shape[3]
    part = cotangent.shape[2]
    length = part * shards
    own = w_query.shape[0]
    heads = decay_log.shape[0] // shards
    taps_n = query_filter.shape[0]
    lanes = 128

    def by_head(weight):
        return weight.reshape(own, shards, weight.shape[1] // shards)

    def spread(columns):
        return jnp.broadcast_to(columns[:, None, :], (own, shards, columns.shape[1]))

    def filter_columns(taps):
        times = taps.shape[1] // own
        return taps.reshape(taps_n, times, own).transpose(2, 1, 0).reshape(own, times * taps_n)

    filters = jnp.concatenate([filter_columns(query_filter), filter_columns(key_filter), filter_columns(value_filter)], 1)
    extra = jnp.concatenate([norm_gain[:, None], ffn_gain[:, None], filters], 1)
    spare = lanes - 2 * heads - extra.shape[1]
    packed = jnp.concatenate(
        [by_head(w_query), by_head(w_key), by_head(w_value), by_head(w_outgate), by_head(w_decay), by_head(w_beta),
         spread(extra), jnp.zeros((own, shards, spare), BF)], 2).transpose(1, 0, 2)
    packed = lax.all_to_all(packed, "seq", split_axis=0, concat_axis=0, tiled=True)
    w_mixer = lax.all_gather(packed, "fsdp", axis=1, tiled=True).reshape(width, packed.shape[2])
    side = w_mixer[:, w_mixer.shape[1] - lanes:].astype(F32)
    at = 2 * heads
    norm_row, ffn_row = side[:, at], side[:, at + 1]
    rows_of = width // shards
    mine = lax.dynamic_slice_in_dim(side, shard_pos * rows_of, rows_of, 0)[:, at + 2:at + 2 + filters.shape[1]]

    def filter_rows(cols):
        times = cols.shape[1] // taps_n
        return cols.reshape(groups, own, times, taps_n).transpose(3, 0, 2, 1).reshape(taps_n, groups * times * own)

    taps = jnp.concatenate([filter_rows(mine[:, :taps_n]), filter_rows(mine[:, taps_n:2 * taps_n]), filter_rows(mine[:, 2 * taps_n:])], 1)
    taps = jnp.pad(taps, ((0, 8 - taps_n), (0, 0)))
    small = jnp.stack([lax.dynamic_slice_in_dim(decay_log, shard_pos * heads, heads, 0),
                       lax.dynamic_slice_in_dim(decay_bias, shard_pos * heads, heads, 0)])
    small = jnp.pad(small, ((0, 6), (0, lanes - heads)))
    gain = jnp.broadcast_to(head_gain.astype(F32)[None], (8, head_gain.shape[0]))
    w_out_t = lax.all_gather(w_output.T, BOTH, axis=0, tiled=True)
    w_ffn = lax.all_gather(jnp.stack([w_gate, w_up, w_down.T]), BOTH, axis=1, tiled=True)
    w_gate_all, w_up_all, w_down_t = w_ffn[0], w_ffn[1], w_ffn[2]

    slot_ids = jnp.arange(slots, dtype=jnp.int32)
    matches = seq_slots[:, :, None] == slot_ids[None, None, :]
    source_of = jnp.sum(jnp.where(matches, slot_ids[None, :, None], 0), axis=1)
    slot_length = jnp.sum(jnp.where(matches, seq_lengths[:, :, None], 0), axis=1)
    per_group = slots // groups
    units = micro * per_group
    local_length = lax.dynamic_slice_in_dim(slot_length, group_pos * per_group, per_group, 1).reshape(units)
    row_ids = shard_pos * part + jnp.arange(part, dtype=jnp.int32)
    valid = (row_ids[None, :] < local_length[:, None]).astype(F32)[..., None]
    ordered = jax.vmap(take_rows)(tokens, source_of)
    dealt = lax.all_to_all(ordered, "fsdp", split_axis=1, concat_axis=2, tiled=True).reshape(units, part, width)
    rows = units * part
    inputs = dealt.reshape(rows, width)
    everything = lax.all_gather(dealt, "seq", axis=1, tiled=True)

    normed = rms_scale(everything.astype(F32), norm_row).astype(BF).reshape(units * length, width)
    pre = product(normed, w_mixer).astype(BF).reshape(units, length, w_mixer.shape[1])
    gated, *saved = mixer_forward(pre, taps, small, gain, heads, shards)
    gated = lax.all_to_all(gated, "seq", split_axis=0, concat_axis=0, tiled=True)
    v_cols = gated.shape[-1]
    gated = gated.reshape(shards, rows, v_cols).transpose(1, 0, 2).reshape(rows, shards * v_cols)

    residual = inputs.astype(F32)
    attended = residual + back_through(gated, w_out_t)
    ffn_in, ffn_back = jax.vjp(rms_scale, attended, ffn_row)
    ffn_in = ffn_in.astype(BF)
    hidden, hidden_back = jax.vjp(swish_gate, product(ffn_in, w_gate_all), product(ffn_in, w_up_all))
    hidden = hidden.astype(BF)
    output = attended + back_through(hidden, w_down_t)
    mixed = (output.reshape(units, part, width) * valid).reshape(micro, per_group, part, width)
    cot = (cotangent.reshape(units, part, width).astype(F32) * valid).reshape(rows, width)
    down_in = cot.astype(BF)
    down_grad = outer_sum(down_in, hidden).astype(BF)
    gate_back, upper_back = hidden_back(product(down_in, w_down_t))
    gate_back, upper_back = gate_back.astype(BF), upper_back.astype(BF)
    gate_grad = outer_sum(ffn_in, gate_back).astype(BF)
    up_grad = outer_sum(ffn_in, upper_back).astype(BF)
    ffn_sum = lax.psum_scatter(jnp.stack([gate_grad, up_grad, down_grad]), BOTH, scatter_dimension=1, tiled=True)
    attended_back, ffn_gain_grad = ffn_back(back_through(gate_back, w_gate_all) + back_through(upper_back, w_up_all))
    attended_back = cot + attended_back
    branch_in = attended_back.astype(BF)
    output_grad = outer_sum(branch_in, gated).astype(BF)
    output_sum = lax.psum_scatter(output_grad, BOTH, scatter_dimension=0, tiled=True)
    gated_back = product(branch_in, w_out_t).astype(BF)
    gated_back = gated_back.reshape(rows, shards, v_cols).transpose(1, 0, 2).reshape(shards, units, part, v_cols)
    gated_back = lax.all_to_all(gated_back, "seq", split_axis=0, concat_axis=0, tiled=True)

    dpre, dtaps, dsmall, dgain = mixer_backward(pre, gated_back, saved, taps, small, gain, heads)
    dpre = dpre.reshape(units * length, dpre.shape[2])
    partial = back_through(dpre, w_mixer).astype(BF).reshape(units, length, width)
    normed_back = lax.psum_scatter(partial, "seq", scatter_dimension=1, tiled=True).reshape(rows, width).astype(F32)
    dw = outer_sum(normed, dpre)
    main = dw.shape[1] - lanes
    norm_gain_part = jnp.sum(dw * jnp.concatenate([w_mixer[:, :main], w_mixer[:, main:main + at], jnp.zeros((width, lanes - at), BF)], 1).astype(F32), 1) / norm_row

    def grad_columns(grads):
        times = grads.shape[1] // rows_of
        return grads.reshape(taps_n, groups, times, own).transpose(1, 3, 2, 0).reshape(rows_of, times * taps_n)

    qk_cols = heads * KD
    filter_part = jnp.concatenate([grad_columns(dtaps[:taps_n, :qk_cols]), grad_columns(dtaps[:taps_n, qk_cols:2 * qk_cols]), grad_columns(dtaps[:taps_n, 2 * qk_cols:])], 1)
    filter_part = lax.dynamic_update_slice_in_dim(jnp.zeros((width, filter_part.shape[1]), F32), filter_part, shard_pos * rows_of, 0)
    dw = jnp.concatenate([dw[:, :main + at], norm_gain_part[:, None], ffn_gain_grad[:, None], filter_part, jnp.zeros((width, spare), F32)], 1)
    dw = dw.astype(BF).reshape(shards, rows_of, dw.shape[1])
    dw = lax.psum_scatter(dw, "fsdp", scatter_dimension=1, tiled=True)
    dw = lax.all_to_all(dw, "seq", split_axis=0, concat_axis=0, tiled=True).astype(F32)

    def columns(start, stop):
        return dw[:, :, start:stop].transpose(1, 0, 2).reshape(own, shards * (stop - start))

    hv = heads * VD
    query_grad, key_grad = columns(0, qk_cols), columns(qk_cols, 2 * qk_cols)
    value_grad, outgate_grad = columns(2 * qk_cols, 2 * qk_cols + hv), columns(2 * qk_cols + hv, main)
    decay_grad, beta_grad = columns(main, main + heads), columns(main + heads, main + 2 * heads)
    gains = jnp.sum(dw[:, :, main + at:main + at + 2], 0)
    filter_own = lax.dynamic_index_in_dim(dw, shard_pos, 0, keepdims=False)[:, main + at + 2:main + at + 2 + filters.shape[1]]

    def filter_grad(cols):
        times = cols.shape[1] // taps_n
        return cols.reshape(own, times, taps_n).transpose(2, 1, 0).reshape(taps_n, times * own)

    filter_grads = (filter_grad(filter_own[:, :taps_n]), filter_grad(filter_own[:, taps_n:2 * taps_n]), filter_grad(filter_own[:, 2 * taps_n:]))

    def placed(values):
        return lax.dynamic_update_slice_in_dim(jnp.zeros(decay_log.shape, F32), values, shard_pos * heads, 0)

    decay_log_grad, decay_bias_grad, head_gain_grad = lax.psum((placed(dsmall[0, :heads]), placed(dsmall[1, :heads]), dgain[0]), BOTH)

    _, norm_back = jax.vjp(rms_scale, residual, norm_row)
    input_back, _ = norm_back(normed_back)
    slot_grad = (attended_back + input_back).astype(BF).reshape(micro, per_group, part, width)
    home = lax.all_to_all(slot_grad, "fsdp", split_axis=2, concat_axis=1, tiled=True)
    tokens_grad = jax.vmap(take_rows)(home, seq_slots).astype(F32)
    ffn_sum = ffn_sum.astype(F32)
    return (mixed, tokens_grad, gains[:, 0], query_grad, key_grad, value_grad, decay_grad, beta_grad, outgate_grad,
            *filter_grads, decay_log_grad, decay_bias_grad, head_gain_grad, output_sum.astype(F32).T, gains[:, 1],
            ffn_sum[0], ffn_sum[1], ffn_sum[2].T)


def solution(mesh):
    placed = (
        P(None, None, ("seq", "fsdp"), None),
        P(None, "fsdp", "seq", None),
        P(),
        P(),
        P(("seq", "fsdp")),
        P(("seq", "fsdp"), None),
        P(("seq", "fsdp"), None),
        P(("seq", "fsdp"), None),
        P(("seq", "fsdp"), None),
        P(("seq", "fsdp"), None),
        P(("seq", "fsdp"), None),
        P(None, ("seq", "fsdp")),
        P(None, ("seq", "fsdp")),
        P(None, ("seq", "fsdp")),
        P(),
        P(),
        P(),
        P(None, ("seq", "fsdp")),
        P(("seq", "fsdp")),
        P(("seq", "fsdp"), None),
        P(("seq", "fsdp"), None),
        P(None, ("seq", "fsdp")),
    )
    return jax.shard_map(
        body,
        mesh=mesh,
        in_specs=placed,
        out_specs=(
            P(None, "fsdp", "seq", None),
            P(None, None, ("seq", "fsdp"), None),
            P(("seq", "fsdp")),
            P(("seq", "fsdp"), None),
            P(("seq", "fsdp"), None),
            P(("seq", "fsdp"), None),
            P(("seq", "fsdp"), None),
            P(("seq", "fsdp"), None),
            P(("seq", "fsdp"), None),
            P(None, ("seq", "fsdp")),
            P(None, ("seq", "fsdp")),
            P(None, ("seq", "fsdp")),
            P(),
            P(),
            P(),
            P(None, ("seq", "fsdp")),
            P(("seq", "fsdp")),
            P(("seq", "fsdp"), None),
            P(("seq", "fsdp"), None),
            P(None, ("seq", "fsdp")),
        ),
        check_vma=False,
    )
```

time: 5040 us -> 1260 us (0.25)
  other arithmetic: 1540 us -> 34.9 us
  matrix products: 1030 us -> 151 us
  local copies, waits for them, and re-layouts: 894 us -> 43.4 us
  blocking collectives: 448 us -> 147 us
  waiting for transfers between devices: 896 us -> 696 us
  Pallas kernels: 0 us -> 148 us
  starting transfers between devices: 157 us -> 19.2 us
    another operation x634 -> x4, other arithmetic: 1100 us -> 8.35 us  [the longest x1 7.25 us: body(): jnp.stack([gate_grad, up_grad, down_grad])]
    dot_general x1134 -> x5, matrix products: 767 us -> 53.7 us  [product(): return jnp.dot(left, right, preferred_element_type=F32)]
    unnamed x44 -> x8, waiting for transfers between devices: 409 us -> 0.8 us
    all_gather x5 -> x0, blocking collectives: 326 us -> none  [the longest x1 66.6 us: body(): lax.all_gather(w_decay, ('seq', 'fsdp'), axis=0, tiled=True)]
    unnamed x840 -> x74, local copies, waits for them, and re-layouts: 236 us -> 5.02 us
    unnamed x51 -> x1, other arithmetic: 202 us -> 0.01 us
    squeeze x192 -> x0, local copies, waits for them, and re-layouts: 154 us -> none  [delta_rule(): lax.scan(jax.checkpoint(span_step), start, (blocks_four(query_in), blocks...]
    pallas_call x0 -> x2, Pallas kernels: none -> 148 us  [the longest x1 77 us: mixer_backward(): pl.pallas_call(functools.partial(backward_kernel, heads, micro), grid=(co...]
where the time goes in v1:
time: 1260 us
  waiting for transfers between devices  696 us (55%)
  matrix products  151 us (12%)
  Pallas kernels  148 us (12%)
  blocking collectives  147 us (12%)
  local copies, waits for them, and re-layouts  43.4 us (3%)
  other arithmetic  34.9 us (3%)
  starting transfers between devices  19.2 us (2%)
  between operations  15.3 us (1%)
    reduce_scatter x1, waiting for transfers between devices, body(): lax.psum_scatter(jnp.stack([gate_grad, up_grad, down_grad]), BOTH, scatte...  355 us
    reduce_scatter x1, waiting for transfers between devices, body(): lax.psum_scatter(output_grad, BOTH, scatter_dimension=0, tiled=True)  82.4 us
    pallas_call x1, Pallas kernels, mixer_backward(): pl.pallas_call(functools.partial(backward_kernel, heads, micro), grid=(co...  77 us
    pallas_call x1, Pallas kernels, mixer_forward(): pl.pallas_call(functools.partial(forward_kernel, heads, micro), grid=(cou...  70.7 us
    all_to_all x1, blocking collectives, body(): lax.all_to_all(ordered, 'fsdp', split_axis=1, concat_axis=2, tiled=True)  68 us
    psum x1, blocking collectives, body(): lax.psum((placed(dsmall[0, :heads]), placed(dsmall[1, :heads]), dgain[0])...  66.9 us
    reduce_scatter x1, waiting for transfers between devices, body(): lax.psum_scatter(partial, 'seq', scatter_dimension=1, tiled=True)  56.6 us
    dot_general x5, matrix products, product(): return jnp.dot(left, right, preferred_element_type=F32)  53.7 us
  transfers between devices with their start and end apart: 12, of which 9 were waited for; matrix products, arithmetic and copies ran while one was open for 10% of the time, Pallas kernels for 6%

profile of v1, /device:TPU:0, one launch (start us, length us, event | category | flops | bytes accessed | tf_op | source)
XLA Modules:
  0.0 1255.0 jit_solution(1297857017432509712)
XLA Ops:
  13.5 11.9 all_to_all.41
  26.7 68.0 %all_to_all.42 = bf16[3,8,32,1024]{3,2,0,1:T(8,128)(2,1)S(1)} all-to-all(bf16[3,8,32,1024]{3,2,0,1:T(8,128)(2,1)S(1)} %copy.200), channel_id=1, replica_groups=mesh['seq'=4,'fsdp'=8] {'fsdp'}, dimensions={1} | all-to-all | bytes 3145728 | tf_op jit(solution)/shard_map/all_to_all | solution.py:427
  98.1 13.4 %all-gather.7.cloned.1.call-done = bf16[4,256,1664]{2,1,0:T(8,128)(2,1)} async-done(((bf16[4,32,1664]{2,1,0:T(8,128)(2,1)}), bf16[4,256,1664]{2,1,0:T(8,128)(2,1)}) %all-gather.7.cloned.1.call-update) | async-done | bytes 3407888 | tf_op jit(solution)/shard_map/all_gather | solution.py:396
  114.1 43.8 %all-gather.5.cloned.1.call-done = bf16[3,1024,1024]{2,1,0:T(8,128)(2,1)} async-done(((bf16[3,256,1024]{2,1,0:T(8,128)(2,1)}), bf16[3,1024,1024]{2,1,0:T(8,128)(2,1)}) %all-gather.5.cloned.1.call-update) | async-done | bytes 6291472 | tf_op jit(solution)/shard_map/all_gather | solution.py:430
  164.5 13.6 %convolution_convert_fusion = bf16[3072,1664]{1,0:T(8,128)(2,1)} fusion(bf16[3072,1024]{1,0:T(8,128)(2,1)S(1)} %bitcast.243, bf16[1024,1664]{1,0:T(8,128)(2,1)S(1)} %bitcast.284), kind=kOutput, calls=%fused_computation.9 | convolution fusion | flops 10474094592 | bytes 19922944 | tf_op jit(solution)/shard_map/dot_general | solution.py:348
  178.1 70.7 %shard_map.365 = (bf16[4,3,256,512]{3,2,1,0:T(8,128)(2,1)}, bf16[8,6,128,256]{3,2,1,0:T(8,128)(2,1)}, bf16[8,6,128,128]{3,2,1,0:T(8,128)(2,1)S(1)}, bf16[8,6,128...) custom-call(bf16[3,1024,1664]{2,1,0:T(8,128)(2,1)} %bitcast.234, bf16[3,1024,1664]{2,1,0:T(8,128)(2,1)} %bitcast.235, ...), custom_call_target="tpu_custom_call" | custom-call | tf_op jit(solution)/shard_map/pallas_call | solution.py:131
  248.8 4.8 all-to-all-start.2
  257.3 49.0 %all-to-all-done.2 = bf16[4,3,256,512]{3,2,1,0:T(8,128)(2,1)} async-done(((bf16[4,3,256,512]{3,2,1,0:T(8,128)(2,1)}), bf16[4,3,256,512]{3,2,1,0:T(8,128)(2,1)}, u32[]{:S(2)}, u32[]{:S(2)}) %all-to-all-start.2) | async-done | bytes 3145760 | tf_op jit(solution)/shard_map/all_to_all | solution.py:435
  311.0 7.2 multiply_reduce_fusion.3
  321.3 37.7 %all-gather.11.cloned.1.call-done = bf16[3,1024,2816]{2,1,0:T(8,128)(2,1)} async-done(((bf16[3,32,2816]{2,1,0:T(8,128)(2,1)}), bf16[3,1024,2816]{2,1,0:T(8,128)(2,1)}) %all-gather.11.cloned.1.call-update) | async-done | bytes 17301520 | tf_op jit(solution)/shard_map/all_gather | solution.py:414
  359.0 11.2 fusion.8
  370.2 9.6 fusion.10
  379.8 15.6 %multiply_convert_fusion = (bf16[768,2816]{1,0:T(8,128)(2,1)S(1)}, bf16[768,2816]{1,0:T(8,128)(2,1)}, bf16[768,2816]{1,0:T(8,128)(2,1)}) fusion(f32[768,2816]{1,0:T(8,128)} %fusion.8, f32[768,2816]{1,0:T(8,128)} %fusion.10, bf16[768,1024]{1,0:T(8,128)(2,1)S(1)} %bitcast.257, bf16[3,1024,2816]{2,1,0:T(8,128)(2,1)} %all-gather.11.cloned.1.call-done), kind=kOutput, calls=%fused_computation.13 | convolution fusion | flops 4463788032 | bytes 37617664 | tf_op jit(solution)/shard_map/dot_general | solution.py:348
  395.4 9.6 fusion.7
  405.0 7.5 multiply_reduce_fusion.1
  426.2 36.5 %all-to-all-done.3.dgated_ref = bf16[4,3,256,512]{3,2,1,0:T(8,128)(2,1)} async-done(((bf16[4,3,256,512]{3,2,1,0:T(8,128)(2,1)}), bf16[4,3,256,512]{3,2,1,0:T(8,128)(2,1)}, u32[]{:S(2)}, u32[]{:S(2)}) %all-to-all-start.3) | async-done | bytes 3145760 | tf_op jit(solution)/shard_map/all_to_all | solution.py:462
  462.7 77.0 %shard_map.366 = (bf16[3,1024,1664]{2,1,0:T(8,128)(2,1)}, f32[8,1024]{1,0:T(8,128)S(1)}, f32[8,128]{1,0:T(8,128)S(1)}, f32[8,256]{1,0:T(8,128)S(1)}) custom-call(bf16[3,1024,1664]{2,1,0:T(8,128)(2,1)} %bitcast.238, bf16[3,1024,1664]{2,1,0:T(8,128)(2,1)} %bitcast.239, bf16[3,1024,1664]{2,1,0:T(8,128)(2,1)} %bitcast.240, bf16[3,1024,1664]{2,1,0:T(8,128)(2,1)} %bitcast.241, ...), custom_call_target="tpu_custom_call" | custom-call | tf_op jit(solution)/shard_map/pallas_call | solution.py:302
  539.7 18.5 %multiply_reduce_fusion = (f32[1024]{0:T(1024)S(1)}, bf16[1024,1664]{1,0:T(8,128)(2,1)}) fusion(pred[1664]{0:T(1024)(128)(4,1)S(1)} %copy-done.32, bf16[4,256,1664]{2,1,0:T(8,128)(2,1)S(1)} %copy-done.24, bf16[3,1024,1024]{2,1,0:T(8,128)(2,1)} %copy-done.10, bf16[3,1024,1664]{2,1,0:T(8,128)(2,1)} %get-tuple-element.35), kind=kOutput, calls=%fused_computation.18 | convolution fusion | flops 10477501440 | bytes 23336576 | tf_op jit(solution)/shard_map/dot_general | solution.py:352
  559.5 6.6 concatenate.38
  566.1 17.1 %convolution_convert_fusion.1 = bf16[3072,1024]{1,0:T(8,128)(2,1)} fusion(bf16[3072,1664]{1,0:T(8,128)(2,1)} %bitcast.298, bf16[1024,1664]{1,0:T(8,128)(2,1)} %bitcast.283), kind=kOutput, calls=%fused_computation.25 | convolution fusion | flops 10472128512 | bytes 19922944 | tf_op jit(solution)/shard_map/dot_general | solution.py:356
  583.5 8.4 convolution_convert_fusion.2
  593.3 7.4 convert_bitcast_fusion.1
  600.7 7.4 convert_bitcast_fusion.2
  608.2 5.2 convert_bitcast_fusion
  613.4 7.2 pad_maximum_fusion
  621.4 20.6 %reduce-scatter.7.cloned.1.call-done = bf16[4,32,1664]{2,1,0:T(8,128)(2,1)} async-done(((bf16[4,256,1664]{2,1,0:T(8,128)(2,1)}), bf16[4,32,1664]{2,1,0:T(8,128)(2,1)}) %reduce-scatter.7.cloned.1.call-update) | async-done | bytes 426000 | tf_op jit(solution)/shard_map/reduce_scatter | solution.py:481
  645.7 56.6 %reduce-scatter.5.cloned.1.call-done = bf16[3,256,1024]{2,1,0:T(8,128)(2,1)} async-done(((bf16[3,1024,1024]{2,1,0:T(8,128)(2,1)}), bf16[3,256,1024]{2,1,0:T(8,128)(2,1)}) %reduce-scatter.5.cloned.1.call-update) | async-done | bytes 1572880 | tf_op jit(solution)/shard_map/reduce_scatter | solution.py:467
  710.6 5.5 all-to-all-start.4
  716.2 9.5 fusion.20
  727.8 66.9 %all-reduce.2 = (f32[8]{0:T(128)}, f32[8]{0:T(128)}, f32[256]{0:T(256)}) all-reduce(f32[8]{0:T(128)S(1)} %bitcast_dynamic-update-slice_fusion.1, f32[8]{0:T(128)S(1)} %bitcast_dynamic-update-slice_fusion, f32[256]{0:T(256)S(1)} %bitcast.291), channel_id=1, replica_groups=mesh['seq'=4,'fsdp'=8] {'seq','fsdp'}, use_global_device_ids=true, to_apply=%region_12.14 | all-reduce | flops 272 | bytes 2176 | tf_op jit(solution)/shard_map/psum | solution.py:503
  794.7 82.4 %reduce-scatter.9.cloned.1.call-done = bf16[32,2048]{1,0:T(8,128)(2,1)} async-done(((bf16[1024,2048]{1,0:T(8,128)(2,1)}), bf16[32,2048]{1,0:T(8,128)(2,1)}) %reduce-scatter.9.cloned.1.call-update) | async-done | bytes 131088 | tf_op jit(solution)/shard_map/reduce_scatter | solution.py:459
  890.2 355.4 %reduce-scatter.11.cloned.1.call-done = bf16[3,32,2816]{2,1,0:T(8,128)(2,1)} async-done(((bf16[3,1024,2816]{2,1,0:T(8,128)(2,1)}), bf16[3,32,2816]{2,1,0:T(8,128)(2,1)}) %reduce-scatter.11.cloned.1.call-update) | async-done | bytes 540688 | tf_op jit(solution)/shard_map/reduce_scatter | solution.py:454
  (205 shorter events, 77.9 us)
Async XLA Ops:
  7.2 18.5 %copy-start = (bf16[3,8,32,1024]{3,2,1,0:T(8,128)(2,1)S(1)}, bf16[3,8,32,1024]{3,2,1,0:T(8,128)(2,1)}, u32[]{:S(2)}) copy-start(bf16[3,8,32,1024]{3,2,1,0:T(8,128)(2,1)} %param.24) | copy-start | bytes 4718596
  7.2 18.3 %copy-start.27 = (s32[3,8]{1,0:T(4,128)S(1)}, s32[3,8]{1,0:T(4,128)}, u32[]{:S(2)}) copy-start(s32[3,8]{1,0:T(4,128)} %param.26) | copy-start | bytes 292
  7.2 18.3 %copy-start.25 = (s32[3,8]{1,0:T(4,128)S(1)}, s32[3,8]{1,0:T(4,128)}, u32[]{:S(2)}) copy-start(s32[3,8]{1,0:T(4,128)} %param.27) | copy-start | bytes 292
  7.2 104.2 %all-gather.7.cloned.1.call-start = ((), (), s32[]{:S(2)}) async-start(), calls=%async_computation.11 | async-start | bytes 3833856 | tf_op jit(solution)/shard_map/all_gather | solution.py:396
  25.4 132.5 %all-gather.5.cloned.1.call-start = ((), (), s32[]{:S(2)}) async-start(), calls=%async_computation.10 | async-start | bytes 7864320 | tf_op jit(solution)/shard_map/all_gather | solution.py:430
  96.2 214.8 %all-gather.9.cloned.1.call-start = ((), (), s32[]{:S(2)}) async-start(), calls=%async_computation.12 | async-start | bytes 4325376 | tf_op jit(solution)/shard_map/all_gather | solution.py:413
  97.0 262.0 %all-gather.11.cloned.1.call-start = ((), (), s32[]{:S(2)}) async-start(), calls=%async_computation.13 | async-start | bytes 17842176 | tf_op jit(solution)/shard_map/all_gather | solution.py:414
  112.5 49.7 %copy-start.8 = (f32[1024,128]{1,0:T(8,128)}, f32[1024,128]{1,0:T(8,128)S(1)}, u32[]{:S(2)}) copy-start(f32[1024,128]{1,0:T(8,128)S(1)} %slice_convert_fusion.1) | copy-start | bytes 1572868
  114.1 48.1 %copy-start.19 = (f32[1024]{0:T(1024)}, f32[1024]{0:T(1024)S(1)}, u32[]{:S(2)}) copy-start(f32[1024]{0:T(1024)S(1)} %get-tuple-element.44) | copy-start | bytes 12292
  164.2 13.9 %copy-start.10 = (bf16[3,1024,1024]{2,1,0:T(8,128)(2,1)}, bf16[3,1024,1024]{2,1,0:T(8,128)(2,1)S(1)}, u32[]{:S(2)}) copy-start(bf16[3,1024,1024]{2,1,0:T(8,128)(2,1)S(1)} %fusion.2) | copy-start | bytes 18874372
  164.5 13.6 %copy-start.30 = (bf16[256]{0:T(256)(128)(2,1)S(1)}, bf16[256]{0:T(256)(128)(2,1)}, u32[]{:S(2)}) copy-start(bf16[256]{0:T(256)(128)(2,1)} %param.40) | copy-start | bytes 1540
  248.8 57.5 %all-to-all-start.2 = ((bf16[4,3,256,512]{3,2,1,0:T(8,128)(2,1)}), bf16[4,3,256,512]{3,2,1,0:T(8,128)(2,1)}, u32[]{:S(2)}, u32[]{:S(2)}) async-start(bf16[4,3,256,512]{3,2,1,0:T(8,128)(2,1)} %get-tuple-element.30), calls=%async_computation.2 | async-start | bytes 6291456 | tf_op jit(solution)/shard_map/all_to_all | solution.py:435
  254.0 56.9 %copy-start.21 = (f32[3,256]{1,0:T(4,128)}, f32[3,256]{1,0:T(4,128)S(1)}, u32[]{:S(2)}) copy-start(f32[3,256]{1,0:T(4,128)S(1)} %compare_convert_fusion.1) | copy-start | bytes 9220
  359.0 11.2 copy-start.14
  370.2 9.6 copy-start.13
  395.4 9.6 copy-start.33
  395.4 9.6 copy-start.6
  421.0 41.7 %all-to-all-start.3 = ((bf16[4,3,256,512]{3,2,1,0:T(8,128)(2,1)}), bf16[4,3,256,512]{3,2,1,0:T(8,128)(2,1)}, u32[]{:S(2)}, u32[]{:S(2)}) async-start(bf16[4,3,256,512]{3,2,1,0:T(8,128)(2,1)} %bitcast.242), calls=%async_computation.3 | async-start | bytes 6291456 | tf_op jit(solution)/shard_map/all_to_all | solution.py:462
  425.7 216.3 %reduce-scatter.7.cloned.1.call-start = ((), (), s32[]{:S(2)}) async-start(), calls=%async_computation.15 | async-start | bytes 3833856 | tf_op jit(solution)/shard_map/reduce_scatter | solution.py:481
  462.7 77.0 %copy-start.24 = (bf16[4,256,1664]{2,1,0:T(8,128)(2,1)S(1)}, bf16[4,256,1664]{2,1,0:T(8,128)(2,1)}, u32[]{:S(2)}) copy-start(bf16[4,256,1664]{2,1,0:T(8,128)(2,1)} %all-gather.7.cloned.1.call-done) | copy-start | bytes 10223620
  462.7 77.0 %copy-start.32 = (pred[1664]{0:T(1024)(128)(4,1)S(1)}, pred[1664]{0:T(1024)(128)(4,1)}, u32[]{:S(2)}) copy-start(pred[1664]{0:T(1024)(128)(4,1)} %constant.59.clone.1) | copy-start | bytes 4996
  539.7 18.7 %copy-start.9 = (f32[1024,128]{1,0:T(8,128)S(1)}, f32[1024,128]{1,0:T(8,128)}, u32[]{:S(2)}) copy-start(f32[1024,128]{1,0:T(8,128)} %copy-done.8) | copy-start | bytes 1572868
  566.1 136.2 %reduce-scatter.5.cloned.1.call-start = ((), (), s32[]{:S(2)}) async-start(), calls=%async_computation.14 | async-start | bytes 7864320 | tf_op jit(solution)/shard_map/reduce_scatter | solution.py:467
  583.2 293.9 %reduce-scatter.9.cloned.1.call-start = ((), (), s32[]{:S(2)}) async-start(), calls=%async_computation.16 | async-start | bytes 4325376 | tf_op jit(solution)/shard_map/reduce_scatter | solution.py:459
  591.9 653.7 %reduce-scatter.11.cloned.1.call-start = ((), (), s32[]{:S(2)}) async-start(), calls=%async_computation.17 | async-start | bytes 17842176 | tf_op jit(solution)/shard_map/reduce_scatter | solution.py:454
  593.3 14.8 %slice-start = ((s8[4325376]{0:T(1024)(128)(4,1)}), s8[4194304]{0:T(1024)(128)(4,1)S(1)}, s32[]{:S(2)}) async-start(s8[4325376]{0:T(1024)(128)(4,1)} %bitcast.299), calls=%async_computation.18 | async-start | bytes 8388608
  620.6 81.7 %copy-start.4 = (bf16[3,8,32,1024]{3,2,0,1:T(8,128)(2,1)S(1)}, bf16[3,8,32,1024]{3,2,0,1:T(8,128)(2,1)}, u32[]{:S(2)}) copy-start(bf16[3,8,32,1024]{3,2,0,1:T(8,128)(2,1)} %copy-done.3) | copy-start | bytes 4718596
  620.6 81.7 %copy-start.20 = (f32[1024]{0:T(1024)S(1)}, f32[1024]{0:T(1024)}, u32[]{:S(2)}) copy-start(f32[1024]{0:T(1024)} %copy-done.19) | copy-start | bytes 12292
  642.0 68.6 %all-to-all-start.5 = ((bf16[4,32,1664]{2,1,0:T(8,128)(2,1)}), bf16[4,32,1664]{2,1,0:T(8,128)(2,1)S(1)}, u32[]{:S(2)}, u32[]{:S(2)}) async-start(bf16[4,32,1664]{2,1,0:T(8,128)(2,1)} %reduce-scatter.7.cloned.1.call-done), calls=%async_computation.7 | async-start | bytes 851968 | tf_op jit(solution)/shard_map/all_to_all | solution.py:482
  710.6 174.8 %all-to-all-start.4 = ((bf16[3,1,256,1024]{3,0,1,2:T(4,128)(2,1)}), bf16[3,1,256,1024]{3,0,1,2:T(4,128)(2,1)}, u32[]{:S(2)}, u32[]{:S(2)}) async-start(bf16[3,1,256,1024]{3,0,1,2:T(4,128)(2,1)} %copy.218), calls=%async_computation.5 | async-start | bytes 4194304 | tf_op jit(solution)/shard_map/all_to_all | solution.py:508
  716.1 9.5 copy-start.22
  888.3 359.5 %copy-start.1 = (bf16[3,8,32,1024]{3,2,1,0:T(8,128)(2,1)S(1)}, bf16[3,8,32,1024]{3,2,1,0:T(8,128)(2,1)}, u32[]{:S(2)}) copy-start(bf16[3,8,32,1024]{3,2,1,0:T(8,128)(2,1)} %param.24) | copy-start | bytes 4718596
  (16 other events, 56.3 us)
Sparse Core Ops, SparseCore 0:
  25.5 85.9 all-gather.6
  113.0 44.8 all-gather.4
  161.0 62.3 all-gather.8
  226.2 132.7 all-gather.10
  566.2 75.7 reduce-scatter.6
  644.6 57.6 reduce-scatter.4
  704.6 172.4 reduce-scatter.8
  879.4 366.1 reduce-scatter.10

commit v2 on v1

--- a/solution.py
+++ b/solution.py
@@ -336,6 +336,130 @@
     )(pre, pre, pre, pre, dgated, mix, inv, upd, state, taps, small, gain)
 
 
+MESH_ID = pl.DeviceIdType.MESH
+
+
+def start_kernel(shards, groups, rows_y, micro, tok_ref, pack_ref, every_ref, wm_ref,
+                 local_sem, send_sem, one_sem, z_sem, y_sem, deal_sem, swap_sem):
+    s, f = lax.axis_index("seq"), lax.axis_index("fsdp")
+    deep = groups // rows_y
+    z, y = f // rows_y, lax.rem(f, rows_y)
+    barrier = pltpu.get_barrier_semaphore()
+    for d in range(1, shards):
+        pl.semaphore_signal(barrier, inc=1, device_id=(jnp.bitwise_xor(s, d), f), device_id_type=MESH_ID)
+    for k in range(1, groups):
+        pl.semaphore_signal(barrier, inc=1, device_id=(s, lax.rem(f + k, groups)), device_id_type=MESH_ID)
+    pl.semaphore_wait(barrier, shards + groups - 2)
+
+    sent = []
+
+    def send(src, dst, sem, device):
+        at = len(sent)
+        copy = pltpu.make_async_remote_copy(src, dst, send_sem.at[at], sem, device_id=device, device_id_type=MESH_ID)
+        copy.start()
+        sent.append(copy)
+        return copy
+
+    place = wm_ref.at[s, z, y]
+    first = []
+    for d in range(1, shards):
+        to = jnp.bitwise_xor(s, d)
+        first.append(send(pack_ref.at[to], place, one_sem.at[d], (to, f)))
+    mine = pltpu.make_async_copy(pack_ref.at[s], place, local_sem.at[0])
+    mine.start()
+    keeps = []
+    for m in range(micro):
+        keep = pltpu.make_async_copy(tok_ref.at[m, f], every_ref.at[m, s, f], local_sem.at[1 + m])
+        keep.start()
+        keeps.append(keep)
+
+    def deal(m):
+        return [send(tok_ref.at[m, lax.rem(f + k, groups)], every_ref.at[m, s, f], deal_sem.at[m, k],
+                     (s, lax.rem(f + k, groups))) for k in range(1, groups)]
+
+    dealt = [deal(0)]
+    columns = []
+    mine.wait()
+    for d in range(shards):
+        block = jnp.bitwise_xor(s, d)
+        if d:
+            first[d - 1].wait_recv()
+        columns.append([send(wm_ref.at[block, z, y], wm_ref.at[block, z, y], z_sem.at[d, k],
+                             (s, lax.rem(z + k, deep) * rows_y + y)) for k in range(1, deep)])
+    for m in range(1, micro):
+        dealt.append(deal(m))
+
+    bits = []
+    bit = shards // 2
+    while bit:
+        bits.append(bit)
+        bit //= 2
+
+    def swap(m, level):
+        bit = bits[level]
+        held = [0]
+        for b in bits[:level]:
+            held = held + [h | b for h in held]
+        return [send(every_ref.at[m, jnp.bitwise_xor(s, h)], every_ref.at[m, jnp.bitwise_xor(s, h)],
+                     swap_sem.at[m, level, i], (jnp.bitwise_xor(s, bit), f)) for i, h in enumerate(held)]
+
+    rows_of = []
+    swaps = {}
+    for m in range(micro):
+        keeps[m].wait()
+        for copy in dealt[m]:
+            copy.wait_recv()
+        swaps[m, 0] = swap(m, 0)
+        if m == 0:
+            for d in range(shards):
+                block = jnp.bitwise_xor(s, d)
+                for copy in columns[d]:
+                    copy.wait_recv()
+                rows_of.append([send(wm_ref.at[block, :, y], wm_ref.at[block, :, y], y_sem.at[d, j],
+                                     (s, z * rows_y + lax.rem(y + j, rows_y))) for j in range(1, rows_y)])
+    for level in range(1, len(bits)):
+        for m in range(micro):
+            for copy in swaps[m, level - 1]:
+                copy.wait_recv()
+            swaps[m, level] = swap(m, level)
+    for m in range(micro):
+        for copy in swaps[m, len(bits) - 1]:
+            copy.wait_recv()
+    for d in range(shards):
+        for copy in rows_of[d]:
+            copy.wait_recv()
+    for copy in sent:
+        copy.wait_send()
+
+
+def start_exchange(tok, pack, shards, groups):
+    micro, _, own, width = tok.shape
+    rows_y = max(shards // 2, 1)
+    deep = groups // rows_y
+    levels = max(shards.bit_length() - 1, 1)
+    copies = (shards - 1) + micro * (groups - 1) + shards * (deep - 1) + shards * (rows_y - 1) + micro * (shards - 1)
+    hbm = pl.BlockSpec(memory_space=pl.ANY)
+    return pl.pallas_call(
+        functools.partial(start_kernel, shards, groups, rows_y, micro),
+        in_specs=[hbm, hbm],
+        out_specs=[hbm, hbm],
+        out_shape=[
+            jax.ShapeDtypeStruct((micro, shards, groups, own, width), tok.dtype),
+            jax.ShapeDtypeStruct((shards, deep, rows_y) + pack.shape[1:], pack.dtype),
+        ],
+        scratch_shapes=[
+            pltpu.SemaphoreType.DMA((1 + micro,)),
+            pltpu.SemaphoreType.DMA((copies,)),
+            pltpu.SemaphoreType.DMA((shards,)),
+            pltpu.SemaphoreType.DMA((shards, deep)),
+            pltpu.SemaphoreType.DMA((shards, rows_y)),
+            pltpu.SemaphoreType.DMA((micro, groups)),
+            pltpu.SemaphoreType.DMA((micro, levels, max(shards // 2, 1))),
+        ],
+        compiler_params=pltpu.CompilerParams(collective_id=0, has_side_effects=True),
+    )(tok, pack)
+
+
 def rms_scale(values, gain):
     return values * lax.rsqrt(jnp.mean(values * values, -1, keepdims=True) + EPS) * gain
 
@@ -361,6 +485,26 @@
 
 
 BOTH = ("seq", "fsdp")
+
+
+def bits_of(size):
+    return [1 << i for i in reversed(range(size.bit_length() - 1))]
+
+
+def reduce_halves(values, names, sizes, order):
+    left = [(name, bit) for name, size in zip(names, sizes) for bit in bits_of(size)]
+    values = values.reshape((2,) * len(left) + values.shape[len(names):])
+    for name, bit in order:
+        at = left.index((name, bit))
+        side = (lax.axis_index(name) // bit) % 2
+        away = lax.dynamic_index_in_dim(values, 1 - side, at, keepdims=False)
+        kept = lax.dynamic_index_in_dim(values, side, at, keepdims=False)
+        came = lax.ppermute(away, name, [(i, i ^ bit) for i in range(sizes[names.index(name)])])
+        values = kept.astype(F32) + came.astype(F32)
+        left.pop(at)
+        if left:
+            values = values.astype(BF)
+    return values
 
 
 def body(tokens, cotangent, seq_lengths, seq_slots, norm_gain, w_query, w_key, w_value, w_decay, w_beta, w_outgate,
@@ -392,8 +536,21 @@
     packed = jnp.concatenate(
         [by_head(w_query), by_head(w_key), by_head(w_value), by_head(w_outgate), by_head(w_decay), by_head(w_beta),
          spread(extra), jnp.zeros((own, shards, spare), BF)], 2).transpose(1, 0, 2)
-    packed = lax.all_to_all(packed, "seq", split_axis=0, concat_axis=0, tiled=True)
-    w_mixer = lax.all_gather(packed, "fsdp", axis=1, tiled=True).reshape(width, packed.shape[2])
+
+    slot_ids = jnp.arange(slots, dtype=jnp.int32)
+    matches = seq_slots[:, :, None] == slot_ids[None, None, :]
+    source_of = jnp.sum(jnp.where(matches, slot_ids[None, :, None], 0), axis=1)
+    slot_length = jnp.sum(jnp.where(matches, seq_lengths[:, :, None], 0), axis=1)
+    units = micro
+    local_length = lax.dynamic_slice_in_dim(slot_length, group_pos, 1, 1).reshape(units)
+    row_ids = shard_pos * part + jnp.arange(part, dtype=jnp.int32)
+    valid = (row_ids[None, :] < local_length[:, None]).astype(F32)[..., None]
+    ordered = jax.vmap(take_rows)(tokens, source_of)
+    everything, w_mixer = start_exchange(ordered, packed, shards, groups)
+    everything = everything.reshape(units, length, width)
+    w_mixer = w_mixer.reshape(width, packed.shape[2])
+    rows = units * part
+    inputs = lax.dynamic_slice_in_dim(everything, shard_pos * part, part, 1).reshape(rows, width)
     side = w_mixer[:, w_mixer.shape[1] - lanes:].astype(F32)
     at = 2 * heads
     norm_row, ffn_row = side[:, at], side[:, at + 1]
@@ -410,24 +567,12 @@
                        lax.dynamic_slice_in_dim(decay_bias, shard_pos * heads, heads, 0)])
     small = jnp.pad(small, ((0, 6), (0, lanes - heads)))
     gain = jnp.broadcast_to(head_gain.astype(F32)[None], (8, head_gain.shape[0]))
-    w_out_t = lax.all_gather(w_output.T, BOTH, axis=0, tiled=True)
-    w_ffn = lax.all_gather(jnp.stack([w_gate, w_up, w_down.T]), BOTH, axis=1, tiled=True)
-    w_gate_all, w_up_all, w_down_t = w_ffn[0], w_ffn[1], w_ffn[2]
-
-    slot_ids = jnp.arange(slots, dtype=jnp.int32)
-    matches = seq_slots[:, :, None] == slot_ids[None, None, :]
-    source_of = jnp.sum(jnp.where(matches, slot_ids[None, :, None], 0), axis=1)
-    slot_length = jnp.sum(jnp.where(matches, seq_lengths[:, :, None], 0), axis=1)
-    per_group = slots // groups
-    units = micro * per_group
-    local_length = lax.dynamic_slice_in_dim(slot_length, group_pos * per_group, per_group, 1).reshape(units)
-    row_ids = shard_pos * part + jnp.arange(part, dtype=jnp.int32)
-    valid = (row_ids[None, :] < local_length[:, None]).astype(F32)[..., None]
-    ordered = jax.vmap(take_rows)(tokens, source_of)
-    dealt = lax.all_to_all(ordered, "fsdp", split_axis=1, concat_axis=2, tiled=True).reshape(units, part, width)
-    rows = units * part
-    inputs = dealt.reshape(rows, width)
-    everything = lax.all_gather(dealt, "seq", axis=1, tiled=True)
+    dense = jnp.concatenate([w_gate, w_up, w_down.T, w_output.T], 1)
+    dense, everything = lax.optimization_barrier((dense, everything))
+    w_dense = lax.all_gather(dense, BOTH, axis=0, tiled=True)
+    hidden_n = w_gate.shape[1]
+    w_gate_all, w_up_all = w_dense[:, :hidden_n], w_dense[:, hidden_n:2 * hidden_n]
+    w_down_t, w_out_t = w_dense[:, 2 * hidden_n:3 * hidden_n], w_dense[:, 3 * hidden_n:]
 
     normed = rms_scale(everything.astype(F32), norm_row).astype(BF).reshape(units * length, width)
     pre = product(normed, w_mixer).astype(BF).reshape(units, length, w_mixer.shape[1])
@@ -443,7 +588,7 @@
     hidden, hidden_back = jax.vjp(swish_gate, product(ffn_in, w_gate_all), product(ffn_in, w_up_all))
     hidden = hidden.astype(BF)
     output = attended + back_through(hidden, w_down_t)
-    mixed = (output.reshape(units, part, width) * valid).reshape(micro, per_group, part, width)
+    mixed = (output.reshape(units, part, width) * valid).reshape(micro, 1, part, width)
     cot = (cotangent.reshape(units, part, width).astype(F32) * valid).reshape(rows, width)
     down_in = cot.astype(BF)
     down_grad = outer_sum(down_in, hidden).astype(BF)
@@ -451,20 +596,25 @@
     gate_back, upper_back = gate_back.astype(BF), upper_back.astype(BF)
     gate_grad = outer_sum(ffn_in, gate_back).astype(BF)
     up_grad = outer_sum(ffn_in, upper_back).astype(BF)
-    ffn_sum = lax.psum_scatter(jnp.stack([gate_grad, up_grad, down_grad]), BOTH, scatter_dimension=1, tiled=True)
     attended_back, ffn_gain_grad = ffn_back(back_through(gate_back, w_gate_all) + back_through(upper_back, w_up_all))
     attended_back = cot + attended_back
     branch_in = attended_back.astype(BF)
     output_grad = outer_sum(branch_in, gated).astype(BF)
-    output_sum = lax.psum_scatter(output_grad, BOTH, scatter_dimension=0, tiled=True)
+    dense_grad = jnp.concatenate([gate_grad, up_grad, down_grad], 1)
     gated_back = product(branch_in, w_out_t).astype(BF)
     gated_back = gated_back.reshape(rows, shards, v_cols).transpose(1, 0, 2).reshape(shards, units, part, v_cols)
     gated_back = lax.all_to_all(gated_back, "seq", split_axis=0, concat_axis=0, tiled=True)
 
+    gated_back, dense_grad, output_grad = lax.optimization_barrier((gated_back, dense_grad, output_grad))
+    dense_sum = lax.psum_scatter(dense_grad, BOTH, scatter_dimension=0, tiled=True)
+    seq_order = [("seq", bit) for bit in reversed(bits_of(shards))]
+    group_order = [("fsdp", bit) for bit in reversed(bits_of(groups))]
+    output_sum = reduce_halves(output_grad.reshape(shards, groups, own, output_grad.shape[1]), BOTH, (shards, groups), seq_order + group_order)
+
     dpre, dtaps, dsmall, dgain = mixer_backward(pre, gated_back, saved, taps, small, gain, heads)
     dpre = dpre.reshape(units * length, dpre.shape[2])
-    partial = back_through(dpre, w_mixer).astype(BF).reshape(units, length, width)
-    normed_back = lax.psum_scatter(partial, "seq", scatter_dimension=1, tiled=True).reshape(rows, width).astype(F32)
+    partial = back_through(dpre, w_mixer).astype(BF).reshape(units, shards, part, width)
+    normed_back = reduce_halves(partial.transpose(1, 0, 2, 3), ("seq",), (shards,), seq_order).reshape(rows, width)
     dw = outer_sum(normed, dpre)
     main = dw.shape[1] - lanes
     norm_gain_part = jnp.sum(dw * jnp.concatenate([w_mixer[:, :main], w_mixer[:, main:main + at], jnp.zeros((width, lanes - at), BF)], 1).astype(F32), 1) / norm_row
@@ -477,8 +627,11 @@
     filter_part = jnp.concatenate([grad_columns(dtaps[:taps_n, :qk_cols]), grad_columns(dtaps[:taps_n, qk_cols:2 * qk_cols]), grad_columns(dtaps[:taps_n, 2 * qk_cols:])], 1)
     filter_part = lax.dynamic_update_slice_in_dim(jnp.zeros((width, filter_part.shape[1]), F32), filter_part, shard_pos * rows_of, 0)
     dw = jnp.concatenate([dw[:, :main + at], norm_gain_part[:, None], ffn_gain_grad[:, None], filter_part, jnp.zeros((width, spare), F32)], 1)
-    dw = dw.astype(BF).reshape(shards, rows_of, dw.shape[1])
-    dw = lax.psum_scatter(dw, "fsdp", scatter_dimension=1, tiled=True)
+    dw = dw.astype(BF).reshape(shards, groups, own, dw.shape[1])
+    half = shards // 2
+    turned = group_order[1:2] + group_order[:1] + group_order[2:]
+    dw = jnp.concatenate([reduce_halves(dw[:half].transpose(1, 0, 2, 3), ("fsdp",), (groups,), group_order),
+                          reduce_halves(dw[half:].transpose(1, 0, 2, 3), ("fsdp",), (groups,), turned)]).astype(BF)
     dw = lax.all_to_all(dw, "seq", split_axis=0, concat_axis=0, tiled=True).astype(F32)
 
     def columns(start, stop):
@@ -500,17 +653,22 @@
     def placed(values):
         return lax.dynamic_update_slice_in_dim(jnp.zeros(decay_log.shape, F32), values, shard_pos * heads, 0)
 
-    decay_log_grad, decay_bias_grad, head_gain_grad = lax.psum((placed(dsmall[0, :heads]), placed(dsmall[1, :heads]), dgain[0]), BOTH)
+    little = jnp.concatenate([placed(dsmall[0, :heads]), placed(dsmall[1, :heads]), dgain[0]])
+    devices = shards * groups
+    little = lax.all_to_all(jnp.broadcast_to(little[None], (devices, little.shape[0])), BOTH, split_axis=0, concat_axis=0, tiled=True)
+    little = jnp.sum(little, 0)
+    count = decay_log.shape[0]
+    decay_log_grad, decay_bias_grad, head_gain_grad = little[:count], little[count:2 * count], little[2 * count:]
 
     _, norm_back = jax.vjp(rms_scale, residual, norm_row)
     input_back, _ = norm_back(normed_back)
-    slot_grad = (attended_back + input_back).astype(BF).reshape(micro, per_group, part, width)
+    slot_grad = (attended_back + input_back).astype(BF).reshape(micro, 1, part, width)
     home = lax.all_to_all(slot_grad, "fsdp", split_axis=2, concat_axis=1, tiled=True)
     tokens_grad = jax.vmap(take_rows)(home, seq_slots).astype(F32)
-    ffn_sum = ffn_sum.astype(F32)
+    dense_sum = dense_sum.astype(F32)
     return (mixed, tokens_grad, gains[:, 0], query_grad, key_grad, value_grad, decay_grad, beta_grad, outgate_grad,
-            *filter_grads, decay_log_grad, decay_bias_grad, head_gain_grad, output_sum.astype(F32).T, gains[:, 1],
-            ffn_sum[0], ffn_sum[1], ffn_sum[2].T)
+            *filter_grads, decay_log_grad, decay_bias_grad, head_gain_grad, output_sum.T, gains[:, 1],
+            dense_sum[:, :hidden_n], dense_sum[:, hidden_n:2 * hidden_n], dense_sum[:, 2 * hidden_n:3 * hidden_n].T)
 
 
 def solution(mesh):

time: 1260 us -> 788 us (0.63)
  waiting for transfers between devices: 696 us -> 215 us
  blocking collectives: 147 us -> 0 us
  Pallas kernels: 148 us -> 244 us
  local copies, waits for them, and re-layouts: 43.4 us -> 65.8 us
  other arithmetic: 34.9 us -> 54.7 us
  starting transfers between devices: 19.2 us -> 38.7 us
    reduce_scatter x4 -> x1, waiting for transfers between devices: 515 us -> 0.01 us  [body(): lax.psum_scatter(dense_grad, BOTH, scatter_dimension=0, tiled=True)]
    ppermute x0 -> x13, waiting for transfers between devices: none -> 108 us  [reduce_halves(): lax.ppermute(away, name, [(i, i ^ bit) for i in range(sizes[names.index(n...]
    pallas_call x0 -> x1, Pallas kernels: none -> 96.7 us  [start_exchange(): pl.pallas_call(functools.partial(start_kernel, shards, groups, rows_y, mi...]
    all_gather x4 -> x1, waiting for transfers between devices: 94.9 us -> 0.01 us  [body(): w_dense = lax.all_gather(dense, BOTH, axis=0, tiled=True)]
    all_to_all x2 -> x0, blocking collectives: 79.9 us -> none  [the longest x1 68 us: body(): lax.all_to_all(ordered, 'fsdp', split_axis=1, concat_axis=2, tiled=True)]
    psum x1 -> x0, blocking collectives: 66.9 us -> none  [body(): lax.psum((placed(dsmall[0, :heads]), placed(dsmall[1, :heads]), dgain[0])...]
    all_to_all x1, waiting for transfers between devices: 0.01 us -> 45.4 us  [body(): lax.all_to_all(dw, 'seq', split_axis=0, concat_axis=0, tiled=True)]
    all_to_all x1, waiting for transfers between devices: 36.5 us -> 17.7 us  [body(): lax.all_to_all(gated_back, 'seq', split_axis=0, concat_axis=0, tiled=True)]
  transfers between devices with their start and end apart: 12 -> 20, of which waited for: 9 -> 9; matrix products, arithmetic and copies ran while one was open for 10% -> 20% of each run, Pallas kernels for 6% -> 19%
where the time goes in v2:
time: 788 us; the launch traced here: 778 us
  Pallas kernels  244 us (31%)
  waiting for transfers between devices  215 us (27%)
  matrix products  144 us (18%)
  local copies, waits for them, and re-layouts  65.8 us (8%)
  other arithmetic  54.7 us (7%)
  starting transfers between devices  38.7 us (5%)
  between operations  15.3 us (2%)
    ppermute x13, waiting for transfers between devices, reduce_halves(): lax.ppermute(away, name, [(i, i ^ bit) for i in range(sizes[names.index(n...  108 us
    pallas_call x1, Pallas kernels, start_exchange(): pl.pallas_call(functools.partial(start_kernel, shards, groups, rows_y, mi...  96.7 us
    pallas_call x1, Pallas kernels, mixer_backward(): pl.pallas_call(functools.partial(backward_kernel, heads, micro), grid=(co...  77 us
    pallas_call x1, Pallas kernels, mixer_forward(): pl.pallas_call(functools.partial(forward_kernel, heads, micro), grid=(cou...  70.8 us
    dot_general x5, matrix products, product(): return jnp.dot(left, right, preferred_element_type=F32)  50.5 us
    dot_general x5, matrix products, back_through(): lax.dot_general(left, right, (((1,), (1,)), ((), ())), preferred_element_...  47.1 us
    dot_general x5, matrix products, outer_sum(): lax.dot_general(left, right, (((0,), (0,)), ((), ())), preferred_element_...  46.9 us
    all_to_all x1, waiting for transfers between devices, body(): lax.all_to_all(dw, 'seq', split_axis=0, concat_axis=0, tiled=True)  45.4 us
  transfers between devices with their start and end apart: 20, of which 9 were waited for; matrix products, arithmetic and copies ran while one was open for 20% of the time, Pallas kernels for 19%

profile of v2, /device:TPU:0, one launch (start us, length us, event | category | flops | bytes accessed | tf_op | source)
XLA Modules:
  0.0 778.1 jit_solution(11028072907725299779)
XLA Ops:
  16.7 96.7 %shard_map.365 = (bf16[3,4,8,32,1024]{4,3,2,1,0:T(8,128)(2,1)}, bf16[4,4,2,32,1664]{4,3,2,1,0:T(8,128)(2,1)}) custom-call(bf16[3,8,32,1024]{3,2,1,0:T(8,128)(2,1)} %broadcast_select_fusion.tok_ref, bf16[4,32,1664]{2,1,0:T(8,128)(2,1)} %bitcast.316), custom_call_target="tpu_custom_call" | custom-call | tf_op jit(solution)/shard_map/pallas_call | solution.py:442
  122.9 13.6 %convolution_convert_fusion = bf16[3072,1664]{1,0:T(8,128)(2,1)} fusion(bf16[3072,1024]{1,0:T(8,128)(2,1)S(1)} %bitcast.304, bf16[1024,1664]{1,0:T(8,128)(2,1)S(1)} %bitcast.340), kind=kOutput, calls=%fused_computation.9 | convolution fusion | flops 10474094592 | bytes 19922944 | tf_op jit(solution)/shard_map/dot_general | solution.py:472
  136.6 70.8 %shard_map.366 = (bf16[4,3,256,512]{3,2,1,0:T(8,128)(2,1)}, bf16[8,6,128,256]{3,2,1,0:T(8,128)(2,1)}, bf16[8,6,128,128]{3,2,1,0:T(8,128)(2,1)S(1)}, bf16[8,6,128...) custom-call(bf16[3,1024,1664]{2,1,0:T(8,128)(2,1)} %bitcast.279, bf16[3,1024,1664]{2,1,0:T(8,128)(2,1)} %bitcast.280, ...), custom_call_target="tpu_custom_call" | custom-call | tf_op jit(solution)/shard_map/pallas_call | solution.py:131
  207.3 4.9 all-to-all-start
  218.2 43.3 %all-to-all-done = bf16[4,3,256,512]{3,2,1,0:T(8,128)(2,1)} async-done(((bf16[4,3,256,512]{3,2,1,0:T(8,128)(2,1)}), bf16[4,3,256,512]{3,2,1,0:T(8,128)(2,1)}, u32[]{:S(2)}, u32[]{:S(2)}) %all-to-all-start) | async-done | bytes 3145760 | tf_op jit(solution)/shard_map/all_to_all | solution.py:580
  261.5 5.0 copy.383
  266.5 7.3 multiply_reduce_fusion.3
  278.0 6.9 fusion.8
  284.9 6.8 fusion.14
  291.7 17.4 %fusion.5 = (bf16[768,2816]{1,0:T(8,128)(2,1)}, bf16[768,2816]{1,0:T(8,128)(2,1)}, bf16[768,2816]{1,0:T(8,128)(2,1)}) fusion(f32[768,2816]{1,0:T(8,128)} %fusion.8, f32[768,2816]{1,0:T(8,128)} %fusion.14, bf16[768,1024]{1,0:T(8,128)(2,1)S(1)} %multiply_convert_fusion.2, bf16[1024,10496]{1,0:T(8,128)(2,1)} %all-gather.2.cloned.1.call-done), kind=kOutput, calls=%fused_computation.12 | convolution fusion | flops 4463788032 | bytes 37617664 | tf_op jit(solution)/shard_map/dot_general | solution.py:472
  309.1 9.4 %convolution_convert_fusion.2 = bf16[1024,2816]{1,0:T(8,128)(2,1)} fusion(bf16[768,1024]{1,0:T(8,128)(2,1)S(1)} %multiply_convert_fusion.2, bf16[768,2816]{1,0:T(8,128)(2,1)} %get-tuple-element.63), kind=kOutput, calls=%fused_computation.22 | convolution fusion | flops 4432068608 | bytes 11665408 | tf_op jit(solution)/shard_map/dot_general | solution.py:476
  318.5 6.6 convolution_convert_fusion.3
  325.1 6.7 fusion.12
  331.8 7.5 multiply_reduce_fusion.1
  341.2 5.1 convolution_convert_fusion.5
  346.3 5.8 fusion.25
  359.0 7.4 convolution_convert_fusion.1
  366.5 11.6 %pad_maximum_fusion = bf16[1024,8448]{1,0:T(8,128)(2,1)} fusion(bf16[1024,2816]{1,0:T(8,128)(2,1)S(1)} %convolution_convert_fusion.1, bf16[1024,2816]{1,0:T(8,128)(2,1)} %convolution_convert_fusion.2, bf16[1024,2816]{1,0:T(8,128)(2,1)} %convolution_convert_fusion.3), kind=kLoop, calls=%fused_computation.2 | loop fusion | flops 51904512 | bytes 34603008 | tf_op jit(solution)/shard_map/concatenate | solution.py:603
  378.1 17.7 %all-to-all-done.1.dgated_ref = bf16[4,3,256,512]{3,2,1,0:T(8,128)(2,1)} async-done(((bf16[4,3,256,512]{3,2,1,0:T(8,128)(2,1)}), bf16[4,3,256,512]{3,2,1,0:T(8,128)(2,1)}, u32[]{:S(2)}, u32[]{:S(2)}) %all-to-all-start.1) | async-done | bytes 3145760 | tf_op jit(solution)/shard_map/all_to_all | solution.py:606
  396.4 11.2 %fusion.39 = f32[768,1024]{1,0:T(8,128)} fusion(f32[768,1024]{1,0:T(8,128)} %copy-done.5, bf16[768,2816]{1,0:T(8,128)(2,1)} %get-tuple-element.64, bf16[1024,10496]{1,0:T(8,128)(2,1)} %all-gather.2.cloned.1.call-done), kind=kOutput, calls=%fused_computation.74 | convolution fusion | flops 4429971456 | bytes 16384000 | tf_op jit(solution)/shard_map/dot_general | solution.py:480
  407.6 77.0 %shard_map.367 = (bf16[3,1024,1664]{2,1,0:T(8,128)(2,1)}, f32[8,1024]{1,0:T(8,128)S(1)}, f32[8,128]{1,0:T(8,128)S(1)}, f32[8,256]{1,0:T(8,128)S(1)}) custom-call(bf16[3,1024,1664]{2,1,0:T(8,128)(2,1)} %bitcast.283, bf16[3,1024,1664]{2,1,0:T(8,128)(2,1)} %bitcast.284, bf16[3,1024,1664]{2,1,0:T(8,128)(2,1)} %bitcast.285, bf16[3,1024,1664]{2,1,0:T(8,128)(2,1)} %bitcast.286, ...), custom_call_target="tpu_custom_call" | custom-call | tf_op jit(solution)/shard_map/pallas_call | solution.py:302
  484.6 14.4 %convolution_convert_fusion.4 = bf16[3072,1024]{1,0:T(8,128)(2,1)S(1)} fusion(bf16[3072,1664]{1,0:T(8,128)(2,1)} %bitcast.356, bf16[1024,1664]{1,0:T(8,128)(2,1)S(1)} %bitcast.341), kind=kOutput, calls=%fused_computation.24 | convolution fusion | flops 10472128512 | bytes 19922944 | tf_op jit(solution)/shard_map/dot_general | solution.py:480
  504.8 18.4 %multiply_reduce_fusion = (f32[1024]{0:T(1024)S(1)}, bf16[1024,1664]{1,0:T(8,128)(2,1)}) fusion(pred[1664]{0:T(1024)(128)(4,1)S(1)} %copy-done.36, bf16[4,4,2,32,1664]{4,3,2,1,0:T(8,128)(2,1)S(1)} %copy-done.30, bf16[3,1024,1024]{2,1,0:T(8,128)(2,1)} %copy-done.10, bf16[3,1024,1664]{2,1,0:T(8,128)(2,1)} %get-tuple-element.47), kind=kOutput, calls=%fused_computation.18 | convolution fusion | flops 10477501440 | bytes 23336576 | tf_op jit(solution)/shard_map/dot_general | solution.py:476
  524.2 6.6 concatenate.40
  544.5 32.6 %collective-permute-done.5 = bf16[2,2,2,32,1664]{4,3,2,0,1:T(8,128)(2,1)} collective-permute-done((bf16[2,2,2,32,1664]{4,3,2,0,1:T(8,128)(2,1)S(1)}, bf16[2,2,2,32,1664]{4,3,2,0,1:T(8,128)(2,1)}, u32[]{:S(2)}, u32[]{:S(2)}) %collective-permute-start.5) | collective-permute-done | bytes 852000 | tf_op jit(solution)/shard_map/ppermute | solution.py:502
  581.7 8.5 %collective-permute-done.6 = bf16[2,2,32,1664]{3,2,1,0:T(8,128)(2,1)S(1)} collective-permute-done((bf16[2,2,32,1664]{3,2,1,0:T(8,128)(2,1)S(1)}, bf16[2,2,32,1664]{3,2,1,0:T(8,128)(2,1)S(1)}, u32[]{:S(2)}, u32[]{:S(2)}) %collective-permute-start.6) | collective-permute-done | bytes 426016 | tf_op jit(solution)/shard_map/ppermute | solution.py:502
  594.5 23.7 %collective-permute-done.7 = bf16[2,32,1664]{2,1,0:T(8,128)(2,1)S(1)} collective-permute-done((bf16[2,32,1664]{2,1,0:T(8,128)(2,1)S(1)}, bf16[2,32,1664]{2,1,0:T(8,128)(2,1)S(1)}, u32[]{:S(2)}, u32[]{:S(2)}) %collective-permute-start.7) | collective-permute-done | bytes 213024 | tf_op jit(solution)/shard_map/ppermute | solution.py:502
  618.2 6.4 collective-permute-done.4
  643.6 45.4 %all-to-all-done.3 = bf16[4,32,1664]{2,1,0:T(8,128)(2,1)S(1)} async-done(((bf16[4,32,1664]{2,1,0:T(8,128)(2,1)}), bf16[4,32,1664]{2,1,0:T(8,128)(2,1)S(1)}, u32[]{:S(2)}, u32[]{:S(2)}) %all-to-all-start.3) | async-done | bytes 426016 | tf_op jit(solution)/shard_map/all_to_all | solution.py:635
  693.0 4.9 fusion.33
  712.5 35.0 %collective-permute-done.11 = bf16[2,32,2048]{2,1,0:T(8,128)(2,1)S(1)} collective-permute-done((bf16[2,32,2048]{2,1,0:T(8,128)(2,1)S(1)}, bf16[2,32,2048]{2,1,0:T(8,128)(2,1)S(1)}, u32[]{:S(2)}, u32[]{:S(2)}) %collective-permute-start.11) | collective-permute-done | bytes 262176 | tf_op jit(solution)/shard_map/ppermute | solution.py:502
  747.6 5.0 collective-permute-start.12
  (264 shorter events, 123.3 us)
Async XLA Ops:
  7.2 259.3 %all-gather.2.cloned.1.call-start = ((), (), s32[]{:S(2)}) async-start(), calls=%async_computation.6 | async-start | bytes 22167552 | tf_op jit(solution)/shard_map/all_gather | solution.py:572
  13.5 99.8 %copy-start.18 = (bf16[2816,32]{0,1:T(8,128)(2,1)S(1)}, bf16[2816,32]{0,1:T(8,128)(2,1)}, u32[]{:S(2)}) copy-start(bf16[2816,32]{0,1:T(8,128)(2,1)} %param.45) | copy-start | bytes 540676
  13.5 99.8 %copy-start.19 = (bf16[32,2816]{1,0:T(8,128)(2,1)S(1)}, bf16[32,2816]{1,0:T(8,128)(2,1)}, u32[]{:S(2)}) copy-start(bf16[32,2816]{1,0:T(8,128)(2,1)} %param.44) | copy-start | bytes 540676
  13.6 99.8 %copy-start.20 = (bf16[32,2816]{1,0:T(8,128)(2,1)S(1)}, bf16[32,2816]{1,0:T(8,128)(2,1)}, u32[]{:S(2)}) copy-start(bf16[32,2816]{1,0:T(8,128)(2,1)} %param.43) | copy-start | bytes 540676
  13.6 99.8 %copy-start.23 = (bf16[2048,32]{0,1:T(8,128)(2,1)S(1)}, bf16[2048,32]{0,1:T(8,128)(2,1)}, u32[]{:S(2)}) copy-start(bf16[2048,32]{0,1:T(8,128)(2,1)} %param.41) | copy-start | bytes 393220
  15.8 100.5 %copy-start.32 = (f32[8]{0:T(128)S(1)}, f32[8]{0:T(128)}, u32[]{:S(2)}) copy-start(f32[8]{0:T(128)} %param.39) | copy-start | bytes 100
  15.8 100.5 %copy-start.33 = (f32[8]{0:T(128)S(1)}, f32[8]{0:T(128)}, u32[]{:S(2)}) copy-start(f32[8]{0:T(128)} %param.38) | copy-start | bytes 100
  207.3 54.1 %all-to-all-start = ((bf16[4,3,256,512]{3,2,1,0:T(8,128)(2,1)}), bf16[4,3,256,512]{3,2,1,0:T(8,128)(2,1)}, u32[]{:S(2)}, u32[]{:S(2)}) async-start(bf16[4,3,256,512]{3,2,1,0:T(8,128)(2,1)} %get-tuple-element.40), calls=%async_computation | async-start | bytes 6291456 | tf_op jit(solution)/shard_map/all_to_all | solution.py:580
  273.8 65.5 %copy-start.5 = (f32[768,1024]{1,0:T(8,128)}, f32[768,1024]{1,0:T(8,128)S(1)}, u32[]{:S(2)}) copy-start(f32[768,1024]{1,0:T(8,128)S(1)} %get-tuple-element.91) | copy-start | bytes 9437188
  354.2 41.6 %all-to-all-start.1 = ((bf16[4,3,256,512]{3,2,1,0:T(8,128)(2,1)}), bf16[4,3,256,512]{3,2,1,0:T(8,128)(2,1)}, u32[]{:S(2)}, u32[]{:S(2)}) async-start(bf16[4,3,256,512]{3,2,1,0:T(8,128)(2,1)} %bitcast.297), calls=%async_computation.1 | async-start | bytes 6291456 | tf_op jit(solution)/shard_map/all_to_all | solution.py:606
  358.8 408.4 %reduce-scatter.2.cloned.1.call-start = ((), (), s32[]{:S(2)}) async-start(), calls=%async_computation.7 | async-start | bytes 17842176 | tf_op jit(solution)/shard_map/reduce_scatter | solution.py:609
  407.6 77.0 %copy-start.29 = (bf16[4,4,2,32,1664]{4,3,2,1,0:T(8,128)(2,1)S(1)}, bf16[4,4,2,32,1664]{4,3,2,1,0:T(8,128)(2,1)}, u32[]{:S(2)}) copy-start(bf16[4,4,2,32,1664]{4,3,2,1,0:T(8,128)(2,1)} %get-tuple-element.39) | copy-start | bytes 10223620
  503.6 123.8 %collective-permute-start = (bf16[2,3,256,1024]{3,2,1,0:T(8,128)(2,1)}, bf16[2,3,256,1024]{3,2,1,0:T(8,128)(2,1)}, u32[]{:S(2)}, u32[]{:S(2)}) collective-permute-start(bf16[2,3,256,1024]{3,2,1,0:T(8,128)(2,1)} %dynamic-slice_bitcast_fusion), channel_id=1, source_target_pairs={{0,8},{8,0},{16,24},{24,16},{1,9},{9,1},{17,25},{25,17},{2,10},{10... | collective-permute-start | bytes 9437192 | tf_op jit(solution)/shard_map/ppermute | solution.py:502
  533.3 43.9 %collective-permute-start.5 = (bf16[2,2,2,32,1664]{4,3,2,0,1:T(8,128)(2,1)S(1)}, bf16[2,2,2,32,1664]{4,3,2,0,1:T(8,128)(2,1)}, u32[]{:S(2)}, u32[]{:S(2)}) collective-permute-start(bf16[2,2,2,32,1664]{4,3,2,0,1:T(8,128)(2,1)S(1)} %copy_bitcast_fusion.5), channel_id=1, source_target_pairs={{0,2},{1,3},{2,0},{3,1},{4,6},{5,7},{6,4},{7,5},{8,10},{9,11},{10,... | collective-permute-start | bytes 2555912 | tf_op jit(solution)/shard_map/ppermute | solution.py:502
  535.9 44.3 %collective-permute-start.2 = (bf16[2,2,2,32,1664]{4,3,2,1,0:T(8,128)(2,1)}, bf16[2,2,2,32,1664]{4,3,2,1,0:T(8,128)(2,1)}, u32[]{:S(2)}, u32[]{:S(2)}) collective-permute-start(bf16[2,2,2,32,1664]{4,3,2,1,0:T(8,128)(2,1)} %dynamic-slice_bitcast_fusion.3), channel_id=1, source_target_pairs={{0,1},{1,0},{2,3},{3,2},{4,5},{5,4},{6,7},{7,6},{8,9},{9,8},{10,11... | collective-permute-start | bytes 2555912 | tf_op jit(solution)/shard_map/ppermute | solution.py:502
  538.1 97.0 %all-to-all-start.4 = ((f32[32,1,272]{2,1,0:T(1,128)}), f32[32,1,272]{2,1,0:T(1,128)S(1)}, u32[]{:S(2)}, u32[]{:S(2)}) async-start(f32[32,1,272]{2,1,0:T(1,128)} %broadcast_in_dim.98), calls=%async_computation.4 | async-start | bytes 98304 | tf_op jit(solution)/shard_map/all_to_all | solution.py:658
  544.0 36.2 %copy-start.9 = (bf16[2,8,32,1664]{3,2,0,1:T(8,128)(2,1)S(1)}, bf16[2,8,32,1664]{3,2,0,1:T(8,128)(2,1)}, u32[]{:S(2)}) copy-start(bf16[2,8,32,1664]{3,2,0,1:T(8,128)(2,1)} %copy-done.8) | copy-start | bytes 5111812
  544.1 81.4 %collective-permute-start.8 = (bf16[2,2,2,2,32,2048]{5,4,1,2,3,0:T(8,128)(2,1)S(1)}, bf16[2,2,2,2,32,2048]{5,4,1,2,3,0:T(8,128)(2,1)S(1)}, u32[]{:S(2)}, u32[]{:S(2)}) collective-permute-start(bf16[2,2,2,2,32,2048]{5,4,1,2,3,0:T(8,128)(2,1)S(1)} %bitcast.315), channel_id=1, source_target_pairs={{0,8},{8,0},{16,24},{24,16},{1,9},{9,1},{17,25},{25,17},{2,10},{10... | collective-permute-start | bytes 6291464 | tf_op jit(solution)/shard_map/ppermute | solution.py:502
  578.6 11.5 %collective-permute-start.6 = (bf16[2,2,32,1664]{3,2,1,0:T(8,128)(2,1)S(1)}, bf16[2,2,32,1664]{3,2,1,0:T(8,128)(2,1)S(1)}, u32[]{:S(2)}, u32[]{:S(2)}) collective-permute-start(bf16[2,2,32,1664]{3,2,1,0:T(8,128)(2,1)S(1)} %dynamic-slice_bitcast_fusion.5), channel_id=1, source_target_pairs={{0,1},{1,0},{2,3},{3,2},{4,5},{5,4},{6,7},{7,6},{8,9},{9,8},{10,11... | collective-permute-start | bytes 1277960 | tf_op jit(solution)/shard_map/ppermute | solution.py:502
  581.6 12.6 %collective-permute-start.3 = (bf16[2,2,32,1664]{3,2,1,0:T(8,128)(2,1)S(1)}, bf16[2,2,32,1664]{3,2,1,0:T(8,128)(2,1)S(1)}, u32[]{:S(2)}, u32[]{:S(2)}) collective-permute-start(bf16[2,2,32,1664]{3,2,1,0:T(8,128)(2,1)S(1)} %dynamic-slice_bitcast_fusion.6), channel_id=1, source_target_pairs={{0,2},{1,3},{2,0},{3,1},{4,6},{5,7},{6,4},{7,5},{8,10},{9,11},{10,... | collective-permute-start | bytes 1277960 | tf_op jit(solution)/shard_map/ppermute | solution.py:502
  590.3 27.9 %collective-permute-start.7 = (bf16[2,32,1664]{2,1,0:T(8,128)(2,1)S(1)}, bf16[2,32,1664]{2,1,0:T(8,128)(2,1)S(1)}, u32[]{:S(2)}, u32[]{:S(2)}) collective-permute-start(bf16[2,32,1664]{2,1,0:T(8,128)(2,1)S(1)} %dynamic-slice_bitcast_fusion.9), channel_id=1, source_target_pairs={{0,4},{1,5},{2,6},{3,7},{4,0},{5,1},{6,2},{7,3},{8,12},{9,13},{10,... | collective-permute-start | bytes 638984 | tf_op jit(solution)/shard_map/ppermute | solution.py:502
  594.4 30.3 %collective-permute-start.4 = (bf16[2,32,1664]{2,1,0:T(8,128)(2,1)S(1)}, bf16[2,32,1664]{2,1,0:T(8,128)(2,1)S(1)}, u32[]{:S(2)}, u32[]{:S(2)}) collective-permute-start(bf16[2,32,1664]{2,1,0:T(8,128)(2,1)S(1)} %dynamic-slice_bitcast_fusion.10), channel_id=1, source_target_pairs={{0,4},{1,5},{2,6},{3,7},{4,0},{5,1},{6,2},{7,3},{8,12},{9,13},{10,... | collective-permute-start | bytes 638984 | tf_op jit(solution)/shard_map/ppermute | solution.py:502
  626.4 63.4 %collective-permute-start.9 = (bf16[2,2,2,32,2048]{4,3,0,1,2:T(8,128)(2,1)S(1)}, bf16[2,2,2,32,2048]{4,3,0,1,2:T(8,128)(2,1)}, u32[]{:S(2)}, u32[]{:S(2)}) collective-permute-start(bf16[2,2,2,32,2048]{4,3,0,1,2:T(8,128)(2,1)S(1)} %dynamic-slice_bitcast_fusion.2), channel_id=1, source_target_pairs={{0,16},{8,24},{16,0},{24,8},{1,17},{9,25},{17,1},{25,9},{2,18},{10... | collective-permute-start | bytes 3145736 | tf_op jit(solution)/shard_map/ppermute | solution.py:502
  634.1 58.9 %collective-permute-start.1 = (bf16[3,256,1024]{2,1,0:T(8,128)(2,1)}, bf16[3,256,1024]{2,1,0:T(8,128)(2,1)}, u32[]{:S(2)}, u32[]{:S(2)}) collective-permute-start(bf16[3,256,1024]{2,1,0:T(8,128)(2,1)} %dynamic-slice_bitcast_fusion.1), channel_id=1, source_target_pairs={{0,16},{8,24},{16,0},{24,8},{1,17},{9,25},{17,1},{25,9},{2,18},{10... | collective-permute-start | bytes 4718600 | tf_op jit(solution)/shard_map/ppermute | solution.py:502
  635.1 54.0 %all-to-all-start.3 = ((bf16[4,32,1664]{2,1,0:T(8,128)(2,1)}), bf16[4,32,1664]{2,1,0:T(8,128)(2,1)S(1)}, u32[]{:S(2)}, u32[]{:S(2)}) async-start(bf16[4,32,1664]{2,1,0:T(8,128)(2,1)} %pad_maximum_fusion.2), calls=%async_computation.3 | async-start | bytes 851968 | tf_op jit(solution)/shard_map/all_to_all | solution.py:635
  642.4 50.7 %copy-start.25 = (f32[1024,1]{0,1:T(1,128)S(1)}, f32[1024,1]{0,1:T(1,128)}, u32[]{:S(2)}) copy-start(f32[1024,1]{0,1:T(1,128)} %copy-done.24) | copy-start | bytes 12292
  692.6 16.6 %collective-permute-start.10 = (bf16[2,2,32,2048]{3,2,0,1:T(8,128)(2,1)}, bf16[2,2,32,2048]{3,2,0,1:T(8,128)(2,1)}, u32[]{:S(2)}, u32[]{:S(2)}) collective-permute-start(bf16[2,2,32,2048]{3,2,0,1:T(8,128)(2,1)} %dynamic-slice_bitcast_fusion.4), channel_id=1, source_target_pairs={{0,1},{1,0},{2,3},{3,2},{4,5},{5,4},{6,7},{7,6},{8,9},{9,8},{10,11... | collective-permute-start | bytes 1572872 | tf_op jit(solution)/shard_map/ppermute | solution.py:502
  704.8 57.7 %all-to-all-start.2 = ((bf16[3,1,256,1024]{3,0,1,2:T(4,128)(2,1)}), bf16[3,1,256,1024]{3,0,1,2:T(4,128)(2,1)}, u32[]{:S(2)}, u32[]{:S(2)}) async-start(bf16[3,1,256,1024]{3,0,1,2:T(4,128)(2,1)} %copy.388), calls=%async_computation.2 | async-start | bytes 4194304 | tf_op jit(solution)/shard_map/all_to_all | solution.py:666
  709.1 43.6 %copy-start.17 = (f32[4,4,8,256]{3,2,1,0:T(8,128)S(1)}, f32[4,4,8,256]{3,2,1,0:T(8,128)}, u32[]{:S(2)}) copy-start(f32[4,4,8,256]{3,2,1,0:T(8,128)} %get-tuple-element.75) | copy-start | bytes 393220
  709.1 44.3 %copy-start.16 = (f32[4,4,8,256]{3,2,1,0:T(8,128)S(1)}, f32[4,4,8,256]{3,2,1,0:T(8,128)}, u32[]{:S(2)}) copy-start(f32[4,4,8,256]{3,2,1,0:T(8,128)} %get-tuple-element.74) | copy-start | bytes 393220
  710.4 37.0 %collective-permute-start.11 = (bf16[2,32,2048]{2,1,0:T(8,128)(2,1)S(1)}, bf16[2,32,2048]{2,1,0:T(8,128)(2,1)S(1)}, u32[]{:S(2)}, u32[]{:S(2)}) collective-permute-start(bf16[2,32,2048]{2,1,0:T(8,128)(2,1)S(1)} %dynamic-slice_bitcast_fusion.7), channel_id=1, source_target_pairs={{0,2},{1,3},{2,0},{3,1},{4,6},{5,7},{6,4},{7,5},{8,10},{9,11},{10,... | collective-permute-start | bytes 786440 | tf_op jit(solution)/shard_map/ppermute | solution.py:502
  747.6 14.1 %collective-permute-start.12 = (bf16[32,2048]{1,0:T(8,128)(2,1)S(1)}, bf16[32,2048]{1,0:T(8,128)(2,1)S(1)}, u32[]{:S(2)}, u32[]{:S(2)}) collective-permute-start(bf16[32,2048]{1,0:T(8,128)(2,1)S(1)} %dynamic-slice_bitcast_fusion.11), channel_id=1, source_target_pairs={{0,4},{1,5},{2,6},{3,7},{4,0},{5,1},{6,2},{7,3},{8,12},{9,13},{10,... | collective-permute-start | bytes 393224 | tf_op jit(solution)/shard_map/ppermute | solution.py:502
  (30 other events, 213.1 us)
Sparse Core Ops, SparseCore 0:
  114.5 151.6 all-gather.1
  395.9 227.5 reduce-scatter.1

commit v3 on v2

--- a/solution.py
+++ b/solution.py
@@ -20,27 +20,35 @@
 def mm(a, b, ca=1, cb=0):
     return lax.dot_general(a.astype(BF), b.astype(BF), (((ca,), (cb,)), ((), ())), preferred_element_type=F32)
 
+def fine(a, b, ca=1, cb=0):
+    a_high, b_high = a.astype(BF), b.astype(BF)
+    a_low, b_low = a - a_high.astype(F32), b - b_high.astype(F32)
+    return mm(a_high, b_high, ca, cb) + (mm(a_high, b_low, ca, cb) + mm(a_low, b_high, ca, cb))
+
+
 def exact(a, b):
     return lax.dot_general(a, b, (((1,), (0,)), ((), ())), precision=HIGHEST, preferred_element_type=F32)
 
-def unit_inverse(low):
+def unit_inverses(lows):
     rows, cols = iota((C, C), 0), iota((C, C), 1)
-    diag = jnp.where(rows // 16 == cols // 16, low, 0.0)
-    packed = jnp.sum(diag.reshape(C // 16, 16, C), axis=0)
+    near = rows // 16 == cols // 16
+    packed = [jnp.sum(jnp.where(near, low, 0.0).reshape(C // 16, 16, C), axis=0) for low in lows]
     prow, pcol = iota((16, C), 0), iota((16, C), 1)
-    inv = jnp.where(prow == pcol % 16, 1.0, 0.0).astype(F32)
     base = (pcol // 16) * 16
+    invs = [jnp.where(prow == pcol % 16, 1.0, 0.0).astype(F32) for _ in lows]
     for j in range(15):
-        col = jnp.take_along_axis(packed, base + j, axis=1)
-        inv = inv - col * inv[j:j + 1, :]
-    full = jnp.broadcast_to(inv[None], (C // 16, 16, C)).reshape(C, C)
-    full = jnp.where(rows // 16 == cols // 16, full, 0.0)
+        columns = [jnp.take_along_axis(p, base + j, axis=1) for p in packed]
+        invs = [inv - column * inv[j:j + 1, :] for inv, column in zip(invs, columns)]
+    fulls = [jnp.where(near, jnp.broadcast_to(inv[None], (C // 16, 16, C)).reshape(C, C), 0.0) for inv in invs]
     size = 16
     while size < C:
-        off = jnp.where((rows // (2 * size) == cols // (2 * size)) & (rows // size == cols // size + 1), low, 0.0)
-        full = full - mm(mm(full, off), full)
+        below = (rows // (2 * size) == cols // (2 * size)) & (rows // size == cols // size + 1)
+        offs = [jnp.where(below, low, 0.0) for low in lows]
+        lefts = [mm(full, off) for full, off in zip(fulls, offs)]
+        fulls = [full - mm(left, full) for full, left in zip(fulls, lefts)]
         size *= 2
-    return full
+    return fulls
+
 
 def gates(pre, dlog, dbias):
     arg = pre + dbias
@@ -78,47 +86,49 @@
     rows, cols = iota((C, C), 0), iota((C, C), 1)
     lower = rows >= cols
     gain = gain_ref[0:1, :]
+    units = [(m, h, m * heads + h) for m in range(micro) for h in range(heads)]
+    acts, cums, cums_t, rates = [], [], [], []
     for m in range(micro):
         ext = ext_ref.at[m]
         load_ext(qkv_ref[m], halo_ref[m], ext, first)
         act = conv_taps(ext, taps, None)
-        act = act * sig(act)
+        acts.append(act * sig(act))
         pre = db_ref[m].astype(F32)
-        _, cum = gates(pre, small_ref[0:1, :], small_ref[1:2, :])
-        rate = sig(pre)
-        cum_t = jnp.transpose(cum)
-        for h in range(heads):
-            u = m * heads + h
-            q = act[:, h * KD:(h + 1) * KD]
-            k = act[:, (heads + h) * KD:(heads + h + 1) * KD]
-            v = act[:, 2 * heads * KD + h * VD:2 * heads * KD + (h + 1) * VD]
-            q = q * (lax.rsqrt(jnp.sum(q * q, -1, keepdims=True) + EPS) * KD ** -0.5)
-            k = k * lax.rsqrt(jnp.sum(k * k, -1, keepdims=True) + EPS)
-            beta = rate[:, heads + h:heads + h + 1]
-            gcol = cum[:, h:h + 1]
-            grow = cum_t[h:h + 1, :]
-            decay = jnp.where(lower, jnp.exp(jnp.where(lower, gcol - grow, 0.0)), 0.0)
-            grow_col = jnp.exp(gcol)
-            glast = cum[C - 1:C, h:h + 1]
-            dots = mm(jnp.concatenate([k, q], 0), k, 1, 1)
-            low = jnp.where(rows > cols, beta * decay * dots[:C], 0.0)
-            scores = decay * dots[C:]
-            inv = unit_inverse(low)
-            mem = mem_ref[u]
-            state_ref[0, u] = mem.astype(state_ref.dtype)
-            from_mem = mm(jnp.concatenate([grow_col * k, grow_col * q], 0), mem)
-            upd = mm(inv, beta * (v - from_mem[:C]))
-            out = from_mem[C:] + mm(scores, upd)
-            mem_ref[u] = jnp.exp(glast) * mem + mm(k * jnp.exp(glast - gcol), upd, 0, 0)
-            inv_ref[0, u] = inv.astype(inv_ref.dtype)
-            upd_ref[0, u] = upd.astype(upd_ref.dtype)
-            mix = out.astype(BF)
-            mix_ref[0, u] = mix
-            mix = mix.astype(F32)
-            og = og_ref[m, :, h * VD:(h + 1) * VD].astype(F32)
-            scale = lax.rsqrt(jnp.mean(mix * mix, -1, keepdims=True) + EPS)
-            gated = mix * scale * gain * (og * sig(og))
-            gated_ref[0, m, :, h * VD:(h + 1) * VD] = gated.astype(BF)
+        cums.append(gates(pre, small_ref[0:1, :], small_ref[1:2, :])[1])
+        rates.append(sig(pre))
+        cums_t.append(jnp.transpose(cums[-1]))
+    qs, ks, betas, decays = [], [], [], []
+    for m, h, u in units:
+        q = acts[m][:, h * KD:(h + 1) * KD]
+        k = acts[m][:, (heads + h) * KD:(heads + h + 1) * KD]
+        qs.append(q * (lax.rsqrt(jnp.sum(q * q, -1, keepdims=True) + EPS) * KD ** -0.5))
+        ks.append(k * lax.rsqrt(jnp.sum(k * k, -1, keepdims=True) + EPS))
+        betas.append(rates[m][:, heads + h:heads + h + 1])
+        decays.append(jnp.where(lower, jnp.exp(jnp.where(lower, cums[m][:, h:h + 1] - cums_t[m][h:h + 1, :], 0.0)), 0.0))
+    dots = [fine(jnp.concatenate([k, q], 0), k, 1, 1) for q, k in zip(qs, ks)]
+    lows = [jnp.where(rows > cols, beta * decay * dot[:C], 0.0) for beta, decay, dot in zip(betas, decays, dots)]
+    scores = [decay * dot[C:] for decay, dot in zip(decays, dots)]
+    invs = unit_inverses(lows)
+    growths = [jnp.exp(cums[m][:, h:h + 1]) for m, h, u in units]
+    mems = [mem_ref[u] for m, h, u in units]
+    from_mems = [mm(jnp.concatenate([growth * k, growth * q], 0), mem) for growth, q, k, mem in zip(growths, qs, ks, mems)]
+    rights = [betas[u] * (acts[m][:, 2 * heads * KD + h * VD:2 * heads * KD + (h + 1) * VD] - from_mems[u][:C]) for m, h, u in units]
+    upds = [fine(inv, right) for inv, right in zip(invs, rights)]
+    for m, h, u in units:
+        glast = cums[m][C - 1:C, h:h + 1]
+        mem_ref[u] = jnp.exp(glast) * mems[u] + mm(ks[u] * jnp.exp(glast - cums[m][:, h:h + 1]), upds[u], 0, 0)
+    outs = [from_mem[C:] + fine(score, upd) for from_mem, score, upd in zip(from_mems, scores, upds)]
+    for m, h, u in units:
+        state_ref[0, u] = mems[u].astype(state_ref.dtype)
+        inv_ref[0, u] = invs[u].astype(inv_ref.dtype)
+        upd_ref[0, u] = upds[u].astype(upd_ref.dtype)
+        mix = outs[u].astype(BF)
+        mix_ref[0, u] = mix
+        mix = mix.astype(F32)
+        og = og_ref[m, :, h * VD:(h + 1) * VD].astype(F32)
+        scale = lax.rsqrt(jnp.mean(mix * mix, -1, keepdims=True) + EPS)
+        gated = mix * scale * gain * (og * sig(og))
+        gated_ref[0, m, :, h * VD:(h + 1) * VD] = gated.astype(BF)
 
 
 def mixer_forward(pre, taps, small, gain, heads, shards):
@@ -161,6 +171,7 @@
         compiler_params=pltpu.CompilerParams(
             dimension_semantics=("arbitrary",), vmem_limit_bytes=50 * 1024 * 1024
         ),
+        cost_estimate=pl.CostEstimate(flops=units * count * 900_000_000, bytes_accessed=40_000_000, transcendentals=0),
     )(pre, pre, pre, pre, taps, small, gain)
 
 
@@ -183,94 +194,106 @@
     upper = jnp.where(rows <= cols, 1.0, 0.0).astype(F32)
     gain = gain_ref[0:1, :]
     qk_cols = heads * KD
+    strict = rows > cols
+    units = [(m, h, m * heads + h) for m in range(micro) for h in range(heads)]
+    acts, dgates, pres, logs, cums, cums_t, rates = [], [], [], [], [], [], []
     for m in range(micro):
         ext, dy = ext_ref.at[m], dy_ref.at[m]
         load_ext(qkv_ref[m], halo_ref[m], ext, step == count - 1)
         dy[pl.ds(C, 8), :] = jnp.where(step == 0, 0.0, dy[pl.ds(0, 8), :])
         conv = conv_taps(ext, taps, None)
         gate = sig(conv)
-        act = conv * gate
-        dgate = gate * (1.0 + conv * (1.0 - gate))
+        acts.append(conv * gate)
+        dgates.append(gate * (1.0 + conv * (1.0 - gate)))
         pre = db_ref[m].astype(F32)
         log_decay, cum = gates(pre, small_ref[0:1, :], small_ref[1:2, :])
-        rate = sig(pre)
-        cum_t = jnp.transpose(cum)
-        dcum = jnp.zeros((C, 128), F32)
-        drate = jnp.zeros((C, 128), F32)
-        for h in range(heads):
-            u = m * heads + h
-            q0 = act[:, h * KD:(h + 1) * KD]
-            k0 = act[:, qk_cols + h * KD:qk_cols + (h + 1) * KD]
-            v = act[:, 2 * qk_cols + h * VD:2 * qk_cols + (h + 1) * VD]
-            qr = lax.rsqrt(jnp.sum(q0 * q0, -1, keepdims=True) + EPS)
-            kr = lax.rsqrt(jnp.sum(k0 * k0, -1, keepdims=True) + EPS)
-            qn, k = q0 * qr, k0 * kr
-            q = qn * KD ** -0.5
-            beta = rate[:, heads + h:heads + h + 1]
-            gcol = cum[:, h:h + 1]
-            grow = cum_t[h:h + 1, :]
-            decay = jnp.where(lower, jnp.exp(jnp.where(lower, gcol - grow, 0.0)), 0.0)
-            growth = jnp.exp(gcol)
-            glast = cum[C - 1:C, h:h + 1]
-            tail = jnp.exp(glast - gcol)
-            dots = mm(jnp.concatenate([k, q], 0), k, 1, 1)
-            near = jnp.where(rows > cols, decay * dots[:C], 0.0)
-            scores = decay * dots[C:]
-            mix = mix_ref[0, u].astype(F32)
-            og = og_ref[m, :, h * VD:(h + 1) * VD].astype(F32)
-            dgated = dgated_ref[0, m, :, h * VD:(h + 1) * VD].astype(F32)
-            scale = lax.rsqrt(jnp.mean(mix * mix, -1, keepdims=True) + EPS)
-            mixn = mix * scale
-            osig = sig(og)
-            dog = dgated * mixn * gain * (osig * (1.0 + og * (1.0 - osig)))
-            dn = dgated * (og * osig)
-            dgain_ref[0:1, :] += jnp.sum(dn * mixn, 0, keepdims=True)
-            dn = dn * gain
-            dout = scale * (dn - mixn * jnp.mean(dn * mixn, -1, keepdims=True))
-            dout = dout.astype(BF)
-            upd, mem, inv, dmem = upd_ref[0, u], state_ref[0, u], inv_ref[0, u], dmem_ref[u]
-            dmem_low = dmem.astype(BF)
-            both = jnp.concatenate([upd, mem], 0)
-            one = mm(dout, both, 1, 1)
-            dscores = jnp.where(lower, one[:, :C], 0.0)
-            dq_in = one[:, C:]
-            ktail = k * tail
-            dupd = mm(scores, dout, 0, 0) + mm(ktail, dmem_low)
-            dres = mm(inv, dupd, 0, 0)
-            two = mm(dres, both, 1, 1)
-            dlow = jnp.where(rows > cols, -two[:, :C], 0.0)
-            dk_in = two[:, C:]
-            kin, qin = growth * k, growth * q
-            dk_scaled = -beta * dk_in
-            dmem_new = jnp.exp(glast) * dmem + mm(qin, dout, 0, 0) - mm(beta * kin, dres, 0, 0)
-            dk_tail = mm(upd, dmem_low, 1, 1)
-            pull = dscores * scores
-            pull_low = dlow * near
-            pulls = pull + beta * pull_low
-            in_parts = jnp.sum(dq_in * qin + dk_scaled * kin - dk_tail * ktail + pulls, -1, keepdims=True)
-            tail_sum = jnp.sum(jnp.sum(dk_tail * ktail, -1, keepdims=True), 0, keepdims=True)
-            mem_sum = jnp.sum(jnp.sum(dmem * mem.astype(F32), -1, keepdims=True), 0, keepdims=True)
-            dcum_col = in_parts - jnp.transpose(jnp.broadcast_to(jnp.sum(pulls, 0, keepdims=True), (C, C)))[:, 0:1]
-            last = iota((C, 1), 0) == C - 1
-            dcum_col = dcum_col + jnp.where(last, tail_sum + jnp.exp(glast) * mem_sum, 0.0)
-            dbeta = jnp.sum(dres * v, -1, keepdims=True) + jnp.sum(pull_low - dk_in * kin, -1, keepdims=True)
-            lane = iota((C, 128), 1)
-            dcum = jnp.where(lane == h, dcum_col, dcum)
-            drate = jnp.where(lane == heads + h, dbeta, drate)
-            dqk = dscores * decay
-            dkk = dlow * decay * beta
-            left = mm(jnp.concatenate([dqk, dkk], 0), k)
-            dq = left[:C] + growth * dq_in
-            dk = left[C:] + mm(dqk, q, 0, 0) + mm(dkk, k, 0, 0) + growth * dk_scaled + tail * dk_tail
-            dv = beta * dres
-            dmem_ref[u] = dmem_new
-            dq = dq * KD ** -0.5
-            dq = qr * (dq - qn * jnp.sum(dq * qn, -1, keepdims=True))
-            dk = kr * (dk - k * jnp.sum(dk * k, -1, keepdims=True))
-            for part, at, wide in ((dq, h * KD, KD), (dk, qk_cols + h * KD, KD), (dv, 2 * qk_cols + h * VD, VD)):
-                dy[pl.ds(0, C), at:at + wide] = part * dgate[:, at:at + wide]
-            at = 2 * qk_cols + heads * VD + h * VD
-            dpre_ref[m, :, at:at + VD] = dog.astype(BF)
+        pres.append(pre)
+        logs.append(log_decay)
+        cums.append(cum)
+        cums_t.append(jnp.transpose(cum))
+        rates.append(sig(pre))
+    douts = []
+    for m, h, u in units:
+        mix = mix_ref[0, u].astype(F32)
+        og = og_ref[m, :, h * VD:(h + 1) * VD].astype(F32)
+        dgated = dgated_ref[0, m, :, h * VD:(h + 1) * VD].astype(F32)
+        scale = lax.rsqrt(jnp.mean(mix * mix, -1, keepdims=True) + EPS)
+        mixn = mix * scale
+        osig = sig(og)
+        dog = dgated * mixn * gain * (osig * (1.0 + og * (1.0 - osig)))
+        dn = dgated * (og * osig)
+        dgain_ref[0:1, :] += jnp.sum(dn * mixn, 0, keepdims=True)
+        dn = dn * gain
+        douts.append((scale * (dn - mixn * jnp.mean(dn * mixn, -1, keepdims=True))).astype(BF))
+        at = 2 * qk_cols + heads * VD + h * VD
+        dpre_ref[m, :, at:at + VD] = dog.astype(BF)
+    qns, qrs, ks, krs, betas, gcols, decays = [], [], [], [], [], [], []
+    for m, h, u in units:
+        q0 = acts[m][:, h * KD:(h + 1) * KD]
+        k0 = acts[m][:, qk_cols + h * KD:qk_cols + (h + 1) * KD]
+        qrs.append(lax.rsqrt(jnp.sum(q0 * q0, -1, keepdims=True) + EPS))
+        krs.append(lax.rsqrt(jnp.sum(k0 * k0, -1, keepdims=True) + EPS))
+        qns.append(q0 * qrs[u])
+        ks.append(k0 * krs[u])
+        betas.append(rates[m][:, heads + h:heads + h + 1])
+        gcols.append(cums[m][:, h:h + 1])
+        decays.append(jnp.where(lower, jnp.exp(jnp.where(lower, gcols[u] - cums_t[m][h:h + 1, :], 0.0)), 0.0))
+    root = KD ** -0.5
+    dots = [fine(jnp.concatenate([k, qn * root], 0), k, 1, 1) for qn, k in zip(qns, ks)]
+    nears = [jnp.where(strict, decay * dot[:C], 0.0) for decay, dot in zip(decays, dots)]
+    scores = [decay * dot[C:] for decay, dot in zip(decays, dots)]
+    growths = [jnp.exp(gcol) for gcol in gcols]
+    glasts = [gcol[C - 1:C, :] for gcol in gcols]
+    tails = [jnp.exp(glast - gcol) for glast, gcol in zip(glasts, gcols)]
+    ktails = [k * tail for k, tail in zip(ks, tails)]
+    dmems = [dmem_ref[u] for m, h, u in units]
+    lows = [dmem.astype(BF) for dmem in dmems]
+    boths = [jnp.concatenate([upd_ref[0, u], state_ref[0, u]], 0) for m, h, u in units]
+    dupds = [mm(score, dout, 0, 0) + mm(ktail, low) for score, dout, ktail, low in zip(scores, douts, ktails, lows)]
+    dress = [mm(inv_ref[0, u], dupds[u], 0, 0) for m, h, u in units]
+    kins = [growth * k for growth, k in zip(growths, ks)]
+    qins = [growth * (qn * root) for growth, qn in zip(growths, qns)]
+    for m, h, u in units:
+        dmem_ref[u] = jnp.exp(glasts[u]) * dmems[u] + mm(qins[u], douts[u], 0, 0) - mm(betas[u] * kins[u], dress[u], 0, 0)
+    ones = [mm(dout, both, 1, 1) for dout, both in zip(douts, boths)]
+    twos = [mm(dres, both, 1, 1) for dres, both in zip(dress, boths)]
+    dk_tails = [mm(upd_ref[0, u], lows[u], 1, 1) for m, h, u in units]
+    dcums = [jnp.zeros((C, 128), F32) for m in range(micro)]
+    drates = [jnp.zeros((C, 128), F32) for m in range(micro)]
+    lane = iota((C, 128), 1)
+    last = iota((C, 1), 0) == C - 1
+    dqks, dkks = [], []
+    for m, h, u in units:
+        dscores = jnp.where(lower, ones[u][:, :C], 0.0)
+        dlow = jnp.where(strict, -twos[u][:, :C], 0.0)
+        pull_low = dlow * nears[u]
+        pulls = dscores * scores[u] + betas[u] * pull_low
+        dk_kin = twos[u][:, C:] * kins[u]
+        dk_ktail = dk_tails[u] * ktails[u]
+        in_parts = jnp.sum(ones[u][:, C:] * qins[u] - betas[u] * dk_kin - dk_ktail + pulls, -1, keepdims=True)
+        tail_sum = jnp.sum(jnp.sum(dk_ktail, -1, keepdims=True), 0, keepdims=True)
+        mem_sum = jnp.sum(jnp.sum(dmems[u] * state_ref[0, u].astype(F32), -1, keepdims=True), 0, keepdims=True)
+        across = jnp.transpose(jnp.broadcast_to(jnp.sum(pulls, 0, keepdims=True), (C, C)))[:, 0:1]
+        dcum_col = in_parts - across + jnp.where(last, tail_sum + jnp.exp(glasts[u]) * mem_sum, 0.0)
+        v = acts[m][:, 2 * qk_cols + h * VD:2 * qk_cols + (h + 1) * VD]
+        dbeta = jnp.sum(dress[u] * v, -1, keepdims=True) + jnp.sum(pull_low - dk_kin, -1, keepdims=True)
+        dcums[m] = jnp.where(lane == h, dcum_col, dcums[m])
+        drates[m] = jnp.where(lane == heads + h, dbeta, drates[m])
+        dqks.append(dscores * decays[u])
+        dkks.append(dlow * decays[u] * betas[u])
+    lefts = [mm(jnp.concatenate([dqk, dkk], 0), k) for dqk, dkk, k in zip(dqks, dkks, ks)]
+    rights = [mm(dqk, qn * root, 0, 0) + mm(dkk, k, 0, 0) for dqk, dkk, qn, k in zip(dqks, dkks, qns, ks)]
+    for m, h, u in units:
+        dy, dgate = dy_ref.at[m], dgates[m]
+        dq = (lefts[u][:C] + growths[u] * ones[u][:, C:]) * root
+        dk = lefts[u][C:] + rights[u] - (growths[u] * betas[u]) * twos[u][:, C:] + tails[u] * dk_tails[u]
+        dq = qrs[u] * (dq - qns[u] * jnp.sum(dq * qns[u], -1, keepdims=True))
+        dk = krs[u] * (dk - ks[u] * jnp.sum(dk * ks[u], -1, keepdims=True))
+        for part, at, wide in ((dq, h * KD, KD), (dk, qk_cols + h * KD, KD), (betas[u] * dress[u], 2 * qk_cols + h * VD, VD)):
+            dy[pl.ds(0, C), at:at + wide] = part * dgate[:, at:at + wide]
+    speed = -jnp.exp(small_ref[0:1, :])
+    for m in range(micro):
+        ext, dy = ext_ref.at[m], dy_ref.at[m]
         grad = dy[pl.ds(0, C), :]
         dx = dy[pl.ds(3, C), :] * taps[0:1, :]
         for i in range(1, 4):
@@ -278,12 +301,11 @@
         dpre_ref[m, :, 0:2 * qk_cols + heads * VD] = dx.astype(BF)
         for i in range(4):
             dtaps_ref[i:i + 1, :] += jnp.sum(grad * ext[pl.ds(5 + i, C), :], 0, keepdims=True)
-        dlog = exact(upper, dcum)
-        speed = -jnp.exp(small_ref[0:1, :])
-        ddecay = dlog * speed * sig(pre + small_ref[1:2, :])
-        dsmall_ref[0:1, :] += jnp.sum(dlog * log_decay, 0, keepdims=True)
+        dlog = exact(upper, dcums[m])
+        ddecay = dlog * speed * sig(pres[m] + small_ref[1:2, :])
+        dsmall_ref[0:1, :] += jnp.sum(dlog * logs[m], 0, keepdims=True)
         dsmall_ref[1:2, :] += jnp.sum(ddecay, 0, keepdims=True)
-        ddb = ddecay + drate * rate * (1.0 - rate)
+        ddb = ddecay + drates[m] * rates[m] * (1.0 - rates[m])
         at = 2 * qk_cols + 2 * heads * VD
         dpre_ref[m, :, at:at + 128] = ddb.astype(BF)
 
@@ -333,6 +355,7 @@
         compiler_params=pltpu.CompilerParams(
             dimension_semantics=("arbitrary",), vmem_limit_bytes=50 * 1024 * 1024
         ),
+        cost_estimate=pl.CostEstimate(flops=units * count * 1_600_000_000, bytes_accessed=60_000_000, transcendentals=0),
     )(pre, pre, pre, pre, dgated, mix, inv, upd, state, taps, small, gain)
 
 
@@ -460,6 +483,134 @@
     )(tok, pack)
 
 
+def finish_kernel(shards, deep, rows_y, dw_ref, wo_ref, little_ref, out_ref, wo_sum_ref, total_ref,
+                  y_buf, y_wo, z_buf, z_wo, mid, mid_wo, fin, little_buf, little_mid,
+                  send_sem, y_sem, z_sem, s_sem, little_sem):
+    s, f = lax.axis_index("seq"), lax.axis_index("fsdp")
+    z, y = f // rows_y, lax.rem(f, rows_y)
+    y_peers = [(s, z * rows_y + lax.rem(y + j, rows_y)) for j in range(1, rows_y)]
+    z_peers = [(s, lax.rem(z + k, deep) * rows_y + y) for k in range(1, deep)]
+    s_peers = [(jnp.bitwise_xor(s, d), f) for d in range(1, shards)]
+    barrier = pltpu.get_barrier_semaphore()
+    for peer in y_peers + z_peers + s_peers:
+        pl.semaphore_signal(barrier, inc=1, device_id=peer, device_id_type=MESH_ID)
+    pl.semaphore_wait(barrier, len(y_peers + z_peers + s_peers))
+
+    sent = []
+
+    def send(src, dst, sem, device):
+        copy = pltpu.make_async_remote_copy(src, dst, send_sem.at[len(sent)], sem, device_id=device, device_id_type=MESH_ID)
+        copy.start()
+        sent.append(copy)
+        return copy
+
+    blocks = [jnp.bitwise_xor(s, d) for d in range(shards)]
+    in_y = [[send(dw_ref.at[b, :, lax.rem(y + j, rows_y)], y_buf.at[j - 1, d], y_sem.at[j, d], y_peers[j - 1])
+             for j in range(1, rows_y)] for d, b in enumerate(blocks)]
+    in_y.append([send(wo_ref.at[:, lax.rem(y + j, rows_y)], y_wo.at[j - 1], y_sem.at[j, shards], y_peers[j - 1])
+                 for j in range(1, rows_y)])
+    little_copies = [send(little_ref, little_buf.at[j], little_sem.at[j], y_peers[j]) for j in range(rows_y - 1)]
+    in_z = []
+    for d, b in enumerate(blocks):
+        for copy in in_y[d]:
+            copy.wait_recv()
+        for part in range(deep):
+            acc = dw_ref[b, part, y].astype(F32)
+            for j in range(rows_y - 1):
+                acc = acc + y_buf[j, d, part].astype(F32)
+            mid[d, part] = acc.astype(BF)
+        in_z.append([send(mid.at[d, lax.rem(z + k, deep)], z_buf.at[k - 1, d], z_sem.at[k, d], z_peers[k - 1])
+                     for k in range(1, deep)])
+    for copy in in_y[shards]:
+        copy.wait_recv()
+    for part in range(deep):
+        acc = wo_ref[part, y].astype(F32)
+        for j in range(rows_y - 1):
+            acc = acc + y_wo[j, part].astype(F32)
+        mid_wo[part] = acc.astype(BF)
+    in_z.append([send(mid_wo.at[lax.rem(z + k, deep)], z_wo.at[k - 1], z_sem.at[k, shards], z_peers[k - 1])
+                 for k in range(1, deep)])
+    at = rows_y - 1
+    for copy in little_copies:
+        copy.wait_recv()
+    little = little_ref[...]
+    for j in range(rows_y - 1):
+        little = little + little_buf[j]
+    little_mid[0] = little
+    little_copies = [send(little_mid.at[0], little_buf.at[at + k], little_sem.at[at + k], z_peers[k]) for k in range(deep - 1)]
+    in_s = []
+    for d, b in enumerate(blocks):
+        for copy in in_z[d]:
+            copy.wait_recv()
+        acc = mid[d, z].astype(F32)
+        for k in range(deep - 1):
+            acc = acc + z_buf[k, d].astype(F32)
+        if d:
+            fin[d - 1] = acc.astype(BF)
+            in_s.append(send(fin.at[d - 1], out_ref.at[s], s_sem.at[d], s_peers[d - 1]))
+        else:
+            out_ref[s] = acc.astype(BF)
+    for copy in in_z[shards]:
+        copy.wait_recv()
+    acc = mid_wo[z].astype(F32)
+    for k in range(deep - 1):
+        acc = acc + z_wo[k].astype(F32)
+    wo_sum_ref[...] = acc
+    for copy in little_copies:
+        copy.wait_recv()
+    for k in range(deep - 1):
+        little = little + little_buf[at + k]
+    little_mid[1] = little
+    at += deep - 1
+    little_copies = [send(little_mid.at[1], little_buf.at[at + d], little_sem.at[at + d], s_peers[d]) for d in range(shards - 1)]
+    for copy in little_copies:
+        copy.wait_recv()
+    for d in range(shards - 1):
+        little = little + little_buf[at + d]
+    total_ref[...] = little
+    for copy in in_s:
+        copy.wait_recv()
+    for copy in sent:
+        copy.wait_send()
+
+
+def finish_sums(dw, wo, little, shards, groups):
+    rows_y = max(shards // 2, 1)
+    deep = groups // rows_y
+    own, cols = dw.shape[2:]
+    wide = wo.shape[2]
+    small_n = (rows_y - 1) + (deep - 1) + (shards - 1)
+    copies = (shards + 2) * (rows_y + deep - 2) + 2 * (shards - 1)
+    vmem = pl.BlockSpec(memory_space=pltpu.VMEM)
+    return pl.pallas_call(
+        functools.partial(finish_kernel, shards, deep, rows_y),
+        in_specs=[vmem] * 3,
+        out_specs=[vmem] * 3,
+        out_shape=[
+            jax.ShapeDtypeStruct((shards, own, cols), BF),
+            jax.ShapeDtypeStruct((own, wide), F32),
+            jax.ShapeDtypeStruct(little.shape, F32),
+        ],
+        scratch_shapes=[
+            pltpu.VMEM((max(rows_y - 1, 1), shards, deep, own, cols), BF),
+            pltpu.VMEM((max(rows_y - 1, 1), deep, own, wide), BF),
+            pltpu.VMEM((max(deep - 1, 1), shards, own, cols), BF),
+            pltpu.VMEM((max(deep - 1, 1), own, wide), BF),
+            pltpu.VMEM((shards, deep, own, cols), BF),
+            pltpu.VMEM((deep, own, wide), BF),
+            pltpu.VMEM((max(shards - 1, 1), own, cols), BF),
+            pltpu.VMEM((small_n,) + little.shape, F32),
+            pltpu.VMEM((2,) + little.shape, F32),
+            pltpu.SemaphoreType.DMA((copies,)),
+            pltpu.SemaphoreType.DMA((rows_y, shards + 1)),
+            pltpu.SemaphoreType.DMA((deep, shards + 1)),
+            pltpu.SemaphoreType.DMA((shards,)),
+            pltpu.SemaphoreType.DMA((small_n,)),
+        ],
+        compiler_params=pltpu.CompilerParams(collective_id=1, has_side_effects=True, vmem_limit_bytes=48 * 1024 * 1024),
+    )(dw.reshape(shards, deep, rows_y, own, cols), wo.reshape(deep, rows_y, own, wide), little)
+
+
 def rms_scale(values, gain):
     return values * lax.rsqrt(jnp.mean(values * values, -1, keepdims=True) + EPS) * gain
 
@@ -491,9 +642,10 @@
     return [1 << i for i in reversed(range(size.bit_length() - 1))]
 
 
-def reduce_halves(values, names, sizes, order):
-    left = [(name, bit) for name, size in zip(names, sizes) for bit in bits_of(size)]
-    values = values.reshape((2,) * len(left) + values.shape[len(names):])
+def reduce_halves(values, names, sizes, order, done=(), last=True):
+    left = [(name, bit) for name, size in zip(names, sizes) for bit in bits_of(size) if (name, bit) not in done]
+    if not done:
+        values = values.reshape((2,) * len(left) + values.shape[len(names):])
     for name, bit in order:
         at = left.index((name, bit))
         side = (lax.axis_index(name) // bit) % 2
@@ -502,7 +654,7 @@
         came = lax.ppermute(away, name, [(i, i ^ bit) for i in range(sizes[names.index(name)])])
         values = kept.astype(F32) + came.astype(F32)
         left.pop(at)
-        if left:
+        if left or not last:
             values = values.astype(BF)
     return values
 
@@ -567,12 +719,13 @@
                        lax.dynamic_slice_in_dim(decay_bias, shard_pos * heads, heads, 0)])
     small = jnp.pad(small, ((0, 6), (0, lanes - heads)))
     gain = jnp.broadcast_to(head_gain.astype(F32)[None], (8, head_gain.shape[0]))
-    dense = jnp.concatenate([w_gate, w_up, w_down.T, w_output.T], 1)
+    dense = jnp.concatenate([w_output.T, w_gate, w_up, w_down.T], 1)
     dense, everything = lax.optimization_barrier((dense, everything))
     w_dense = lax.all_gather(dense, BOTH, axis=0, tiled=True)
-    hidden_n = w_gate.shape[1]
-    w_gate_all, w_up_all = w_dense[:, :hidden_n], w_dense[:, hidden_n:2 * hidden_n]
-    w_down_t, w_out_t = w_dense[:, 2 * hidden_n:3 * hidden_n], w_dense[:, 3 * hidden_n:]
+    hidden_n, mixer_n = w_gate.shape[1], w_output.shape[0]
+    w_out_t = w_dense[:, :mixer_n]
+    w_gate_all, w_up_all = w_dense[:, mixer_n:mixer_n + hidden_n], w_dense[:, mixer_n + hidden_n:mixer_n + 2 * hidden_n]
+    w_down_t = w_dense[:, mixer_n + 2 * hidden_n:]
 
     normed = rms_scale(everything.astype(F32), norm_row).astype(BF).reshape(units * length, width)
     pre = product(normed, w_mixer).astype(BF).reshape(units, length, w_mixer.shape[1])
@@ -605,19 +758,26 @@
     gated_back = gated_back.reshape(rows, shards, v_cols).transpose(1, 0, 2).reshape(shards, units, part, v_cols)
     gated_back = lax.all_to_all(gated_back, "seq", split_axis=0, concat_axis=0, tiled=True)
 
-    gated_back, dense_grad, output_grad = lax.optimization_barrier((gated_back, dense_grad, output_grad))
-    dense_sum = lax.psum_scatter(dense_grad, BOTH, scatter_dimension=0, tiled=True)
     seq_order = [("seq", bit) for bit in reversed(bits_of(shards))]
     group_order = [("fsdp", bit) for bit in reversed(bits_of(groups))]
-    output_sum = reduce_halves(output_grad.reshape(shards, groups, own, output_grad.shape[1]), BOTH, (shards, groups), seq_order + group_order)
+    order = seq_order + group_order
+    output_grad = output_grad.reshape(shards, groups, own, output_grad.shape[1])
+    output_sum = reduce_halves(output_grad, BOTH, (shards, groups), order[:1], last=False)
+    gated_back, dense_grad, output_sum = lax.optimization_barrier((gated_back, dense_grad, output_sum))
+    dense_sum = lax.psum_scatter(dense_grad, BOTH, scatter_dimension=0, tiled=True)
+    output_sum = reduce_halves(output_sum, BOTH, (shards, groups), seq_order[1:], done=order[:1], last=False)
 
     dpre, dtaps, dsmall, dgain = mixer_backward(pre, gated_back, saved, taps, small, gain, heads)
+    dpre, output_sum = lax.optimization_barrier((dpre, output_sum))
+    normed_back = []
+    for m in range(units):
+        partial = back_through(dpre[m], w_mixer).astype(BF).reshape(shards, part, width)
+        normed_back.append(reduce_halves(partial, ("seq",), (shards,), seq_order))
     dpre = dpre.reshape(units * length, dpre.shape[2])
-    partial = back_through(dpre, w_mixer).astype(BF).reshape(units, shards, part, width)
-    normed_back = reduce_halves(partial.transpose(1, 0, 2, 3), ("seq",), (shards,), seq_order).reshape(rows, width)
-    dw = outer_sum(normed, dpre)
+    dw = outer_sum(normed, dpre).astype(BF)
     main = dw.shape[1] - lanes
-    norm_gain_part = jnp.sum(dw * jnp.concatenate([w_mixer[:, :main], w_mixer[:, main:main + at], jnp.zeros((width, lanes - at), BF)], 1).astype(F32), 1) / norm_row
+    used = main + at
+    norm_gain_part = jnp.sum(dw[:, :used].astype(F32) * w_mixer[:, :used].astype(F32), 1) / norm_row
 
     def grad_columns(grads):
         times = grads.shape[1] // rows_of
@@ -626,13 +786,18 @@
     qk_cols = heads * KD
     filter_part = jnp.concatenate([grad_columns(dtaps[:taps_n, :qk_cols]), grad_columns(dtaps[:taps_n, qk_cols:2 * qk_cols]), grad_columns(dtaps[:taps_n, 2 * qk_cols:])], 1)
     filter_part = lax.dynamic_update_slice_in_dim(jnp.zeros((width, filter_part.shape[1]), F32), filter_part, shard_pos * rows_of, 0)
-    dw = jnp.concatenate([dw[:, :main + at], norm_gain_part[:, None], ffn_gain_grad[:, None], filter_part, jnp.zeros((width, spare), F32)], 1)
-    dw = dw.astype(BF).reshape(shards, groups, own, dw.shape[1])
-    half = shards // 2
-    turned = group_order[1:2] + group_order[:1] + group_order[2:]
-    dw = jnp.concatenate([reduce_halves(dw[:half].transpose(1, 0, 2, 3), ("fsdp",), (groups,), group_order),
-                          reduce_halves(dw[half:].transpose(1, 0, 2, 3), ("fsdp",), (groups,), turned)]).astype(BF)
-    dw = lax.all_to_all(dw, "seq", split_axis=0, concat_axis=0, tiled=True).astype(F32)
+    side = jnp.concatenate([norm_gain_part[:, None], ffn_gain_grad[:, None], filter_part], 1).astype(BF)
+    dw = lax.dynamic_update_slice(dw, side, (0, used)).reshape(shards, groups, own, dw.shape[1])
+
+    def placed(values):
+        return lax.dynamic_update_slice_in_dim(jnp.zeros((lanes,), F32), values, shard_pos * heads, 0)
+
+    little = jnp.concatenate([placed(dsmall[0, :heads])[None], placed(dsmall[1, :heads])[None], dgain[0].reshape(-1, lanes)])
+    little = jnp.pad(little, ((0, 8 - little.shape[0]), (0, 0)))
+    dw, output_sum, little = finish_sums(dw, output_sum.reshape(groups, own, output_sum.shape[-1]), little, shards, groups)
+    dw = dw.astype(F32)
+    count = decay_log.shape[0]
+    decay_log_grad, decay_bias_grad, head_gain_grad = little[0, :count], little[1, :count], little[2:2 + dgain.shape[1] // lanes].reshape(-1)
 
     def columns(start, stop):
         return dw[:, :, start:stop].transpose(1, 0, 2).reshape(own, shards * (stop - start))
@@ -650,21 +815,14 @@
 
     filter_grads = (filter_grad(filter_own[:, :taps_n]), filter_grad(filter_own[:, taps_n:2 * taps_n]), filter_grad(filter_own[:, 2 * taps_n:]))
 
-    def placed(values):
-        return lax.dynamic_update_slice_in_dim(jnp.zeros(decay_log.shape, F32), values, shard_pos * heads, 0)
-
-    little = jnp.concatenate([placed(dsmall[0, :heads]), placed(dsmall[1, :heads]), dgain[0]])
-    devices = shards * groups
-    little = lax.all_to_all(jnp.broadcast_to(little[None], (devices, little.shape[0])), BOTH, split_axis=0, concat_axis=0, tiled=True)
-    little = jnp.sum(little, 0)
-    count = decay_log.shape[0]
-    decay_log_grad, decay_bias_grad, head_gain_grad = little[:count], little[count:2 * count], little[2 * count:]
-
-    _, norm_back = jax.vjp(rms_scale, residual, norm_row)
-    input_back, _ = norm_back(normed_back)
-    slot_grad = (attended_back + input_back).astype(BF).reshape(micro, 1, part, width)
-    home = lax.all_to_all(slot_grad, "fsdp", split_axis=2, concat_axis=1, tiled=True)
-    tokens_grad = jax.vmap(take_rows)(home, seq_slots).astype(F32)
+    home = []
+    for m in range(units):
+        _, norm_back = jax.vjp(rms_scale, residual[m * part:(m + 1) * part], norm_row)
+        input_back, _ = norm_back(normed_back[m])
+        slot_grad = (attended_back[m * part:(m + 1) * part] + input_back).astype(BF).reshape(groups, own, width)
+        back = lax.all_to_all(slot_grad, "fsdp", split_axis=0, concat_axis=0, tiled=True)
+        home.append(take_rows(back, seq_slots[m]))
+    tokens_grad = jnp.stack(home).astype(F32)
     dense_sum = dense_sum.astype(F32)
     return (mixed, tokens_grad, gains[:, 0], query_grad, key_grad, value_grad, decay_grad, beta_grad, outgate_grad,
             *filter_grads, decay_log_grad, decay_bias_grad, head_gain_grad, output_sum.T, gains[:, 1],

time: 788 us -> 732 us (0.929)
  waiting for transfers between devices: 215 us -> 148 us
  Pallas kernels: 244 us -> 281 us
  local copies, waits for them, and re-layouts: 65.8 us -> 51 us
  starting transfers between devices: 38.7 us -> 29.7 us
    ppermute x13 -> x8, waiting for transfers between devices: 108 us -> 27.9 us  [reduce_halves(): lax.ppermute(away, name, [(i, i ^ bit) for i in range(sizes[names.index(n...]
    pallas_call x0 -> x1, Pallas kernels: none -> 70.8 us  [finish_sums(): pl.pallas_call(functools.partial(finish_kernel, shards, deep, rows_y), in...]
    pallas_call x1, Pallas kernels: 70.8 us -> 40.5 us  [mixer_forward(): pl.pallas_call(functools.partial(forward_kernel, heads, micro), grid=(cou...]
    all_to_all x3, waiting for transfers between devices: 45.4 us -> 16.6 us  [body(): lax.all_to_all(slot_grad, 'fsdp', split_axis=0, concat_axis=0, tiled=True)]
    all_gather x1, waiting for transfers between devices: 0.01 us -> 27.8 us  [body(): w_dense = lax.all_gather(dense, BOTH, axis=0, tiled=True)]
    all_to_all x1, waiting for transfers between devices: 43.3 us -> 61.5 us  [body(): lax.all_to_all(gated, 'seq', split_axis=0, concat_axis=0, tiled=True)]
    ppermute x13 -> x8, starting transfers between devices: 17.9 us -> 5.45 us  [reduce_halves(): lax.ppermute(away, name, [(i, i ^ bit) for i in range(sizes[names.index(n...]
    dot_general x5 -> x7, matrix products: 47.1 us -> 47.3 us  [back_through(): lax.dot_general(left, right, (((1,), (1,)), ((), ())), preferred_element_...]
  transfers between devices with their start and end apart: 20 -> 15, of which waited for: 9 -> 7; matrix products, arithmetic and copies ran while one was open for 20% -> 20% of each run, Pallas kernels for 19% -> 25%
where the time goes in v3:
time: 732 us; the launch traced here: 723 us
  Pallas kernels  281 us (38%)
  waiting for transfers between devices  148 us (20%)
  matrix products  144 us (20%)
  other arithmetic  54.2 us (7%)
  local copies, waits for them, and re-layouts  51 us (7%)
  starting transfers between devices  29.7 us (4%)
  between operations  15.5 us (2%)
    pallas_call x1, Pallas kernels, start_exchange(): pl.pallas_call(functools.partial(start_kernel, shards, groups, rows_y, mi...  96.7 us
    pallas_call x1, Pallas kernels, mixer_backward(): pl.pallas_call(functools.partial(backward_kernel, heads, micro), grid=(co...  72.7 us
    pallas_call x1, Pallas kernels, finish_sums(): pl.pallas_call(functools.partial(finish_kernel, shards, deep, rows_y), in...  70.8 us
    all_to_all x1, waiting for transfers between devices, body(): lax.all_to_all(gated, 'seq', split_axis=0, concat_axis=0, tiled=True)  61.5 us
    dot_general x5, matrix products, product(): return jnp.dot(left, right, preferred_element_type=F32)  50.5 us
    dot_general x7, matrix products, back_through(): lax.dot_general(left, right, (((1,), (1,)), ((), ())), preferred_element_...  47.3 us
    dot_general x5, matrix products, outer_sum(): lax.dot_general(left, right, (((0,), (0,)), ((), ())), preferred_element_...  45.8 us
    pallas_call x1, Pallas kernels, mixer_forward(): pl.pallas_call(functools.partial(forward_kernel, heads, micro), grid=(cou...  40.5 us
  transfers between devices with their start and end apart: 15, of which 7 were waited for; matrix products, arithmetic and copies ran while one was open for 20% of the time, Pallas kernels for 25%

profile of v3, /device:TPU:0, one launch (start us, length us, event | category | flops | bytes accessed | tf_op | source)
XLA Modules:
  0.0 722.8 jit_solution(12376819777399515347)
XLA Ops:
  17.5 96.7 %shard_map.365 = (bf16[3,4,8,32,1024]{4,3,2,1,0:T(8,128)(2,1)}, bf16[4,4,2,32,1664]{4,3,2,1,0:T(8,128)(2,1)}) custom-call(bf16[3,8,32,1024]{3,2,1,0:T(8,128)(2,1)} %broadcast_select_fusion.tok_ref, bf16[4,32,1664]{2,1,0:T(8,128)(2,1)} %bitcast.319), custom_call_target="tpu_custom_call" | custom-call | tf_op jit(solution)/shard_map/pallas_call | solution.py:465
  123.6 13.6 %convolution_convert_fusion = bf16[3072,1664]{1,0:T(8,128)(2,1)} fusion(bf16[3072,1024]{1,0:T(8,128)(2,1)S(1)} %bitcast.293, bf16[1024,1664]{1,0:T(8,128)(2,1)S(1)} %bitcast.304), kind=kOutput, calls=%fused_computation.11 | convolution fusion | flops 10474094592 | bytes 19922944 | tf_op jit(solution)/shard_map/dot_general | solution.py:623
  137.2 40.5 %shard_map.366 = (bf16[4,3,256,512]{3,2,1,0:T(8,128)(2,1)}, bf16[8,6,128,256]{3,2,1,0:T(8,128)(2,1)}, bf16[8,6,128,128]{3,2,1,0:T(8,128)(2,1)S(1)}, bf16[8,6,128...) custom-call(bf16[3,1024,1664]{2,1,0:T(8,128)(2,1)} %bitcast.357, bf16[3,1024,1664]{2,1,0:T(8,128)(2,1)} %bitcast.358, ...), custom_call_target="tpu_custom_call" | custom-call | flops 43200000000 | bytes 40000000 | tf_op jit(solution)/shard_map/pallas_call | solution.py:141
  177.7 4.8 all-to-all-start
  188.0 61.5 %all-to-all-done = bf16[4,3,256,512]{3,2,1,0:T(8,128)(2,1)} async-done(((bf16[4,3,256,512]{3,2,1,0:T(8,128)(2,1)}), bf16[4,3,256,512]{3,2,1,0:T(8,128)(2,1)}, u32[]{:S(2)}, u32[]{:S(2)}) %all-to-all-start) | async-done | bytes 3145760 | tf_op jit(solution)/shard_map/all_to_all | solution.py:733
  249.5 4.6 copy.310
  254.1 27.8 %all-gather.2.cloned.1.call-done = bf16[1024,10496]{1,0:T(8,128)(2,1)} async-done(((bf16[32,10496]{1,0:T(8,128)(2,1)}), bf16[1024,10496]{1,0:T(8,128)(2,1)}) %all-gather.2.cloned.1.call-update) | async-done | bytes 21495824 | tf_op jit(solution)/shard_map/all_gather | solution.py:724
  281.9 7.7 %multiply_reduce_fusion.3 = (f32[768]{0:T(1024)S(1)}, f32[768,1024]{1,0:T(8,128)S(1)}) fusion(bf16[768,2048]{0,1:T(8,128)(2,1)} %bitcast.307, bf16[1024,10496]{1,0:T(8,128)(2,1)} %all-gather.2.cloned.1.call-done, f32[3,256,1024]{2,1,0:T(8,128)} %dynamic-slice_convert_fusion), kind=kOutput, calls=%fused_computation.62 | convolution fusion | flops 3223584000 | bytes 13634560 | tf_op jit(solution)/shard_map/dot_general | solution.py:631
  293.9 6.9 fusion.7
  300.8 6.8 fusion.13
  307.6 17.3 %fusion.5 = (bf16[768,2816]{1,0:T(8,128)(2,1)}, bf16[768,2816]{1,0:T(8,128)(2,1)}, bf16[768,2816]{1,0:T(8,128)(2,1)}) fusion(f32[768,2816]{1,0:T(8,128)} %fusion.7, f32[768,2816]{1,0:T(8,128)} %fusion.13, bf16[768,1024]{1,0:T(8,128)(2,1)S(1)} %multiply_convert_fusion.2, bf16[1024,10496]{1,0:T(8,128)(2,1)} %all-gather.2.cloned.1.call-done), kind=kOutput, calls=%fused_computation.14 | convolution fusion | flops 4463788032 | bytes 37617664 | tf_op jit(solution)/shard_map/dot_general | solution.py:623
  325.0 9.5 %convolution_convert_fusion.2 = bf16[1024,2816]{1,0:T(8,128)(2,1)} fusion(bf16[768,1024]{1,0:T(8,128)(2,1)S(1)} %multiply_convert_fusion.2, bf16[768,2816]{1,0:T(8,128)(2,1)} %get-tuple-element.82), kind=kOutput, calls=%fused_computation.22 | convolution fusion | flops 4432068608 | bytes 11665408 | tf_op jit(solution)/shard_map/dot_general | solution.py:627
  334.5 6.6 convolution_convert_fusion.3
  341.1 6.7 fusion.11
  347.8 7.4 %multiply_reduce_fusion.1 = (bf16[1024]{0:T(1024)(128)(2,1)S(1)}, f32[768]{0:T(1024)S(1)}, f32[768,1024]{1,0:T(8,128)S(1)}) fusion(f32[768,1024]{1,0:T(8,128)S(1)} %get-tuple-element.118, f32[768]{0:T(1024)S(1)} %fusion.70, f32[1024]{0:T(1024)S(1)} %bitcast.339, f32[768,1024]{1,0:T(8,128)S(1)} %fusion.11, bf16[768,2816]{1,0:T(8,128)(2,1)S(1)} %copy-done.48, ...), kind=kOutput, calls=%fused_computation.59 | convolution fusion | flops 4434688000 | bytes 19542016 | tf_op jit(solution)/shard_map/dot_general | solution.py:631
  357.1 5.1 convolution_convert_fusion.4
  362.3 5.8 fusion.33
  370.1 4.7 all-to-all-start.1
  378.8 7.5 %convolution_convert_fusion.1 = bf16[1024,2816]{1,0:T(8,128)(2,1)S(1)} fusion(bf16[768,1024]{1,0:T(8,128)(2,1)S(1)} %copy-done.30, bf16[768,2816]{1,0:T(8,128)(2,1)} %get-tuple-element.83), kind=kOutput, calls=%fused_computation.21 | convolution fusion | flops 4432068608 | bytes 11665408 | tf_op jit(solution)/shard_map/dot_general | solution.py:627
  386.3 6.7 pad_maximum_fusion
  397.4 14.3 %all-to-all-done.1.dgated_ref = bf16[4,3,256,512]{3,2,1,0:T(8,128)(2,1)} async-done(((bf16[4,3,256,512]{3,2,1,0:T(8,128)(2,1)}), bf16[4,3,256,512]{3,2,1,0:T(8,128)(2,1)}, u32[]{:S(2)}, u32[]{:S(2)}) %all-to-all-start.1) | async-done | bytes 3145760 | tf_op jit(solution)/shard_map/all_to_all | solution.py:759
  413.7 9.5 %fusion.54 = f32[768,1024]{1,0:T(8,128)S(1)} fusion(f32[768,1024]{1,0:T(8,128)} %copy-done.15, bf16[768,2816]{1,0:T(8,128)(2,1)} %get-tuple-element.83, bf16[1024,10496]{1,0:T(8,128)(2,1)} %all-gather.2.cloned.1.call-done), kind=kOutput, calls=%fused_computation.76 | convolution fusion | flops 4429971456 | bytes 16384000 | tf_op jit(solution)/shard_map/dot_general | solution.py:631
  426.4 72.7 %shard_map.367 = (bf16[3,1024,1664]{2,1,0:T(8,128)(2,1)}, f32[8,1024]{1,0:T(8,128)S(1)}, f32[8,128]{1,0:T(8,128)S(1)}, f32[8,256]{1,0:T(8,128)S(1)}) custom-call(bf16[3,1024,1664]{2,1,0:T(8,128)(2,1)} %bitcast.361, bf16[3,1024,1664]{2,1,0:T(8,128)(2,1)} %bitcast.362, bf16[3,1024,1664]{2,1,0:T(8,128)(2,1)} %bitcast.363, bf16[3,1024,1664]{2,1,0:T(8,128)(2,1)} %bitcast.364, ...), custom_call_target="tpu_custom_call" | custom-call | flops 76800000000 | bytes 60000000 | tf_op jit(solution)/shard_map/pallas_call | solution.py:324
  502.8 7.2 fusion.42
  511.6 4.6 fusion.48
  532.5 17.1 %bitcast_convert_fusion = bf16[1024,1664]{1,0:T(8,128)(2,1)S(1)} fusion(bf16[3,1024,1024]{2,1,0:T(8,128)(2,1)} %copy-done.19, bf16[3,1024,1664]{2,1,0:T(8,128)(2,1)} %get-tuple-element.54), kind=kOutput, calls=%fused_computation.19 | convolution fusion | flops 10470686720 | bytes 19922944 | tf_op jit(solution)/shard_map/dot_general | solution.py:627
  549.6 9.2 %collective-permute-done.7 = bf16[256,1024]{1,0:T(8,128)(2,1)S(1)} collective-permute-done((bf16[256,1024]{1,0:T(8,128)(2,1)S(1)}, bf16[256,1024]{1,0:T(8,128)(2,1)S(1)}, u32[]{:S(2)}, u32[]{:S(2)}) %collective-permute-start.7) | collective-permute-done | bytes 524320 | tf_op jit(solution)/shard_map/ppermute | solution.py:654
  558.9 18.7 %collective-permute-done.5 = bf16[256,1024]{1,0:T(8,128)(2,1)S(1)} collective-permute-done((bf16[256,1024]{1,0:T(8,128)(2,1)S(1)}, bf16[256,1024]{1,0:T(8,128)(2,1)S(1)}, u32[]{:S(2)}, u32[]{:S(2)}) %collective-permute-start.5) | collective-permute-done | bytes 524320 | tf_op jit(solution)/shard_map/ppermute | solution.py:654
  580.2 6.8 all-to-all-start.4
  593.0 8.9 %all-to-all-done.4 = bf16[8,32,1024]{2,1,0:T(8,128)(2,1)} async-done(((bf16[8,32,1024]{2,1,0:T(8,128)(2,1)}), bf16[8,32,1024]{2,1,0:T(8,128)(2,1)}, u32[]{:S(2)}, u32[]{:S(2)}) %all-to-all-start.4) | async-done | bytes 524320 | tf_op jit(solution)/shard_map/all_to_all | solution.py:823
  614.1 70.8 %shard_map.368 = (bf16[4,32,1664]{2,1,0:T(8,128)(2,1)S(1)}, f32[32,2048]{1,0:T(8,128)S(1)}, f32[8,128]{1,0:T(8,128)S(1)}) custom-call(bf16[4,4,2,32,1664]{4,3,2,1,0:T(8,128)(2,1)S(1)} %bitcast.286, bf16[4,2,32,2048]{3,2,1,0:T(8,128)(2,1)S(1)} %bitcast.287, f32[8,128]{1,0:T(8,128)S(1)} %select_maximum_fusion.2.little_ref), custom_call_target="tpu_custom_call" | custom-call | tf_op jit(solution)/shard_map/pallas_call | solution.py:585
  700.7 7.7 %all-to-all-done.2 = bf16[8,32,1024]{2,1,0:T(8,128)(2,1)S(1)} async-done(((bf16[8,32,1024]{2,1,0:T(8,128)(2,1)}), bf16[8,32,1024]{2,1,0:T(8,128)(2,1)S(1)}, u32[]{:S(2)}, u32[]{:S(2)}) %all-to-all-start.2) | async-done | bytes 524320 | tf_op jit(solution)/shard_map/all_to_all | solution.py:823
  (278 shorter events, 111.5 us)
Async XLA Ops:
  7.2 274.7 %all-gather.2.cloned.1.call-start = ((), (), s32[]{:S(2)}) async-start(), calls=%async_computation.6 | async-start | bytes 22167552 | tf_op jit(solution)/shard_map/all_gather | solution.py:724
  13.5 100.6 %copy-start.34 = (bf16[2816,32]{0,1:T(8,128)(2,1)S(1)}, bf16[2816,32]{0,1:T(8,128)(2,1)}, u32[]{:S(2)}) copy-start(bf16[2816,32]{0,1:T(8,128)(2,1)} %param.45) | copy-start | bytes 540676
  13.6 100.6 %copy-start.35 = (bf16[32,2816]{1,0:T(8,128)(2,1)S(1)}, bf16[32,2816]{1,0:T(8,128)(2,1)}, u32[]{:S(2)}) copy-start(bf16[32,2816]{1,0:T(8,128)(2,1)} %param.44) | copy-start | bytes 540676
  13.6 100.6 %copy-start.36 = (bf16[32,2816]{1,0:T(8,128)(2,1)S(1)}, bf16[32,2816]{1,0:T(8,128)(2,1)}, u32[]{:S(2)}) copy-start(bf16[32,2816]{1,0:T(8,128)(2,1)} %param.43) | copy-start | bytes 540676
  13.6 100.6 %copy-start.39 = (bf16[2048,32]{0,1:T(8,128)(2,1)S(1)}, bf16[2048,32]{0,1:T(8,128)(2,1)}, u32[]{:S(2)}) copy-start(bf16[2048,32]{0,1:T(8,128)(2,1)} %param.41) | copy-start | bytes 393220
  16.5 100.4 %copy-start.44 = (f32[8]{0:T(128)S(1)}, f32[8]{0:T(128)}, u32[]{:S(2)}) copy-start(f32[8]{0:T(128)} %param.39) | copy-start | bytes 100
  16.6 100.4 %copy-start.45 = (f32[8]{0:T(128)S(1)}, f32[8]{0:T(128)}, u32[]{:S(2)}) copy-start(f32[8]{0:T(128)} %param.38) | copy-start | bytes 100
  117.1 20.1 %copy-start.9 = (f32[8,128]{1,0:T(8,128)}, f32[8,128]{1,0:T(8,128)S(1)}, u32[]{:S(2)}) copy-start(f32[8,128]{1,0:T(8,128)S(1)} %select_maximum_fusion.4.small_ref) | copy-start | bytes 12292
  117.1 20.1 %copy-start.5 = (f32[8,1024]{1,0:T(8,128)}, f32[8,1024]{1,0:T(8,128)S(1)}, u32[]{:S(2)}) copy-start(f32[8,1024]{1,0:T(8,128)S(1)} %select_maximum_fusion.taps_ref) | copy-start | bytes 98308
  137.2 40.5 %copy-start.7 = (f32[8,256]{1,0:T(8,128)}, f32[8,256]{1,0:T(8,128)S(1)}, u32[]{:S(2)}) copy-start(f32[8,256]{1,0:T(8,128)S(1)} %broadcast_in_dim.105.gain_ref) | copy-start | bytes 24580
  177.7 71.8 %all-to-all-start = ((bf16[4,3,256,512]{3,2,1,0:T(8,128)(2,1)}), bf16[4,3,256,512]{3,2,1,0:T(8,128)(2,1)}, u32[]{:S(2)}, u32[]{:S(2)}) async-start(bf16[4,3,256,512]{3,2,1,0:T(8,128)(2,1)} %get-tuple-element.45), calls=%async_computation | async-start | bytes 6291456 | tf_op jit(solution)/shard_map/all_to_all | solution.py:733
  289.6 65.6 %copy-start.15 = (f32[768,1024]{1,0:T(8,128)}, f32[768,1024]{1,0:T(8,128)S(1)}, u32[]{:S(2)}) copy-start(f32[768,1024]{1,0:T(8,128)S(1)} %get-tuple-element.118) | copy-start | bytes 9437188
  325.0 16.1 %slice-start.7 = ((s8[4325376]{0:T(1024)(128)(4,1)}), s8[4194304]{0:T(1024)(128)(4,1)S(1)}, s32[]{:S(2)}) async-start(s8[4325376]{0:T(1024)(128)(4,1)} %bitcast.367), calls=%async_computation.15 | async-start | bytes 8388608
  370.1 41.7 %all-to-all-start.1 = ((bf16[4,3,256,512]{3,2,1,0:T(8,128)(2,1)}), bf16[4,3,256,512]{3,2,1,0:T(8,128)(2,1)}, u32[]{:S(2)}, u32[]{:S(2)}) async-start(bf16[4,3,256,512]{3,2,1,0:T(8,128)(2,1)} %bitcast.292), calls=%async_computation.1 | async-start | bytes 6291456 | tf_op jit(solution)/shard_map/all_to_all | solution.py:759
  374.8 336.5 %reduce-scatter.2.cloned.1.call-start = ((), (), s32[]{:S(2)}) async-start(), calls=%async_computation.7 | async-start | bytes 17842176 | tf_op jit(solution)/shard_map/reduce_scatter | solution.py:767
  378.4 14.6 %collective-permute-start = (bf16[2,2,2,2,32,2048]{5,4,3,2,1,0:T(8,128)(2,1)}, bf16[2,2,2,2,32,2048]{5,4,3,2,1,0:T(8,128)(2,1)}, u32[]{:S(2)}, u32[]{:S(2)}) collective-permute-start(bf16[2,2,2,2,32,2048]{5,4,3,2,1,0:T(8,128)(2,1)} %dynamic-slice_bitcast_fusion), channel_id=1, source_target_pairs={{0,8},{8,0},{16,24},{24,16},{1,9},{9,1},{17,25},{25,17},{2,10},{10... | collective-permute-start | bytes 6291464 | tf_op jit(solution)/shard_map/ppermute | solution.py:654
  397.4 14.4 %copy-start.32 = (bf16[1024,128]{0,1:T(8,128)(2,1)S(1)}, bf16[1024,128]{0,1:T(8,128)(2,1)}, u32[]{:S(2)}) copy-start(bf16[1024,128]{0,1:T(8,128)(2,1)} %copy-done.31) | copy-start | bytes 786436
  397.4 15.3 %copy-start.43 = (s32[3,8]{1,0:T(4,128)S(1)}, s32[3,8]{1,0:T(4,128)}, u32[]{:S(2)}) copy-start(s32[3,8]{1,0:T(4,128)} %param.27) | copy-start | bytes 292
  425.9 73.7 %collective-permute-start.1 = (bf16[2,2,2,32,2048]{4,3,2,1,0:T(8,128)(2,1)S(1)}, bf16[2,2,2,32,2048]{4,3,2,1,0:T(8,128)(2,1)}, u32[]{:S(2)}, u32[]{:S(2)}) collective-permute-start(bf16[2,2,2,32,2048]{4,3,2,1,0:T(8,128)(2,1)S(1)} %dynamic-slice_bitcast_fusion.4), channel_id=1, source_target_pairs={{0,16},{8,24},{16,0},{24,8},{1,17},{9,25},{17,1},{25,9},{2,18},{10... | collective-permute-start | bytes 3145736 | tf_op jit(solution)/shard_map/ppermute | solution.py:654
  511.6 11.3 %collective-permute-start.2 = (bf16[2,256,1024]{2,1,0:T(8,128)(2,1)}, bf16[2,256,1024]{2,1,0:T(8,128)(2,1)}, u32[]{:S(2)}, u32[]{:S(2)}) collective-permute-start(bf16[2,256,1024]{2,1,0:T(8,128)(2,1)} %dynamic-slice_bitcast_fusion.3), channel_id=1, source_target_pairs={{0,8},{8,0},{16,24},{24,16},{1,9},{9,1},{17,25},{25,17},{2,10},{10... | collective-permute-start | bytes 3145736 | tf_op jit(solution)/shard_map/ppermute | solution.py:654
  517.4 9.4 %collective-permute-start.6 = (bf16[2,256,1024]{2,1,0:T(8,128)(2,1)}, bf16[2,256,1024]{2,1,0:T(8,128)(2,1)}, u32[]{:S(2)}, u32[]{:S(2)}) collective-permute-start(bf16[2,256,1024]{2,1,0:T(8,128)(2,1)} %dynamic-slice_bitcast_fusion.1), channel_id=1, source_target_pairs={{0,8},{8,0},{16,24},{24,16},{1,9},{9,1},{17,25},{25,17},{2,10},{10... | collective-permute-start | bytes 3145736 | tf_op jit(solution)/shard_map/ppermute | solution.py:654
  522.2 6.7 collective-permute-start.4
  525.0 24.6 %collective-permute-start.3 = (bf16[256,1024]{1,0:T(8,128)(2,1)S(1)}, bf16[256,1024]{1,0:T(8,128)(2,1)S(1)}, u32[]{:S(2)}, u32[]{:S(2)}) collective-permute-start(bf16[256,1024]{1,0:T(8,128)(2,1)S(1)} %dynamic-slice_bitcast_fusion.7), channel_id=1, source_target_pairs={{0,16},{8,24},{16,0},{24,8},{1,17},{9,25},{17,1},{25,9},{2,18},{10... | collective-permute-start | bytes 1572872 | tf_op jit(solution)/shard_map/ppermute | solution.py:654
  528.6 30.2 %collective-permute-start.7 = (bf16[256,1024]{1,0:T(8,128)(2,1)S(1)}, bf16[256,1024]{1,0:T(8,128)(2,1)S(1)}, u32[]{:S(2)}, u32[]{:S(2)}) collective-permute-start(bf16[256,1024]{1,0:T(8,128)(2,1)S(1)} %dynamic-slice_bitcast_fusion.5), channel_id=1, source_target_pairs={{0,16},{8,24},{16,0},{24,8},{1,17},{9,25},{17,1},{25,9},{2,18},{10... | collective-permute-start | bytes 1572872 | tf_op jit(solution)/shard_map/ppermute | solution.py:654
  530.6 47.0 %copy-start.17 = (bf16[2,256,1024]{2,1,0:T(8,128)(2,1)}, bf16[2,256,1024]{2,1,0:T(8,128)(2,1)S(1)}, u32[]{:S(2)}) copy-start(bf16[2,256,1024]{2,1,0:T(8,128)(2,1)S(1)} %fusion.39) | copy-start | bytes 3145732
  530.6 46.9 %copy-start.12 = (f32[3,256,1024]{2,1,0:T(8,128)S(1)}, f32[3,256,1024]{2,1,0:T(8,128)}, u32[]{:S(2)}) copy-start(f32[3,256,1024]{2,1,0:T(8,128)} %dynamic-slice_convert_fusion) | copy-start | bytes 9437188
  530.6 46.9 %copy-start.41 = (f32[1024,1]{0,1:T(1,128)S(1)}, f32[1024,1]{0,1:T(1,128)}, u32[]{:S(2)}) copy-start(f32[1024,1]{0,1:T(1,128)} %copy-done.40) | copy-start | bytes 12292
  530.6 46.9 %collective-permute-start.5 = (bf16[256,1024]{1,0:T(8,128)(2,1)S(1)}, bf16[256,1024]{1,0:T(8,128)(2,1)S(1)}, u32[]{:S(2)}, u32[]{:S(2)}) collective-permute-start(bf16[256,1024]{1,0:T(8,128)(2,1)S(1)} %dynamic-slice_bitcast_fusion.6), channel_id=1, source_target_pairs={{0,16},{8,24},{16,0},{24,8},{1,17},{9,25},{17,1},{25,9},{2,18},{10... | collective-permute-start | bytes 1572872 | tf_op jit(solution)/shard_map/ppermute | solution.py:654
  549.6 28.9 %copy-start.14 = (f32[768,1024]{1,0:T(8,128)S(1)}, f32[768,1024]{1,0:T(8,128)}, u32[]{:S(2)}) copy-start(f32[768,1024]{1,0:T(8,128)} %copy-done.13) | copy-start | bytes 9437188
  580.2 21.7 %all-to-all-start.4 = ((bf16[8,32,1024]{2,1,0:T(8,128)(2,1)}), bf16[8,32,1024]{2,1,0:T(8,128)(2,1)}, u32[]{:S(2)}, u32[]{:S(2)}) async-start(bf16[8,32,1024]{2,1,0:T(8,128)(2,1)} %bitcast.311), calls=%async_computation.4 | async-start | bytes 1048576 | tf_op jit(solution)/shard_map/all_to_all | solution.py:823
  601.9 88.1 %all-to-all-start.3 = ((bf16[8,32,1024]{2,1,0:T(8,128)(2,1)}), bf16[8,32,1024]{2,1,0:T(8,128)(2,1)}, u32[]{:S(2)}, u32[]{:S(2)}) async-start(bf16[8,32,1024]{2,1,0:T(8,128)(2,1)} %bitcast.318), calls=%async_computation.3 | async-start | bytes 1048576 | tf_op jit(solution)/shard_map/all_to_all | solution.py:823
  689.9 18.5 %all-to-all-start.2 = ((bf16[8,32,1024]{2,1,0:T(8,128)(2,1)}), bf16[8,32,1024]{2,1,0:T(8,128)(2,1)S(1)}, u32[]{:S(2)}, u32[]{:S(2)}) async-start(bf16[8,32,1024]{2,1,0:T(8,128)(2,1)} %bitcast.51), calls=%async_computation.2 | async-start | bytes 1048576 | tf_op jit(solution)/shard_map/all_to_all | solution.py:823
  (41 other events, 255.3 us)
Sparse Core Ops, SparseCore 0:
  115.2 166.6 all-gather.1
  411.9 223.3 reduce-scatter.1
